TPU v7x, 768 devices: a whole 4x8x12 slice. The times are simulated.
768 devices in a mesh: seq: 12 (over x, z_lo), segment: 64 (over y, z_hi, core).
Axes of the slice: x: 4, y: 8, z: 12 (z_hi: 4, z_lo: 3; z = z_hi * 3 + z_lo), core: 2. Of those that a mesh axis runs over, the one named last changes fastest.
Arguments:
- stream: bfloat16 [1536, 32768], P('seq', 'segment'), may hold values from -6 to 6
- w_query: bfloat16 [4096, 16384], P(None, 'segment'), may hold values from -0.09375 to 0.09375
- w_out: bfloat16 [16384, 4096], P('segment'), may hold values from -0.125 to 0.125
- neighbour_kv: bfloat16 [2, 2, 6144, 16384], P(None, None, 'seq', 'segment'), may hold values from -6 to 6
Outputs:
- first: bfloat16 [1536, 32768], P('seq', 'segment')
- second: bfloat16 [1536, 32768], P('seq', 'segment')
All inputs are finite; a program needn't handle non-finite values.
Results may differ from a plain program's by a relative error of at most 0.0075.
Values may be sent and summed in bfloat16 or wider, within the bound.
No kernel may reach another device: no remote copies, remote signals or barrier semaphores. Data moves between devices by JAX's collectives and lax.ppermute only.
A program may use at most 32 MiB of HBM per device.

v0:
```python
import jax
import jax.numpy as jnp
from jax import lax
from jax.sharding import PartitionSpec as P

HD = 128
SECT = 8
CH = 64
NEIGH = 2
NBL = 128
TICKS = 2


EPS = 1e-05


def swapped(block, axis, apart):
    count = lax.axis_size(axis)
    route = []
    for low in range(count):
        high = low | 1 << apart
        if high != low and high < count:
            route += [(low, high), (high, low)]
    return lax.ppermute(block, axis, route)


def passed_along(block, axis, distance):
    devices = range(lax.axis_size(axis))
    route = [(i - distance, i) for i in devices if i - distance in devices]
    return lax.ppermute(block, axis, route)


def assemble(piece, head_group, bit_order, total_bits):
    current = piece
    for bit_index in bit_order:
        other = swapped(current, "segment", bit_index)
        is_upper = head_group // 2**bit_index % 2 == 1
        lower_half = jnp.where(is_upper, other, current)
        upper_half = jnp.where(is_upper, current, other)
        current = jnp.stack([lower_half, upper_half], axis=1)
    count_bits = len(bit_order)
    permutation = [0]
    for target in range(count_bits):
        wanted = total_bits - 1 - target
        permutation.append(1 + (count_bits - 1 - bit_order.index(wanted)))
    permutation.append(count_bits + 1)
    current = jnp.transpose(current, permutation)
    return current.reshape(piece.shape[0], -1)


def share_sums(term, head_group, bit_order, total_bits):
    partial_value = term.astype(jnp.float32)
    tok_rows = partial_value.shape[0]
    current = partial_value.reshape(
        (tok_rows,) + (2,) * total_bits + (partial_value.shape[1] // 2**total_bits,)
    )
    remaining = list(range(total_bits - 1, -1, -1))
    for bit_index in bit_order:
        axis_pos = 1 + remaining.index(bit_index)
        lower_half = lax.index_in_dim(current, 0, axis_pos, keepdims=False)
        upper_half = lax.index_in_dim(current, 1, axis_pos, keepdims=False)
        is_upper = head_group // 2**bit_index % 2 == 1
        kept_half = jnp.where(is_upper, upper_half, lower_half)
        sent_half = jnp.where(is_upper, lower_half, upper_half)
        current = kept_half + swapped(sent_half.astype(jnp.bfloat16), "segment", bit_index).astype(
            sent_half.dtype
        )
        remaining = [bit_left for bit_left in remaining if bit_left != bit_index]
    return current


def local_layer(whole, keys_values, edge_kv, w_query, w_out):
    wide = whole.astype(jnp.float32)
    normed = (wide * lax.rsqrt(jnp.mean(wide * wide, axis=-1, keepdims=True) + EPS)).astype(
        jnp.bfloat16
    )
    queries = jnp.dot(normed, w_query, preferred_element_type=jnp.float32).astype(jnp.bfloat16)
    tokens = queries.shape[0]
    head_cols = queries.shape[1]
    groups = tokens // CH + 1
    padded = jnp.concatenate(
        [
            jnp.zeros((1, head_cols), jnp.bfloat16),
            queries,
            jnp.zeros((CH - 1, head_cols), jnp.bfloat16),
        ],
        axis=0,
    )
    padded = padded.reshape(groups, CH, head_cols // HD, HD)
    extended = jnp.concatenate([edge_kv, keys_values], axis=1).reshape(
        2, groups, NEIGH * NBL, head_cols // HD, HD
    )
    scores = jnp.einsum(
        "gchd,gkhd->ghck", padded, extended[0], preferred_element_type=jnp.float32
    ) * HD ** (-0.5)
    exponent = jnp.exp(scores)
    weights = (exponent / jnp.sum(exponent, axis=-1, keepdims=True)).astype(jnp.bfloat16)
    attended = jnp.einsum(
        "ghck,gkhd->gchd", weights, extended[1], preferred_element_type=jnp.float32
    ).astype(jnp.bfloat16)
    attended = attended.reshape(-1, head_cols)[1 : 1 + tokens]
    term = jnp.dot(attended, w_out, preferred_element_type=jnp.float32).astype(jnp.bfloat16)
    return lax.optimization_barrier(term)


def per_device(stream, w_query, w_out, neighbour_kv):
    groups_per = lax.axis_size("segment") // SECT
    head_group = lax.axis_index("segment") % groups_per
    total_bits = groups_per.bit_length() - 1
    bit_order = list(range(total_bits))
    edge_rows = NEIGH * NBL
    edges = passed_along(neighbour_kv[:, :, neighbour_kv.shape[2] - edge_rows :, :], "seq", 1)
    current = stream
    whole = assemble(current, head_group, bit_order, total_bits)
    outputs = []
    for tick_no in range(TICKS):
        term = local_layer(whole, neighbour_kv[tick_no], edges[tick_no], w_query, w_out)
        summed = share_sums(term, head_group, bit_order, total_bits)
        result = (current.astype(jnp.float32) + summed).astype(jnp.bfloat16)
        outputs.append(result)
        if tick_no + 1 < TICKS:
            current = passed_along(result, "segment", groups_per)
            whole = assemble(current, head_group, bit_order, total_bits)
    return (outputs[0], outputs[TICKS - 1])


def solution(mesh):
    placed = (
        P("seq", "segment"),
        P(None, "segment"),
        P("segment", None),
        P(None, None, "seq", "segment"),
    )
    return jax.shard_map(
        per_device,
        mesh=mesh,
        in_specs=placed,
        out_specs=(P("seq", "segment"), P("seq", "segment")),
        check_vma=False,
    )
```

profile of v0, /device:TPU:38, one launch (start us, length us, event | category | flops | bytes accessed | tf_op | source)
XLA Modules:
  0.0 279.8 jit_solution(2707750827553385166)
XLA Ops:
  0.6 1.2 copy.12
  1.8 1.9 collective-permute-start.1
  3.8 1.4 collective-permute-done.1
  5.2 0.9 select_bitcast_fusion.11
  6.1 0.8 pad_maximum_fusion.4
  6.9 7.9 %collective-permute-start.2 = (bf16[128,2,512]{0,2,1:T(8,128)(2,1)}, bf16[128,2,512]{0,2,1:T(8,128)(2,1)}, u32[]{:S(2)}, u32[]{:S(2)}) collective-permute-start(bf16[128,2,512]{0,2,1:T(8,128)(2,1)} %pad_maximum_fusion.4), channel_id=1, source_target_pairs={{0,2},{2,0},{1,3},{3,1},{4,6},{6,4},{5,7},{7,5},{8,10},{10,8},{9,1... | collective-permute-start | bytes 786440 | tf_op jit(solution)/shard_map/ppermute | solution.py:24
  14.8 1.9 slice.73
  16.7 5.5 %collective-permute-start = (bf16[2,2,256,256]{3,2,1,0:T(8,128)(2,1)}, bf16[2,2,256,256]{3,2,1,0:T(8,128)(2,1)}, u32[]{:S(2)}, u32[]{:S(2)}) collective-permute-start(bf16[2,2,256,256]{3,2,1,0:T(8,128)(2,1)} %slice.73), channel_id=1, source_target_pairs={{0,64},{64,128},{128,192},{192,256},{256,320},{320,384},{384,448},... | collective-permute-start | bytes 1572872 | tf_op jit(solution)/shard_map/ppermute | solution.py:30
  22.2 10.7 %collective-permute-done.2 = bf16[128,2,512]{0,2,1:T(8,128)(2,1)} collective-permute-done((bf16[128,2,512]{0,2,1:T(8,128)(2,1)}, bf16[128,2,512]{0,2,1:T(8,128)(2,1)}, u32[]{:S(2)}, u32[]{:S(2)}) %collective-permute-start.2) | collective-permute-done | bytes 262176 | tf_op jit(solution)/shard_map/ppermute | solution.py:24
  33.0 1.1 select_bitcast_fusion.7
  34.1 0.7 copy-done.6
  34.8 0.9 pad_maximum_fusion
  35.6 13.9 %collective-permute-start.3 = (bf16[128,2,2,512]{0,3,2,1:T(8,128)(2,1)}, bf16[128,2,2,512]{0,3,2,1:T(8,128)(2,1)}, u32[]{:S(2)}, u32[]{:S(2)}) collective-permute-start(bf16[128,2,2,512]{0,3,2,1:T(8,128)(2,1)} %pad_maximum_fusion), channel_id=1, source_target_pairs={{0,4},{4,0},{1,5},{5,1},{2,6},{6,2},{3,7},{7,3},{8,12},{12,8},{9,1... | collective-permute-start | bytes 1572872 | tf_op jit(solution)/shard_map/ppermute | solution.py:24
  49.5 1.1 slice_bitcast_fusion
  50.7 1.1 slice_bitcast_fusion.2
  51.8 2.2 fusion.8
  54.0 0.8 squeeze.18
  54.9 28.6 %collective-permute-done.3 = bf16[128,2,2,512]{0,3,2,1:T(8,128)(2,1)} collective-permute-done((bf16[128,2,2,512]{0,3,2,1:T(8,128)(2,1)}, bf16[128,2,2,512]{0,3,2,1:T(8,128)(2,1)}, u32[]{:S(2)}, u32[]{:S(2)}) %collective-permute-start.3) | collective-permute-done | bytes 524320 | tf_op jit(solution)/shard_map/ppermute | solution.py:24
  83.5 1.1 select_bitcast_fusion.3
  84.6 0.6 multiply_reduce_fusion.1
  85.5 1.4 copy-done.3
  86.9 0.6 convolution_convert_fusion.5
  87.6 0.3 fusion.3
  87.9 1.3 fusion.4
  89.3 0.4 convolution_convert_fusion.1
  89.8 3.0 %reshape.102 = f32[128,2,2,2,512]{4,3,2,1,0:T(2,128)} reshape(bf16[128,4096]{1,0:T(8,128)(2,1)S(1)} %convolution_convert_fusion.1) | data formatting | bytes 3145728 | tf_op jit(solution)/shard_map/reshape | solution.py:54
  92.8 5.7 %fusion.33 = (f32[128,2,2,1,512]{4,3,2,1,0:T(1,128)}, f32[128,2,2,1,512]{4,3,2,1,0:T(1,128)}) fusion(f32[128,2,2,2,512]{4,3,2,1,0:T(2,128)} %reshape.102), kind=kLoop, calls=%fused_computation.91 | loop fusion | bytes 4194304 | tf_op jit(solution)/shard_map/slice | solution.py:61
  98.5 2.3 copy.30
  100.8 3.6 %copy.31 = f32[128,2,2,1,512]{0,4,1,2,3:T(8,128)} copy(f32[128,2,2,1,512]{4,3,2,1,0:T(1,128)} %get-tuple-element.7) | data formatting | bytes 2097152
  104.6 2.1 collective-permute-start.4
  106.6 1.9 collective-permute-done.4
  108.8 1.9 collective-permute-start.5
  110.7 15.7 %collective-permute-done.5 = bf16[128,2,512]{0,2,1:T(8,128)(2,1)S(1)} collective-permute-done((bf16[128,2,512]{0,2,1:T(8,128)(2,1)S(1)}, bf16[128,2,512]{0,2,1:T(8,128)(2,1)S(1)}, u32[]{:S(2)}, u32[]{:S(2)}) %collective-permute-start.5) | collective-permute-done | bytes 262176 | tf_op jit(solution)/shard_map/ppermute | solution.py:24
  126.5 13.0 %collective-permute-start.6 = (bf16[128,512]{0,1:T(8,128)(2,1)S(1)}, bf16[128,512]{0,1:T(8,128)(2,1)S(1)}, u32[]{:S(2)}, u32[]{:S(2)}) collective-permute-start(bf16[128,512]{0,1:T(8,128)(2,1)S(1)} %fusion.24), channel_id=1, source_target_pairs={{0,4},{4,0},{1,5},{5,1},{2,6},{6,2},{3,7},{7,3},{8,12},{12,8},{9,1... | collective-permute-start | bytes 393224 | tf_op jit(solution)/shard_map/ppermute | solution.py:24
  139.5 7.3 %collective-permute-done.6 = bf16[128,512]{0,1:T(8,128)(2,1)S(1)} collective-permute-done((bf16[128,512]{0,1:T(8,128)(2,1)S(1)}, bf16[128,512]{0,1:T(8,128)(2,1)S(1)}, u32[]{:S(2)}, u32[]{:S(2)}) %collective-permute-start.6) | collective-permute-done | bytes 131104 | tf_op jit(solution)/shard_map/ppermute | solution.py:24
  146.9 2.7 collective-permute-start.7
  149.7 5.5 %collective-permute-done.7 = bf16[128,512]{0,1:T(8,128)(2,1)S(1)} collective-permute-done((bf16[128,512]{0,1:T(8,128)(2,1)S(1)}, bf16[128,512]{0,1:T(8,128)(2,1)S(1)}, u32[]{:S(2)}, u32[]{:S(2)}) %collective-permute-start.7) | collective-permute-done | bytes 131104 | tf_op jit(solution)/shard_map/ppermute | solution.py:30
  155.1 1.9 collective-permute-start.8
  157.1 1.3 collective-permute-done.8
  158.4 2.1 collective-permute-start.9
  160.5 19.5 %collective-permute-done.9 = bf16[128,2,512]{0,2,1:T(8,128)(2,1)S(1)} collective-permute-done((bf16[128,2,512]{0,2,1:T(8,128)(2,1)S(1)}, bf16[128,2,512]{0,2,1:T(8,128)(2,1)S(1)}, u32[]{:S(2)}, u32[]{:S(2)}) %collective-permute-start.9) | collective-permute-done | bytes 262176 | tf_op jit(solution)/shard_map/ppermute | solution.py:24
  180.0 0.9 pad_maximum_fusion.1
  180.9 5.9 %collective-permute-start.10 = (bf16[128,2,2,512]{0,3,2,1:T(8,128)(2,1)}, bf16[128,2,2,512]{0,3,2,1:T(8,128)(2,1)}, u32[]{:S(2)}, u32[]{:S(2)}) collective-permute-start(bf16[128,2,2,512]{0,3,2,1:T(8,128)(2,1)} %pad_maximum_fusion.1), channel_id=1, source_target_pairs={{0,4},{4,0},{1,5},{5,1},{2,6},{6,2},{3,7},{7,3},{8,12},{12,8},{9,1... | collective-permute-start | bytes 1572872 | tf_op jit(solution)/shard_map/ppermute | solution.py:24
  186.9 0.8 squeeze.43
  187.8 29.8 %collective-permute-done.10 = bf16[128,2,2,512]{0,3,2,1:T(8,128)(2,1)} collective-permute-done((bf16[128,2,2,512]{0,3,2,1:T(8,128)(2,1)}, bf16[128,2,2,512]{0,3,2,1:T(8,128)(2,1)}, u32[]{:S(2)}, u32[]{:S(2)}) %collective-permute-start.10) | collective-permute-done | bytes 524320 | tf_op jit(solution)/shard_map/ppermute | solution.py:24
  217.6 1.1 select_bitcast_fusion.1
  218.7 0.6 multiply_reduce_fusion
  219.6 1.4 copy-done.4
  221.0 0.6 convolution_convert_fusion.4
  222.0 0.3 fusion.2
  222.3 0.3 fusion.5
  222.7 0.4 convolution_convert_fusion
  223.1 3.0 %reshape.105 = f32[128,2,2,2,512]{4,3,2,1,0:T(2,128)} reshape(bf16[128,4096]{1,0:T(8,128)(2,1)S(1)} %convolution_convert_fusion) | data formatting | bytes 3145728 | tf_op jit(solution)/shard_map/reshape | solution.py:54
  226.2 5.7 %fusion.32 = (f32[128,2,2,1,512]{4,3,2,1,0:T(1,128)}, f32[128,2,2,1,512]{4,3,2,1,0:T(1,128)}) fusion(f32[128,2,2,2,512]{4,3,2,1,0:T(2,128)} %reshape.105), kind=kLoop, calls=%fused_computation.90 | loop fusion | bytes 4194304 | tf_op jit(solution)/shard_map/slice | solution.py:61
  231.9 2.3 copy.32
  234.2 3.6 %copy.33 = f32[128,2,2,1,512]{0,4,1,2,3:T(8,128)} copy(f32[128,2,2,1,512]{4,3,2,1,0:T(1,128)} %get-tuple-element.5) | data formatting | bytes 2097152
  237.9 3.0 %collective-permute-start.11 = (bf16[128,2,2,512]{0,3,1,2:T(8,128)(2,1)S(1)}, bf16[128,2,2,512]{0,3,1,2:T(8,128)(2,1)S(1)}, u32[]{:S(2)}, u32[]{:S(2)}) collective-permute-start(bf16[128,2,2,512]{0,3,1,2:T(8,128)(2,1)S(1)} %fusion.7), channel_id=1, source_target_pairs={{0,1},{1,0},{2,3},{3,2},{4,5},{5,4},{6,7},{7,6},{8,9},{9,8},{10,11... | collective-permute-start | bytes 1572872 | tf_op jit(solution)/shard_map/ppermute | solution.py:24
  241.0 1.5 collective-permute-done.11
  242.7 7.5 %collective-permute-start.12 = (bf16[128,2,512]{0,2,1:T(8,128)(2,1)S(1)}, bf16[128,2,512]{0,2,1:T(8,128)(2,1)S(1)}, u32[]{:S(2)}, u32[]{:S(2)}) collective-permute-start(bf16[128,2,512]{0,2,1:T(8,128)(2,1)S(1)} %fusion.15), channel_id=1, source_target_pairs={{0,2},{2,0},{1,3},{3,1},{4,6},{6,4},{5,7},{7,5},{8,10},{10,8},{9,1... | collective-permute-start | bytes 786440 | tf_op jit(solution)/shard_map/ppermute | solution.py:24
  250.2 12.4 %collective-permute-done.12 = bf16[128,2,512]{0,2,1:T(8,128)(2,1)S(1)} collective-permute-done((bf16[128,2,512]{0,2,1:T(8,128)(2,1)S(1)}, bf16[128,2,512]{0,2,1:T(8,128)(2,1)S(1)}, u32[]{:S(2)}, u32[]{:S(2)}) %collective-permute-start.12) | collective-permute-done | bytes 262176 | tf_op jit(solution)/shard_map/ppermute | solution.py:24
  262.8 7.4 %collective-permute-start.13 = (bf16[128,512]{0,1:T(8,128)(2,1)S(1)}, bf16[128,512]{0,1:T(8,128)(2,1)S(1)}, u32[]{:S(2)}, u32[]{:S(2)}) collective-permute-start(bf16[128,512]{0,1:T(8,128)(2,1)S(1)} %fusion.25), channel_id=1, source_target_pairs={{0,4},{4,0},{1,5},{5,1},{2,6},{6,2},{3,7},{7,3},{8,12},{12,8},{9,1... | collective-permute-start | bytes 393224 | tf_op jit(solution)/shard_map/ppermute | solution.py:24
  270.2 0.8 copy.28
  271.0 8.0 %collective-permute-done.13 = bf16[128,512]{0,1:T(8,128)(2,1)S(1)} collective-permute-done((bf16[128,512]{0,1:T(8,128)(2,1)S(1)}, bf16[128,512]{0,1:T(8,128)(2,1)S(1)}, u32[]{:S(2)}, u32[]{:S(2)}) %collective-permute-start.13) | collective-permute-done | bytes 131104 | tf_op jit(solution)/shard_map/ppermute | solution.py:24
  279.1 0.8 copy.29
  (62 shorter events, 2.7 us)
Async XLA Ops:
  0.6 88.7 %copy-start = (bf16[256,4096]{1,0:T(8,128)(2,1)S(1)}, bf16[256,4096]{1,0:T(8,128)(2,1)}, u32[]{:S(2)}) copy-start(bf16[256,4096]{1,0:T(8,128)(2,1)} %param.6) | copy-start | bytes 6291460
  1.8 3.4 %collective-permute-start.1 = (bf16[128,512]{0,1:T(8,128)(2,1)S(1)}, bf16[128,512]{0,1:T(8,128)(2,1)}, u32[]{:S(2)}, u32[]{:S(2)}) collective-permute-start(bf16[128,512]{0,1:T(8,128)(2,1)S(1)} %copy.12), channel_id=1, source_target_pairs={{0,1},{1,0},{2,3},{3,2},{4,5},{5,4},{6,7},{7,6},{8,9},{9,8},{10,11... | collective-permute-start | bytes 393224 | tf_op jit(solution)/shard_map/ppermute | solution.py:24
  3.8 45.7 %copy-start.5 = (bf16[2,2,512,256]{3,2,1,0:T(8,128)(2,1)S(1)}, bf16[2,2,512,256]{3,2,1,0:T(8,128)(2,1)}, u32[]{:S(2)}) copy-start(bf16[2,2,512,256]{3,2,1,0:T(8,128)(2,1)} %param.7) | copy-start | bytes 3145732
  6.1 16.1 %copy-start.11 = (bf16[128,1,512]{0,2,1:T(8,128)(2,1)}, bf16[128,1,512]{0,2,1:T(8,128)(2,1)S(1)}, u32[]{:S(2)}) copy-start(bf16[128,1,512]{0,2,1:T(8,128)(2,1)S(1)} %get-tuple-element.26) | copy-start | bytes 393220
  6.1 16.1 %copy-start.12 = (bf16[128,1,512]{0,2,1:T(8,128)(2,1)}, bf16[128,1,512]{0,2,1:T(8,128)(2,1)S(1)}, u32[]{:S(2)}) copy-start(bf16[128,1,512]{0,2,1:T(8,128)(2,1)S(1)} %get-tuple-element.27) | copy-start | bytes 393220
  6.9 26.0 %collective-permute-start.2 = (bf16[128,2,512]{0,2,1:T(8,128)(2,1)}, bf16[128,2,512]{0,2,1:T(8,128)(2,1)}, u32[]{:S(2)}, u32[]{:S(2)}) collective-permute-start(bf16[128,2,512]{0,2,1:T(8,128)(2,1)} %pad_maximum_fusion.4), channel_id=1, source_target_pairs={{0,2},{2,0},{1,3},{3,1},{4,6},{6,4},{5,7},{7,5},{8,10},{10,8},{9,1... | collective-permute-start | bytes 786440 | tf_op jit(solution)/shard_map/ppermute | solution.py:24
  16.7 34.0 %collective-permute-start = (bf16[2,2,256,256]{3,2,1,0:T(8,128)(2,1)}, bf16[2,2,256,256]{3,2,1,0:T(8,128)(2,1)}, u32[]{:S(2)}, u32[]{:S(2)}) collective-permute-start(bf16[2,2,256,256]{3,2,1,0:T(8,128)(2,1)} %slice.73), channel_id=1, source_target_pairs={{0,64},{64,128},{128,192},{192,256},{256,320},{320,384},{384,448},... | collective-permute-start | bytes 1572872 | tf_op jit(solution)/shard_map/ppermute | solution.py:30
  34.1 0.7 copy-start.6
  35.6 47.9 %collective-permute-start.3 = (bf16[128,2,2,512]{0,3,2,1:T(8,128)(2,1)}, bf16[128,2,2,512]{0,3,2,1:T(8,128)(2,1)}, u32[]{:S(2)}, u32[]{:S(2)}) collective-permute-start(bf16[128,2,2,512]{0,3,2,1:T(8,128)(2,1)} %pad_maximum_fusion), channel_id=1, source_target_pairs={{0,4},{4,0},{1,5},{5,1},{2,6},{6,2},{3,7},{7,3},{8,12},{12,8},{9,1... | collective-permute-start | bytes 1572872 | tf_op jit(solution)/shard_map/ppermute | solution.py:24
  51.7 31.7 %copy-start.7 = (bf16[128,1,2,512]{0,3,2,1:T(8,128)(2,1)S(1)}, bf16[128,1,2,512]{0,3,2,1:T(8,128)(2,1)}, u32[]{:S(2)}) copy-start(bf16[128,1,2,512]{0,3,2,1:T(8,128)(2,1)} %copy-done.6) | copy-start | bytes 786436
  85.3 1.6 copy-start.3
  104.5 4.1 %copy-start.2 = (f32[128,2,2,1,512]{0,4,1,2,3:T(8,128)S(1)}, f32[128,2,2,1,512]{0,4,1,2,3:T(8,128)}, u32[]{:S(2)}) copy-start(f32[128,2,2,1,512]{0,4,1,2,3:T(8,128)} %copy.31) | copy-start | bytes 3145732
  104.6 3.9 %collective-permute-start.4 = (bf16[128,2,2,512]{0,3,1,2:T(8,128)(2,1)S(1)}, bf16[128,2,2,512]{0,3,1,2:T(8,128)(2,1)S(1)}, u32[]{:S(2)}, u32[]{:S(2)}) collective-permute-start(bf16[128,2,2,512]{0,3,1,2:T(8,128)(2,1)S(1)} %fusion.6), channel_id=1, source_target_pairs={{0,1},{1,0},{2,3},{3,2},{4,5},{5,4},{6,7},{7,6},{8,9},{9,8},{10,11... | collective-permute-start | bytes 1572872 | tf_op jit(solution)/shard_map/ppermute | solution.py:24
  108.8 17.7 %collective-permute-start.5 = (bf16[128,2,512]{0,2,1:T(8,128)(2,1)S(1)}, bf16[128,2,512]{0,2,1:T(8,128)(2,1)S(1)}, u32[]{:S(2)}, u32[]{:S(2)}) collective-permute-start(bf16[128,2,512]{0,2,1:T(8,128)(2,1)S(1)} %fusion.14), channel_id=1, source_target_pairs={{0,2},{2,0},{1,3},{3,1},{4,6},{6,4},{5,7},{7,5},{8,10},{10,8},{9,1... | collective-permute-start | bytes 786440 | tf_op jit(solution)/shard_map/ppermute | solution.py:24
  126.5 60.3 %copy-start.9 = (bf16[1,768,256]{2,1,0:T(8,128)(2,1)S(1)}, bf16[1,768,256]{2,1,0:T(8,128)(2,1)}, u32[]{:S(2)}) copy-start(bf16[1,768,256]{2,1,0:T(8,128)(2,1)} %get-tuple-element.14) | copy-start | bytes 1179652
  126.5 20.3 %collective-permute-start.6 = (bf16[128,512]{0,1:T(8,128)(2,1)S(1)}, bf16[128,512]{0,1:T(8,128)(2,1)S(1)}, u32[]{:S(2)}, u32[]{:S(2)}) collective-permute-start(bf16[128,512]{0,1:T(8,128)(2,1)S(1)} %fusion.24), channel_id=1, source_target_pairs={{0,4},{4,0},{1,5},{5,1},{2,6},{6,2},{3,7},{7,3},{8,12},{12,8},{9,1... | collective-permute-start | bytes 393224 | tf_op jit(solution)/shard_map/ppermute | solution.py:24
  146.9 10.1 %copy-start.13 = (bf16[128,512]{0,1:T(8,128)(2,1)}, bf16[128,512]{0,1:T(8,128)(2,1)S(1)}, u32[]{:S(2)}) copy-start(bf16[128,512]{0,1:T(8,128)(2,1)S(1)} %fusion.19) | copy-start | bytes 393220
  146.9 40.8 %copy-start.8 = (bf16[1,768,256]{2,1,0:T(8,128)(2,1)S(1)}, bf16[1,768,256]{2,1,0:T(8,128)(2,1)}, u32[]{:S(2)}) copy-start(bf16[1,768,256]{2,1,0:T(8,128)(2,1)} %get-tuple-element.15) | copy-start | bytes 1179652
  146.9 8.2 %collective-permute-start.7 = (bf16[128,512]{0,1:T(8,128)(2,1)S(1)}, bf16[128,512]{0,1:T(8,128)(2,1)S(1)}, u32[]{:S(2)}, u32[]{:S(2)}) collective-permute-start(bf16[128,512]{0,1:T(8,128)(2,1)S(1)} %fusion.19), channel_id=1, source_target_pairs={{0,8},{1,9},{2,10},{3,11},{4,12},{5,13},{6,14},{7,15},{8,16},{9,17... | collective-permute-start | bytes 393224 | tf_op jit(solution)/shard_map/ppermute | solution.py:30
  155.1 3.2 %collective-permute-start.8 = (bf16[128,512]{0,1:T(8,128)(2,1)S(1)}, bf16[128,512]{0,1:T(8,128)(2,1)S(1)}, u32[]{:S(2)}, u32[]{:S(2)}) collective-permute-start(bf16[128,512]{0,1:T(8,128)(2,1)S(1)} %collective-permute-done.7), channel_id=1, source_target_pairs={{0,1},{1,0},{2,3},{3,2},{4,5},{5,4},{6,7},{7,6},{8,9},{9,8},{10,11... | collective-permute-start | bytes 393224 | tf_op jit(solution)/shard_map/ppermute | solution.py:24
  158.4 21.6 %collective-permute-start.9 = (bf16[128,2,512]{0,2,1:T(8,128)(2,1)S(1)}, bf16[128,2,512]{0,2,1:T(8,128)(2,1)S(1)}, u32[]{:S(2)}, u32[]{:S(2)}) collective-permute-start(bf16[128,2,512]{0,2,1:T(8,128)(2,1)S(1)} %pad_maximum_fusion.5), channel_id=1, source_target_pairs={{0,2},{2,0},{1,3},{3,1},{4,6},{6,4},{5,7},{7,5},{8,10},{10,8},{9,1... | collective-permute-start | bytes 786440 | tf_op jit(solution)/shard_map/ppermute | solution.py:24
  180.9 36.7 %collective-permute-start.10 = (bf16[128,2,2,512]{0,3,2,1:T(8,128)(2,1)}, bf16[128,2,2,512]{0,3,2,1:T(8,128)(2,1)}, u32[]{:S(2)}, u32[]{:S(2)}) collective-permute-start(bf16[128,2,2,512]{0,3,2,1:T(8,128)(2,1)} %pad_maximum_fusion.1), channel_id=1, source_target_pairs={{0,4},{4,0},{1,5},{5,1},{2,6},{6,2},{3,7},{7,3},{8,12},{12,8},{9,1... | collective-permute-start | bytes 1572872 | tf_op jit(solution)/shard_map/ppermute | solution.py:24
  219.4 1.6 copy-start.4
  221.0 1.0 copy-start.10
  237.8 4.7 %copy-start.1 = (f32[128,2,2,1,512]{0,4,1,2,3:T(8,128)S(1)}, f32[128,2,2,1,512]{0,4,1,2,3:T(8,128)}, u32[]{:S(2)}) copy-start(f32[128,2,2,1,512]{0,4,1,2,3:T(8,128)} %copy.33) | copy-start | bytes 3145732
  237.9 4.6 %collective-permute-start.11 = (bf16[128,2,2,512]{0,3,1,2:T(8,128)(2,1)S(1)}, bf16[128,2,2,512]{0,3,1,2:T(8,128)(2,1)S(1)}, u32[]{:S(2)}, u32[]{:S(2)}) collective-permute-start(bf16[128,2,2,512]{0,3,1,2:T(8,128)(2,1)S(1)} %fusion.7), channel_id=1, source_target_pairs={{0,1},{1,0},{2,3},{3,2},{4,5},{5,4},{6,7},{7,6},{8,9},{9,8},{10,11... | collective-permute-start | bytes 1572872 | tf_op jit(solution)/shard_map/ppermute | solution.py:24
  242.7 27.5 %copy-start.14 = (bf16[128,512]{0,1:T(8,128)(2,1)S(1)}, bf16[128,512]{0,1:T(8,128)(2,1)}, u32[]{:S(2)}) copy-start(bf16[128,512]{0,1:T(8,128)(2,1)} %copy-done.13) | copy-start | bytes 393220
  242.7 19.9 %collective-permute-start.12 = (bf16[128,2,512]{0,2,1:T(8,128)(2,1)S(1)}, bf16[128,2,512]{0,2,1:T(8,128)(2,1)S(1)}, u32[]{:S(2)}, u32[]{:S(2)}) collective-permute-start(bf16[128,2,512]{0,2,1:T(8,128)(2,1)S(1)} %fusion.15), channel_id=1, source_target_pairs={{0,2},{2,0},{1,3},{3,1},{4,6},{6,4},{5,7},{7,5},{8,10},{10,8},{9,1... | collective-permute-start | bytes 786440 | tf_op jit(solution)/shard_map/ppermute | solution.py:24
  262.8 16.2 %collective-permute-start.13 = (bf16[128,512]{0,1:T(8,128)(2,1)S(1)}, bf16[128,512]{0,1:T(8,128)(2,1)S(1)}, u32[]{:S(2)}, u32[]{:S(2)}) collective-permute-start(bf16[128,512]{0,1:T(8,128)(2,1)S(1)} %fusion.25), channel_id=1, source_target_pairs={{0,4},{4,0},{1,5},{5,1},{2,6},{6,2},{3,7},{7,3},{8,12},{12,8},{9,1... | collective-permute-start | bytes 393224 | tf_op jit(solution)/shard_map/ppermute | solution.py:24
where the time goes:
time: 281 us; the launch traced here: 280 us
  waiting for transfers between devices  144 us (51%)
  starting transfers between devices  76.7 us (27%)
  local copies, waits for them, and re-layouts  42.2 us (15%)
  other arithmetic  11.9 us (4%)
  matrix products  4.09 us (1%)
    ppermute x12, waiting for transfers between devices, swapped(): return lax.ppermute(block, axis, route)  138 us
    ppermute x12, starting transfers between devices, swapped(): return lax.ppermute(block, axis, route)  68.5 us
    unnamed x39, local copies, waits for them, and re-layouts  18.6 us
    slice x2, local copies, waits for them, and re-layouts, share_sums(): upper_half = lax.index_in_dim(current, 1, axis_pos, keepdims=False)  11.4 us
    ppermute x2, starting transfers between devices, passed_along(): return lax.ppermute(block, axis, route)  8.2 us
    another operation x10, other arithmetic, assemble(): current = jnp.stack([lower_half, upper_half], axis=1)  6.82 us
    reshape x2, local copies, waits for them, and re-layouts, share_sums(): partial_value.reshape((tok_rows,) + (2,) * total_bits + (partial_value.sh...  6.1 us
  transfers between devices with their start and end apart: 14, of which 13 were waited for; matrix products, arithmetic and copies ran while one was open for 4% of the time, Pallas kernels for 0%

commit v1 on v0

v1 whole, which is shorter than its diff:
```python
import functools

import jax
import jax.numpy as jnp
from jax import lax
from jax.experimental import pallas as pl
from jax.experimental.pallas import tpu as pltpu
from jax.sharding import PartitionSpec as P

HD = 128
SECT = 8
CH = 64
SPAN = 256
EPS = 1e-05
CORES = 2


def z_route(size, per_section, step, sections_on=0, swap_core=False):
    route = []
    chips = per_section // CORES
    for source in range(size):
        section, group = divmod(source, per_section)
        chip, core = divmod(group, CORES)
        target_section = section + sections_on
        if target_section >= size // per_section:
            continue
        core = core ^ 1 if swap_core else core
        target = target_section * per_section + (chip + step) % chips * CORES + core
        route.append((source, target))
    return route


def along_z(block, step, sections_on=0, swap_core=False):
    size = lax.axis_size("segment")
    return lax.ppermute(block, "segment", z_route(size, size // SECT, step, sections_on, swap_core))


def along_seq(block, step):
    size = lax.axis_size("seq")
    return lax.ppermute(block, "seq", [(i, (i + step) % size) for i in range(size)])


def layer_kernel(chips, where_ref, x_refs, other_ref, wq_ref, kv_ref, wo_ref, mine_ref, send_ref):
    chip = where_ref[0]
    core = where_ref[1]
    masked = where_ref[2]
    rows = x_refs[0].shape[0]
    width = x_refs[0].shape[1]
    total = jnp.zeros((rows, 1), jnp.float32)
    queries = jnp.zeros((rows, wq_ref.shape[1]), jnp.float32)
    for k in range(chips):
        source = lax.rem(chip - k + chips, chips) * CORES
        for part, owner in ((x_refs[k][...], core), (other_ref[pl.ds(k * rows, rows), :], 1 - core)):
            wide = part.astype(jnp.float32)
            total += jnp.sum(wide * wide, axis=-1, keepdims=True)
            offset = pl.multiple_of((source + owner) * width, width)
            queries += jnp.dot(part, wq_ref[pl.ds(offset, width), :], preferred_element_type=jnp.float32)
    scale = lax.rsqrt(total / (2 * chips * width) + EPS)
    queries = (queries * scale).astype(jnp.bfloat16)
    heads = []
    for h in range(queries.shape[1] // HD):
        cols = slice(h * HD, (h + 1) * HD)
        scores = lax.dot_general(
            queries[:, cols], kv_ref[0, :, cols], (((1,), (1,)), ((), ())), preferred_element_type=jnp.float32
        ) * HD ** (-0.5)
        exponent = jnp.exp(scores)
        weights = (exponent / jnp.sum(exponent, axis=-1, keepdims=True)).astype(jnp.bfloat16)
        heads.append(jnp.dot(weights, kv_ref[1, :, cols], preferred_element_type=jnp.float32))
    attended = jnp.concatenate(heads, axis=1)
    row = lax.broadcasted_iota(jnp.int32, attended.shape, 0)
    attended = jnp.where((masked > 0) & (row < rows - 1), 0.0, attended).astype(jnp.bfloat16)
    for k in range(chips):
        target = lax.rem(chip + k, chips) * CORES
        for out_ref, owner in ((mine_ref, core), (send_ref, 1 - core)):
            offset = pl.multiple_of((target + owner) * width, width)
            out_ref[pl.ds(k * rows, rows), :] = jnp.dot(
                attended, wo_ref[:, pl.ds(offset, width)], preferred_element_type=jnp.float32
            ).astype(jnp.bfloat16)


def layer(where, blocks, other, w_query, kv, w_out):
    chips = len(blocks)
    rows, width = blocks[0].shape

    def body(where_ref, *refs):
        layer_kernel(chips, where_ref, refs[:chips], *refs[chips:])

    vmem = pl.BlockSpec(memory_space=pltpu.VMEM)
    shape = jax.ShapeDtypeStruct((chips * rows, width), jnp.bfloat16)
    return pl.pallas_call(
        body,
        in_specs=[pl.BlockSpec(memory_space=pltpu.SMEM)] + [vmem] * (chips + 4),
        out_specs=(vmem, vmem),
        out_shape=(shape, shape),
        cost_estimate=pl.CostEstimate(flops=300_000_000, bytes_accessed=10_000_000, transcendentals=40_000),
        name="layer",
    )(where, *blocks, other, w_query, kv, w_out)


def per_device(stream, w_query, w_out, neighbour_kv):
    per_section = lax.axis_size("segment") // SECT
    chips = per_section // CORES
    group = lax.axis_index("segment") % per_section
    seq = lax.axis_index("seq")
    last = (seq == lax.axis_size("seq") - 1).astype(jnp.int32)
    half = stream.shape[0] // 2
    top, low = stream[:half], stream[half:]
    row = lax.broadcasted_iota(jnp.int32, low.shape, 0)
    end = row == half - 1
    inputs = [jnp.where(end, top[half - 1 :], low)]
    inputs.append(jnp.where(end, low[half - 1 :], along_seq(top, -1)))
    outputs = [[], []]
    results = [None, None]
    for tick in range(2):
        for chunk in range(2):
            where = jnp.stack([group // CORES, group % CORES, last * chunk]).astype(jnp.int32)
            kv = neighbour_kv[tick, :, chunk * SPAN : (chunk + 1) * SPAN, :]
            if tick == 0:
                blocks = [inputs[chunk]] + [along_z(inputs[chunk], k) for k in range(1, chips)]
            else:
                blocks = [along_z(results[chunk], k, 1) for k in range(chips)]
            other = along_z(jnp.concatenate(blocks, axis=0), 0, 0, True)
            mine, send = layer(where, blocks, other, w_query, kv, w_out)
            received = along_z(send, 0, 0, True)
            total = mine.astype(jnp.float32) + received.astype(jnp.float32)
            sums = total.astype(jnp.bfloat16)
            rest = [along_z(sums[k * half : (k + 1) * half], k) for k in range(1, chips)]
            result = blocks[0].astype(jnp.float32) + total[:half]
            for part in rest:
                result = result + part.astype(jnp.float32)
            results[chunk] = result.astype(jnp.bfloat16)
        moved = along_seq(results[1], 1)
        outputs[tick] = jnp.concatenate(
            [jnp.where(end, results[0][half - 1 :], moved), jnp.where(end, results[1][half - 1 :], results[0])], axis=0
        )
    return tuple(outputs)


def solution(mesh):
    placed = (
        P("seq", "segment"),
        P(None, "segment"),
        P("segment", None),
        P(None, None, "seq", "segment"),
    )
    return jax.shard_map(
        per_device,
        mesh=mesh,
        in_specs=placed,
        out_specs=(P("seq", "segment"), P("seq", "segment")),
        check_vma=False,
    )
```

time: 281 us -> 222 us (0.79)
  the two profiles are of different devices: /device:TPU:38 before, /device:TPU:8 now
where the time goes in v1:
time: 222 us; the launch traced here: 221 us
  starting transfers between devices  163 us (73%)
  waiting for transfers between devices  23.7 us (11%)
  Pallas kernels  20.8 us (9%)
  local copies, waits for them, and re-layouts  5.94 us (3%)
  other arithmetic  5.73 us (3%)
    ppermute x34, starting transfers between devices, along_z(): lax.ppermute(block, 'segment', z_route(size, size // SECT, step, sections...  147 us
    ppermute x34, waiting for transfers between devices, along_z(): lax.ppermute(block, 'segment', z_route(size, size // SECT, step, sections...  23.7 us
    pallas_call x4, Pallas kernels, layer(): pl.pallas_call(body, in_specs=[pl.BlockSpec(memory_space=pltpu.SMEM)] + [...  20.8 us
    ppermute x3, starting transfers between devices, along_seq(): lax.ppermute(block, 'seq', [(i, (i + step) % size) for i in range(size)])  16.1 us
  transfers between devices with their start and end apart: 37, of which 10 were waited for; matrix products, arithmetic and copies ran while one was open for 2% of the time, Pallas kernels for 9%

profile of v1, /device:TPU:8, one launch (start us, length us, event | category | flops | bytes accessed | tf_op | source)
XLA Modules:
  0.0 221.1 jit_solution(13731330461187250991)
XLA Ops:
  0.6 0.7 slice_reduce_fusion.4
  1.4 1.0 slice_select_fusion
  2.3 8.3 %collective-permute-start.8 = (bf16[64,512]{1,0:T(8,128)(2,1)S(1)}, bf16[64,512]{1,0:T(8,128)(2,1)S(1)}, u32[]{:S(2)}, u32[]{:S(2)}) collective-permute-start(bf16[64,512]{1,0:T(8,128)(2,1)S(1)} %get-tuple-element.49), channel_id=1, source_target_pairs={{0,704},{64,0},{128,64},{192,128},{256,192},{320,256},{384,320},{4... | collective-permute-start | bytes 196616 | tf_op jit(solution)/shard_map/ppermute | solution.py:40
  10.6 9.1 %collective-permute-start = (bf16[64,512]{1,0:T(8,128)(2,1)S(1)}, bf16[64,512]{1,0:T(8,128)(2,1)S(1)}, u32[]{:S(2)}, u32[]{:S(2)}) collective-permute-start(bf16[64,512]{1,0:T(8,128)(2,1)S(1)} %get-tuple-element.48.refs_0_), channel_id=1, source_target_pairs={{0,2},{1,3},{2,4},{3,5},{4,6},{5,7},{6,0},{7,1},{8,10},{9,11},{10,... | collective-permute-start | bytes 196616 | tf_op jit(solution)/shard_map/ppermute | solution.py:35
  19.8 10.0 %collective-permute-start.1 = (bf16[64,512]{1,0:T(8,128)(2,1)S(1)}, bf16[64,512]{1,0:T(8,128)(2,1)S(1)}, u32[]{:S(2)}, u32[]{:S(2)}) collective-permute-start(bf16[64,512]{1,0:T(8,128)(2,1)S(1)} %get-tuple-element.48.refs_0_), channel_id=1, source_target_pairs={{0,4},{1,5},{2,6},{3,7},{4,0},{5,1},{6,2},{7,3},{8,12},{9,13},{10,... | collective-permute-start | bytes 196616 | tf_op jit(solution)/shard_map/ppermute | solution.py:35
  29.8 3.0 %collective-permute-start.2 = (bf16[64,512]{1,0:T(8,128)(2,1)S(1)}, bf16[64,512]{1,0:T(8,128)(2,1)S(1)}, u32[]{:S(2)}, u32[]{:S(2)}) collective-permute-start(bf16[64,512]{1,0:T(8,128)(2,1)S(1)} %get-tuple-element.48.refs_0_), channel_id=1, source_target_pairs={{0,6},{1,7},{2,0},{3,1},{4,2},{5,3},{6,4},{7,5},{8,14},{9,15},{10,... | collective-permute-start | bytes 196616 | tf_op jit(solution)/shard_map/ppermute | solution.py:35
  33.0 4.6 %collective-permute-start.9 = (bf16[64,512]{1,0:T(8,128)(2,1)S(1)}, bf16[64,512]{1,0:T(8,128)(2,1)S(1)}, u32[]{:S(2)}, u32[]{:S(2)}) collective-permute-start(bf16[64,512]{1,0:T(8,128)(2,1)S(1)} %broadcast_select_fusion.4.refs_0_), channel_id=1, source_target_pairs={{0,2},{1,3},{2,4},{3,5},{4,6},{5,7},{6,0},{7,1},{8,10},{9,11},{10,... | collective-permute-start | bytes 196616 | tf_op jit(solution)/shard_map/ppermute | solution.py:35
  37.6 3.7 %collective-permute-start.10 = (bf16[64,512]{1,0:T(8,128)(2,1)S(1)}, bf16[64,512]{1,0:T(8,128)(2,1)S(1)}, u32[]{:S(2)}, u32[]{:S(2)}) collective-permute-start(bf16[64,512]{1,0:T(8,128)(2,1)S(1)} %broadcast_select_fusion.4.refs_0_), channel_id=1, source_target_pairs={{0,4},{1,5},{2,6},{3,7},{4,0},{5,1},{6,2},{7,3},{8,12},{9,13},{10,... | collective-permute-start | bytes 196616 | tf_op jit(solution)/shard_map/ppermute | solution.py:35
  41.3 5.2 %collective-permute-start.11 = (bf16[64,512]{1,0:T(8,128)(2,1)S(1)}, bf16[64,512]{1,0:T(8,128)(2,1)S(1)}, u32[]{:S(2)}, u32[]{:S(2)}) collective-permute-start(bf16[64,512]{1,0:T(8,128)(2,1)S(1)} %broadcast_select_fusion.4.refs_0_), channel_id=1, source_target_pairs={{0,6},{1,7},{2,0},{3,1},{4,2},{5,3},{6,4},{7,5},{8,14},{9,15},{10,... | collective-permute-start | bytes 196616 | tf_op jit(solution)/shard_map/ppermute | solution.py:35
  46.6 1.9 collective-permute-start.3
  48.5 2.2 slice_bitcast_fusion.1
  50.7 0.9 collective-permute-done.11.refs_3_
  51.7 1.9 collective-permute-start.12
  53.6 0.6 pad_add_fusion.where_ref
  54.2 0.7 copy-done.19
  54.9 5.2 %layer.4 = (bf16[256,512]{1,0:T(8,128)(2,1)}, bf16[256,512]{1,0:T(8,128)(2,1)}) custom-call(s32[3]{0:T(128)} %pad_add_fusion.where_ref, bf16[64,512]{1,0:T(8,128)(2,1)} %copy-done, bf16[64,512]{1,0:T(8,128)(2,1)} %copy-done.10, bf16[64,512]{1,0:T(8,128)(2,1)} %copy-done.11, bf16[64,512]{1,0:T(8,128)(2,1)} %copy-done.12, bf16[256,512]{1,0:T(8,128)(2,1)} %copy-done.19, ...), custom_call_target="tpu_custom_call" | custom-call | flops 300000000 | bytes 10000000 | tf_op jit(solution)/shard_map/layer/pallas_call | solution.py:90
  60.1 2.4 %collective-permute-start.4 = (bf16[256,512]{1,0:T(8,128)(2,1)}, bf16[256,512]{1,0:T(8,128)(2,1)S(1)}, u32[]{:S(2)}, u32[]{:S(2)}) collective-permute-start(bf16[256,512]{1,0:T(8,128)(2,1)} %get-tuple-element.11), channel_id=1, source_target_pairs={{0,1},{1,0},{2,3},{3,2},{4,5},{5,4},{6,7},{7,6},{8,9},{9,8},{10,11... | collective-permute-start | bytes 786440 | tf_op jit(solution)/shard_map/ppermute | solution.py:35
  62.6 0.7 pad_add_fusion.2.where_ref
  63.2 0.7 copy-done.22
  63.9 5.2 %layer.5 = (bf16[256,512]{1,0:T(8,128)(2,1)}, bf16[256,512]{1,0:T(8,128)(2,1)}) custom-call(s32[3]{0:T(128)} %pad_add_fusion.2.where_ref, bf16[64,512]{1,0:T(8,128)(2,1)} %copy-done.6, bf16[64,512]{1,0:T(8,128)(2,1)} %copy-done.7, bf16[64,512]{1,0:T(8,128)(2,1)} %copy-done.8, bf16[64,512]{1,0:T(8,128)(2,1)} %copy-done.9, bf16[256,512]{1,0:T(8,128)(2,1)} %copy-done.22, ...), custom_call_target="tpu_custom_call" | custom-call | flops 300000000 | bytes 10000000 | tf_op jit(solution)/shard_map/layer/pallas_call | solution.py:90
  69.1 1.9 collective-permute-start.13
  71.2 1.6 collective-permute-done.13
  72.8 1.0 fusion.17
  73.8 4.9 %collective-permute-start.16 = (bf16[64,512]{1,0:T(8,128)(2,1)S(1)}, bf16[64,512]{1,0:T(8,128)(2,1)S(1)}, u32[]{:S(2)}, u32[]{:S(2)}) collective-permute-start(bf16[64,512]{1,0:T(8,128)(2,1)S(1)} %get-tuple-element.46), channel_id=1, source_target_pairs={{0,6},{1,7},{2,0},{3,1},{4,2},{5,3},{6,4},{7,5},{8,14},{9,15},{10,... | collective-permute-start | bytes 196616 | tf_op jit(solution)/shard_map/ppermute | solution.py:35
  78.8 7.3 %collective-permute-start.15 = (bf16[64,512]{1,0:T(8,128)(2,1)S(1)}, bf16[64,512]{1,0:T(8,128)(2,1)S(1)}, u32[]{:S(2)}, u32[]{:S(2)}) collective-permute-start(bf16[64,512]{1,0:T(8,128)(2,1)S(1)} %get-tuple-element.47), channel_id=1, source_target_pairs={{0,4},{1,5},{2,6},{3,7},{4,0},{5,1},{6,2},{7,3},{8,12},{9,13},{10,... | collective-permute-start | bytes 196616 | tf_op jit(solution)/shard_map/ppermute | solution.py:35
  86.1 3.4 %collective-permute-start.14 = (bf16[64,512]{1,0:T(8,128)(2,1)S(1)}, bf16[64,512]{1,0:T(8,128)(2,1)S(1)}, u32[]{:S(2)}, u32[]{:S(2)}) collective-permute-start(bf16[64,512]{1,0:T(8,128)(2,1)S(1)} %get-tuple-element.45), channel_id=1, source_target_pairs={{0,2},{1,3},{2,4},{3,5},{4,6},{5,7},{6,0},{7,1},{8,10},{9,11},{10,... | collective-permute-start | bytes 196616 | tf_op jit(solution)/shard_map/ppermute | solution.py:35
  89.5 5.4 %collective-permute-start.7 = (bf16[64,512]{1,0:T(8,128)(2,1)S(1)}, bf16[64,512]{1,0:T(8,128)(2,1)S(1)}, u32[]{:S(2)}, u32[]{:S(2)}) collective-permute-start(bf16[64,512]{1,0:T(8,128)(2,1)S(1)} %get-tuple-element.43), channel_id=1, source_target_pairs={{0,6},{1,7},{2,0},{3,1},{4,2},{5,3},{6,4},{7,5},{8,14},{9,15},{10,... | collective-permute-start | bytes 196616 | tf_op jit(solution)/shard_map/ppermute | solution.py:35
  95.0 0.2 collective-permute-done.15
  95.2 1.4 collective-permute-done.14
  96.5 0.1 fusion.11
  96.7 3.5 %collective-permute-start.27 = (bf16[64,512]{1,0:T(8,128)(2,1)S(1)}, bf16[64,512]{1,0:T(8,128)(2,1)S(1)}, u32[]{:S(2)}, u32[]{:S(2)}) collective-permute-start(bf16[64,512]{1,0:T(8,128)(2,1)S(1)} %fusion.11), channel_id=1, source_target_pairs={{0,8},{1,9},{2,10},{3,11},{4,12},{5,13},{6,14},{7,15},{8,16},{9,17... | collective-permute-start | bytes 196616 | tf_op jit(solution)/shard_map/ppermute | solution.py:35
  100.2 4.1 %collective-permute-start.28 = (bf16[64,512]{1,0:T(8,128)(2,1)S(1)}, bf16[64,512]{1,0:T(8,128)(2,1)S(1)}, u32[]{:S(2)}, u32[]{:S(2)}) collective-permute-start(bf16[64,512]{1,0:T(8,128)(2,1)S(1)} %fusion.11), channel_id=1, source_target_pairs={{0,10},{1,11},{2,12},{3,13},{4,14},{5,15},{6,8},{7,9},{8,18},{9,19... | collective-permute-start | bytes 196616 | tf_op jit(solution)/shard_map/ppermute | solution.py:35
  104.3 8.4 %collective-permute-start.29 = (bf16[64,512]{1,0:T(8,128)(2,1)S(1)}, bf16[64,512]{1,0:T(8,128)(2,1)S(1)}, u32[]{:S(2)}, u32[]{:S(2)}) collective-permute-start(bf16[64,512]{1,0:T(8,128)(2,1)S(1)} %fusion.11), channel_id=1, source_target_pairs={{0,12},{1,13},{2,14},{3,15},{4,8},{5,9},{6,10},{7,11},{8,20},{9,21... | collective-permute-start | bytes 196616 | tf_op jit(solution)/shard_map/ppermute | solution.py:35
  112.7 4.1 %collective-permute-start.30 = (bf16[64,512]{1,0:T(8,128)(2,1)S(1)}, bf16[64,512]{1,0:T(8,128)(2,1)S(1)}, u32[]{:S(2)}, u32[]{:S(2)}) collective-permute-start(bf16[64,512]{1,0:T(8,128)(2,1)S(1)} %fusion.11), channel_id=1, source_target_pairs={{0,14},{1,15},{2,8},{3,9},{4,10},{5,11},{6,12},{7,13},{8,22},{9,23... | collective-permute-start | bytes 196616 | tf_op jit(solution)/shard_map/ppermute | solution.py:35
  116.8 8.3 %collective-permute-start.6 = (bf16[64,512]{1,0:T(8,128)(2,1)S(1)}, bf16[64,512]{1,0:T(8,128)(2,1)S(1)}, u32[]{:S(2)}, u32[]{:S(2)}) collective-permute-start(bf16[64,512]{1,0:T(8,128)(2,1)S(1)} %get-tuple-element.44), channel_id=1, source_target_pairs={{0,4},{1,5},{2,6},{3,7},{4,0},{5,1},{6,2},{7,3},{8,12},{9,13},{10,... | collective-permute-start | bytes 196616 | tf_op jit(solution)/shard_map/ppermute | solution.py:35
  125.2 1.9 collective-permute-start.5
  127.2 1.9 collective-permute-start.31
  129.2 1.9 collective-permute-done.6
  131.0 4.9 %collective-permute-done.5 = bf16[64,512]{1,0:T(8,128)(2,1)S(1)} collective-permute-done((bf16[64,512]{1,0:T(8,128)(2,1)S(1)}, bf16[64,512]{1,0:T(8,128)(2,1)S(1)}, u32[]{:S(2)}, u32[]{:S(2)}) %collective-permute-start.5) | collective-permute-done | bytes 65568 | tf_op jit(solution)/shard_map/ppermute | solution.py:35
  136.1 2.6 %collective-permute-start.18 = (bf16[64,512]{1,0:T(8,128)(2,1)S(1)}, bf16[64,512]{1,0:T(8,128)(2,1)S(1)}, u32[]{:S(2)}, u32[]{:S(2)}) collective-permute-start(bf16[64,512]{1,0:T(8,128)(2,1)S(1)} %get-tuple-element.23), channel_id=1, source_target_pairs={{0,8},{1,9},{2,10},{3,11},{4,12},{5,13},{6,14},{7,15},{8,16},{9,17... | collective-permute-start | bytes 196616 | tf_op jit(solution)/shard_map/ppermute | solution.py:35
  138.7 2.6 %collective-permute-start.19 = (bf16[64,512]{1,0:T(8,128)(2,1)S(1)}, bf16[64,512]{1,0:T(8,128)(2,1)S(1)}, u32[]{:S(2)}, u32[]{:S(2)}) collective-permute-start(bf16[64,512]{1,0:T(8,128)(2,1)S(1)} %get-tuple-element.23), channel_id=1, source_target_pairs={{0,10},{1,11},{2,12},{3,13},{4,14},{5,15},{6,8},{7,9},{8,18},{9,19... | collective-permute-start | bytes 196616 | tf_op jit(solution)/shard_map/ppermute | solution.py:35
  141.3 5.7 %collective-permute-start.20 = (bf16[64,512]{1,0:T(8,128)(2,1)S(1)}, bf16[64,512]{1,0:T(8,128)(2,1)S(1)}, u32[]{:S(2)}, u32[]{:S(2)}) collective-permute-start(bf16[64,512]{1,0:T(8,128)(2,1)S(1)} %get-tuple-element.23), channel_id=1, source_target_pairs={{0,12},{1,13},{2,14},{3,15},{4,8},{5,9},{6,10},{7,11},{8,20},{9,21... | collective-permute-start | bytes 196616 | tf_op jit(solution)/shard_map/ppermute | solution.py:35
  147.0 4.1 %collective-permute-start.21 = (bf16[64,512]{1,0:T(8,128)(2,1)S(1)}, bf16[64,512]{1,0:T(8,128)(2,1)S(1)}, u32[]{:S(2)}, u32[]{:S(2)}) collective-permute-start(bf16[64,512]{1,0:T(8,128)(2,1)S(1)} %get-tuple-element.23), channel_id=1, source_target_pairs={{0,14},{1,15},{2,8},{3,9},{4,10},{5,11},{6,12},{7,13},{8,22},{9,23... | collective-permute-start | bytes 196616 | tf_op jit(solution)/shard_map/ppermute | solution.py:35
  151.2 3.7 %collective-permute-done.20.refs_2_ = bf16[64,512]{1,0:T(8,128)(2,1)S(1)} collective-permute-done((bf16[64,512]{1,0:T(8,128)(2,1)S(1)}, bf16[64,512]{1,0:T(8,128)(2,1)S(1)}, u32[]{:S(2)}, u32[]{:S(2)}) %collective-permute-start.20) | collective-permute-done | bytes 65568 | tf_op jit(solution)/shard_map/ppermute | solution.py:35
  154.9 2.8 %collective-permute-done.21.refs_3_ = bf16[64,512]{1,0:T(8,128)(2,1)S(1)} collective-permute-done((bf16[64,512]{1,0:T(8,128)(2,1)S(1)}, bf16[64,512]{1,0:T(8,128)(2,1)S(1)}, u32[]{:S(2)}, u32[]{:S(2)}) %collective-permute-start.21) | collective-permute-done | bytes 65568 | tf_op jit(solution)/shard_map/ppermute | solution.py:35
  157.7 1.9 collective-permute-start.22
  159.7 0.7 copy-done.20
  160.4 5.2 %layer.7 = (bf16[256,512]{1,0:T(8,128)(2,1)}, bf16[256,512]{1,0:T(8,128)(2,1)}) custom-call(s32[3]{0:T(128)} %pad_add_fusion.2.where_ref, bf16[64,512]{1,0:T(8,128)(2,1)} %copy-done.2, bf16[64,512]{1,0:T(8,128)(2,1)} %copy-done.13, bf16[64,512]{1,0:T(8,128)(2,1)} %copy-done.14, bf16[64,512]{1,0:T(8,128)(2,1)} %copy-done.15, bf16[256,512]{1,0:T(8,128)(2,1)} %copy-done.20, ...), custom_call_target="tpu_custom_call" | custom-call | flops 300000000 | bytes 10000000 | tf_op jit(solution)/shard_map/layer/pallas_call | solution.py:90
  165.6 2.4 %collective-permute-start.32 = (bf16[256,512]{1,0:T(8,128)(2,1)}, bf16[256,512]{1,0:T(8,128)(2,1)S(1)}, u32[]{:S(2)}, u32[]{:S(2)}) collective-permute-start(bf16[256,512]{1,0:T(8,128)(2,1)} %get-tuple-element.17), channel_id=1, source_target_pairs={{0,1},{1,0},{2,3},{3,2},{4,5},{5,4},{6,7},{7,6},{8,9},{9,8},{10,11... | collective-permute-start | bytes 786440 | tf_op jit(solution)/shard_map/ppermute | solution.py:35
  168.0 3.5 %collective-permute-start.17 = (bf16[64,512]{1,0:T(8,128)(2,1)S(1)}, bf16[64,512]{1,0:T(8,128)(2,1)S(1)}, u32[]{:S(2)}, u32[]{:S(2)}) collective-permute-start(bf16[64,512]{1,0:T(8,128)(2,1)S(1)} %fusion.11), channel_id=1, source_target_pairs={{0,64},{64,128},{128,192},{192,256},{256,320},{320,384},{384,448},... | collective-permute-start | bytes 196616 | tf_op jit(solution)/shard_map/ppermute | solution.py:40
  171.6 0.7 copy-done.24
  172.3 5.3 %layer.6 = (bf16[256,512]{1,0:T(8,128)(2,1)}, bf16[256,512]{1,0:T(8,128)(2,1)}) custom-call(s32[3]{0:T(128)} %pad_add_fusion.where_ref, bf16[64,512]{1,0:T(8,128)(2,1)} %copy-done.4, bf16[64,512]{1,0:T(8,128)(2,1)} %copy-done.16, bf16[64,512]{1,0:T(8,128)(2,1)} %copy-done.17, bf16[64,512]{1,0:T(8,128)(2,1)} %copy-done.18, bf16[256,512]{1,0:T(8,128)(2,1)} %copy-done.24, ...), custom_call_target="tpu_custom_call" | custom-call | flops 300000000 | bytes 10000000 | tf_op jit(solution)/shard_map/layer/pallas_call | solution.py:90
  177.6 2.0 collective-permute-start.23
  179.8 4.4 %collective-permute-start.35 = (bf16[64,512]{1,0:T(8,128)(2,1)S(1)}, bf16[64,512]{1,0:T(8,128)(2,1)S(1)}, u32[]{:S(2)}, u32[]{:S(2)}) collective-permute-start(bf16[64,512]{1,0:T(8,128)(2,1)S(1)} %get-tuple-element.40), channel_id=1, source_target_pairs={{0,6},{1,7},{2,0},{3,1},{4,2},{5,3},{6,4},{7,5},{8,14},{9,15},{10,... | collective-permute-start | bytes 196616 | tf_op jit(solution)/shard_map/ppermute | solution.py:35
  184.2 7.3 %collective-permute-start.34 = (bf16[64,512]{1,0:T(8,128)(2,1)S(1)}, bf16[64,512]{1,0:T(8,128)(2,1)S(1)}, u32[]{:S(2)}, u32[]{:S(2)}) collective-permute-start(bf16[64,512]{1,0:T(8,128)(2,1)S(1)} %get-tuple-element.41), channel_id=1, source_target_pairs={{0,4},{1,5},{2,6},{3,7},{4,0},{5,1},{6,2},{7,3},{8,12},{9,13},{10,... | collective-permute-start | bytes 196616 | tf_op jit(solution)/shard_map/ppermute | solution.py:35
  191.5 5.1 %collective-permute-start.33 = (bf16[64,512]{1,0:T(8,128)(2,1)S(1)}, bf16[64,512]{1,0:T(8,128)(2,1)S(1)}, u32[]{:S(2)}, u32[]{:S(2)}) collective-permute-start(bf16[64,512]{1,0:T(8,128)(2,1)S(1)} %get-tuple-element.39), channel_id=1, source_target_pairs={{0,2},{1,3},{2,4},{3,5},{4,6},{5,7},{6,0},{7,1},{8,10},{9,11},{10,... | collective-permute-start | bytes 196616 | tf_op jit(solution)/shard_map/ppermute | solution.py:35
  196.6 1.0 convert_add_fusion.1
  197.7 3.8 %collective-permute-start.26 = (bf16[64,512]{1,0:T(8,128)(2,1)S(1)}, bf16[64,512]{1,0:T(8,128)(2,1)S(1)}, u32[]{:S(2)}, u32[]{:S(2)}) collective-permute-start(bf16[64,512]{1,0:T(8,128)(2,1)S(1)} %get-tuple-element.37), channel_id=1, source_target_pairs={{0,6},{1,7},{2,0},{3,1},{4,2},{5,3},{6,4},{7,5},{8,14},{9,15},{10,... | collective-permute-start | bytes 196616 | tf_op jit(solution)/shard_map/ppermute | solution.py:35
  201.5 5.1 %collective-permute-start.25 = (bf16[64,512]{1,0:T(8,128)(2,1)S(1)}, bf16[64,512]{1,0:T(8,128)(2,1)S(1)}, u32[]{:S(2)}, u32[]{:S(2)}) collective-permute-start(bf16[64,512]{1,0:T(8,128)(2,1)S(1)} %get-tuple-element.38), channel_id=1, source_target_pairs={{0,4},{1,5},{2,6},{3,7},{4,0},{5,1},{6,2},{7,3},{8,12},{9,13},{10,... | collective-permute-start | bytes 196616 | tf_op jit(solution)/shard_map/ppermute | solution.py:35
  206.6 3.0 %collective-permute-start.24 = (bf16[64,512]{1,0:T(8,128)(2,1)S(1)}, bf16[64,512]{1,0:T(8,128)(2,1)S(1)}, u32[]{:S(2)}, u32[]{:S(2)}) collective-permute-start(bf16[64,512]{1,0:T(8,128)(2,1)S(1)} %get-tuple-element.36), channel_id=1, source_target_pairs={{0,2},{1,3},{2,4},{3,5},{4,6},{5,7},{6,0},{7,1},{8,10},{9,11},{10,... | collective-permute-start | bytes 196616 | tf_op jit(solution)/shard_map/ppermute | solution.py:35
  209.7 4.3 %collective-permute-start.36 = (bf16[64,512]{1,0:T(8,128)(2,1)S(1)}, bf16[64,512]{1,0:T(8,128)(2,1)S(1)}, u32[]{:S(2)}, u32[]{:S(2)}) collective-permute-start(bf16[64,512]{1,0:T(8,128)(2,1)S(1)} %fusion.3), channel_id=1, source_target_pairs={{0,64},{64,128},{128,192},{192,256},{256,320},{320,384},{384,448},... | collective-permute-start | bytes 196616 | tf_op jit(solution)/shard_map/ppermute | solution.py:40
  214.0 1.6 collective-permute-done.25
  215.6 4.6 %collective-permute-done.24 = bf16[64,512]{1,0:T(8,128)(2,1)S(1)} collective-permute-done((bf16[64,512]{1,0:T(8,128)(2,1)S(1)}, bf16[64,512]{1,0:T(8,128)(2,1)S(1)}, u32[]{:S(2)}, u32[]{:S(2)}) %collective-permute-start.24) | collective-permute-done | bytes 65568 | tf_op jit(solution)/shard_map/ppermute | solution.py:35
  220.4 0.7 pad_maximum_fusion.4
  (93 shorter events, 0.9 us)
Async XLA Ops:
  2.3 51.9 %copy-start = (bf16[64,512]{1,0:T(8,128)(2,1)}, bf16[64,512]{1,0:T(8,128)(2,1)S(1)}, u32[]{:S(2)}) copy-start(bf16[64,512]{1,0:T(8,128)(2,1)S(1)} %get-tuple-element.48.refs_0_) | copy-start | bytes 196612
  2.3 30.5 %collective-permute-start.8 = (bf16[64,512]{1,0:T(8,128)(2,1)S(1)}, bf16[64,512]{1,0:T(8,128)(2,1)S(1)}, u32[]{:S(2)}, u32[]{:S(2)}) collective-permute-start(bf16[64,512]{1,0:T(8,128)(2,1)S(1)} %get-tuple-element.49), channel_id=1, source_target_pairs={{0,704},{64,0},{128,64},{192,128},{256,192},{320,256},{384,320},{4... | collective-permute-start | bytes 196616 | tf_op jit(solution)/shard_map/ppermute | solution.py:40
  10.6 30.6 %collective-permute-start = (bf16[64,512]{1,0:T(8,128)(2,1)S(1)}, bf16[64,512]{1,0:T(8,128)(2,1)S(1)}, u32[]{:S(2)}, u32[]{:S(2)}) collective-permute-start(bf16[64,512]{1,0:T(8,128)(2,1)S(1)} %get-tuple-element.48.refs_0_), channel_id=1, source_target_pairs={{0,2},{1,3},{2,4},{3,5},{4,6},{5,7},{6,0},{7,1},{8,10},{9,11},{10,... | collective-permute-start | bytes 196616 | tf_op jit(solution)/shard_map/ppermute | solution.py:35
  19.8 26.8 %collective-permute-start.1 = (bf16[64,512]{1,0:T(8,128)(2,1)S(1)}, bf16[64,512]{1,0:T(8,128)(2,1)S(1)}, u32[]{:S(2)}, u32[]{:S(2)}) collective-permute-start(bf16[64,512]{1,0:T(8,128)(2,1)S(1)} %get-tuple-element.48.refs_0_), channel_id=1, source_target_pairs={{0,4},{1,5},{2,6},{3,7},{4,0},{5,1},{6,2},{7,3},{8,12},{9,13},{10,... | collective-permute-start | bytes 196616 | tf_op jit(solution)/shard_map/ppermute | solution.py:35
  29.8 16.7 %collective-permute-start.2 = (bf16[64,512]{1,0:T(8,128)(2,1)S(1)}, bf16[64,512]{1,0:T(8,128)(2,1)S(1)}, u32[]{:S(2)}, u32[]{:S(2)}) collective-permute-start(bf16[64,512]{1,0:T(8,128)(2,1)S(1)} %get-tuple-element.48.refs_0_), channel_id=1, source_target_pairs={{0,6},{1,7},{2,0},{3,1},{4,2},{5,3},{6,4},{7,5},{8,14},{9,15},{10,... | collective-permute-start | bytes 196616 | tf_op jit(solution)/shard_map/ppermute | solution.py:35
  33.0 27.2 %copy-start.6 = (bf16[64,512]{1,0:T(8,128)(2,1)}, bf16[64,512]{1,0:T(8,128)(2,1)S(1)}, u32[]{:S(2)}) copy-start(bf16[64,512]{1,0:T(8,128)(2,1)S(1)} %broadcast_select_fusion.4.refs_0_) | copy-start | bytes 196612
  33.0 17.7 %collective-permute-start.9 = (bf16[64,512]{1,0:T(8,128)(2,1)S(1)}, bf16[64,512]{1,0:T(8,128)(2,1)S(1)}, u32[]{:S(2)}, u32[]{:S(2)}) collective-permute-start(bf16[64,512]{1,0:T(8,128)(2,1)S(1)} %broadcast_select_fusion.4.refs_0_), channel_id=1, source_target_pairs={{0,2},{1,3},{2,4},{3,5},{4,6},{5,7},{6,0},{7,1},{8,10},{9,11},{10,... | collective-permute-start | bytes 196616 | tf_op jit(solution)/shard_map/ppermute | solution.py:35
  37.6 13.1 %collective-permute-start.10 = (bf16[64,512]{1,0:T(8,128)(2,1)S(1)}, bf16[64,512]{1,0:T(8,128)(2,1)S(1)}, u32[]{:S(2)}, u32[]{:S(2)}) collective-permute-start(bf16[64,512]{1,0:T(8,128)(2,1)S(1)} %broadcast_select_fusion.4.refs_0_), channel_id=1, source_target_pairs={{0,4},{1,5},{2,6},{3,7},{4,0},{5,1},{6,2},{7,3},{8,12},{9,13},{10,... | collective-permute-start | bytes 196616 | tf_op jit(solution)/shard_map/ppermute | solution.py:35
  41.3 12.9 %copy-start.10 = (bf16[64,512]{1,0:T(8,128)(2,1)}, bf16[64,512]{1,0:T(8,128)(2,1)S(1)}, u32[]{:S(2)}) copy-start(bf16[64,512]{1,0:T(8,128)(2,1)S(1)} %collective-permute-done.refs_1_) | copy-start | bytes 196612
  41.3 10.4 %collective-permute-start.11 = (bf16[64,512]{1,0:T(8,128)(2,1)S(1)}, bf16[64,512]{1,0:T(8,128)(2,1)S(1)}, u32[]{:S(2)}, u32[]{:S(2)}) collective-permute-start(bf16[64,512]{1,0:T(8,128)(2,1)S(1)} %broadcast_select_fusion.4.refs_0_), channel_id=1, source_target_pairs={{0,6},{1,7},{2,0},{3,1},{4,2},{5,3},{6,4},{7,5},{8,14},{9,15},{10,... | collective-permute-start | bytes 196616 | tf_op jit(solution)/shard_map/ppermute | solution.py:35
  46.5 7.7 %copy-start.11 = (bf16[64,512]{1,0:T(8,128)(2,1)}, bf16[64,512]{1,0:T(8,128)(2,1)S(1)}, u32[]{:S(2)}) copy-start(bf16[64,512]{1,0:T(8,128)(2,1)S(1)} %collective-permute-done.1.refs_2_) | copy-start | bytes 196612
  46.5 7.7 %copy-start.12 = (bf16[64,512]{1,0:T(8,128)(2,1)}, bf16[64,512]{1,0:T(8,128)(2,1)S(1)}, u32[]{:S(2)}) copy-start(bf16[64,512]{1,0:T(8,128)(2,1)S(1)} %collective-permute-done.2.refs_3_) | copy-start | bytes 196612
  46.6 7.6 %collective-permute-start.3 = (bf16[256,512]{1,0:T(8,128)(2,1)S(1)}, bf16[256,512]{1,0:T(8,128)(2,1)S(1)}, u32[]{:S(2)}, u32[]{:S(2)}) collective-permute-start(bf16[256,512]{1,0:T(8,128)(2,1)S(1)} %pad_maximum_fusion), channel_id=1, source_target_pairs={{0,1},{1,0},{2,3},{3,2},{4,5},{5,4},{6,7},{7,6},{8,9},{9,8},{10,11... | collective-permute-start | bytes 786440 | tf_op jit(solution)/shard_map/ppermute | solution.py:35
  50.7 9.4 %copy-start.7 = (bf16[64,512]{1,0:T(8,128)(2,1)}, bf16[64,512]{1,0:T(8,128)(2,1)S(1)}, u32[]{:S(2)}) copy-start(bf16[64,512]{1,0:T(8,128)(2,1)S(1)} %collective-permute-done.9.refs_1_) | copy-start | bytes 196612
  50.7 9.4 %copy-start.8 = (bf16[64,512]{1,0:T(8,128)(2,1)}, bf16[64,512]{1,0:T(8,128)(2,1)S(1)}, u32[]{:S(2)}) copy-start(bf16[64,512]{1,0:T(8,128)(2,1)S(1)} %collective-permute-done.10.refs_2_) | copy-start | bytes 196612
  51.7 8.4 %copy-start.9 = (bf16[64,512]{1,0:T(8,128)(2,1)}, bf16[64,512]{1,0:T(8,128)(2,1)S(1)}, u32[]{:S(2)}) copy-start(bf16[64,512]{1,0:T(8,128)(2,1)S(1)} %collective-permute-done.11.refs_3_) | copy-start | bytes 196612
  51.7 11.5 %collective-permute-start.12 = (bf16[256,512]{1,0:T(8,128)(2,1)S(1)}, bf16[256,512]{1,0:T(8,128)(2,1)S(1)}, u32[]{:S(2)}, u32[]{:S(2)}) collective-permute-start(bf16[256,512]{1,0:T(8,128)(2,1)S(1)} %pad_maximum_fusion.1), channel_id=1, source_target_pairs={{0,1},{1,0},{2,3},{3,2},{4,5},{5,4},{6,7},{7,6},{8,9},{9,8},{10,11... | collective-permute-start | bytes 786440 | tf_op jit(solution)/shard_map/ppermute | solution.py:35
  54.2 0.7 copy-start.19
  60.1 10.9 %collective-permute-start.4 = (bf16[256,512]{1,0:T(8,128)(2,1)}, bf16[256,512]{1,0:T(8,128)(2,1)S(1)}, u32[]{:S(2)}, u32[]{:S(2)}) collective-permute-start(bf16[256,512]{1,0:T(8,128)(2,1)} %get-tuple-element.11), channel_id=1, source_target_pairs={{0,1},{1,0},{2,3},{3,2},{4,5},{5,4},{6,7},{7,6},{8,9},{9,8},{10,11... | collective-permute-start | bytes 786440 | tf_op jit(solution)/shard_map/ppermute | solution.py:35
  63.2 0.7 copy-start.22
  63.9 7.2 %copy-start.21 = (bf16[256,512]{1,0:T(8,128)(2,1)S(1)}, bf16[256,512]{1,0:T(8,128)(2,1)}, u32[]{:S(2)}) copy-start(bf16[256,512]{1,0:T(8,128)(2,1)} %get-tuple-element.10) | copy-start | bytes 786436
  69.1 3.6 %collective-permute-start.13 = (bf16[256,512]{1,0:T(8,128)(2,1)}, bf16[256,512]{1,0:T(8,128)(2,1)S(1)}, u32[]{:S(2)}, u32[]{:S(2)}) collective-permute-start(bf16[256,512]{1,0:T(8,128)(2,1)} %get-tuple-element.13), channel_id=1, source_target_pairs={{0,1},{1,0},{2,3},{3,2},{4,5},{5,4},{6,7},{7,6},{8,9},{9,8},{10,11... | collective-permute-start | bytes 786440 | tf_op jit(solution)/shard_map/ppermute | solution.py:35
  71.1 64.9 %copy-start.1 = (bf16[64,512]{1,0:T(8,128)(2,1)S(1)}, bf16[64,512]{1,0:T(8,128)(2,1)}, u32[]{:S(2)}) copy-start(bf16[64,512]{1,0:T(8,128)(2,1)} %copy-done) | copy-start | bytes 196612
  73.8 21.1 %collective-permute-start.16 = (bf16[64,512]{1,0:T(8,128)(2,1)S(1)}, bf16[64,512]{1,0:T(8,128)(2,1)S(1)}, u32[]{:S(2)}, u32[]{:S(2)}) collective-permute-start(bf16[64,512]{1,0:T(8,128)(2,1)S(1)} %get-tuple-element.46), channel_id=1, source_target_pairs={{0,6},{1,7},{2,0},{3,1},{4,2},{5,3},{6,4},{7,5},{8,14},{9,15},{10,... | collective-permute-start | bytes 196616 | tf_op jit(solution)/shard_map/ppermute | solution.py:35
  78.8 16.4 %collective-permute-start.15 = (bf16[64,512]{1,0:T(8,128)(2,1)S(1)}, bf16[64,512]{1,0:T(8,128)(2,1)S(1)}, u32[]{:S(2)}, u32[]{:S(2)}) collective-permute-start(bf16[64,512]{1,0:T(8,128)(2,1)S(1)} %get-tuple-element.47), channel_id=1, source_target_pairs={{0,4},{1,5},{2,6},{3,7},{4,0},{5,1},{6,2},{7,3},{8,12},{9,13},{10,... | collective-permute-start | bytes 196616 | tf_op jit(solution)/shard_map/ppermute | solution.py:35
  86.1 10.5 %collective-permute-start.14 = (bf16[64,512]{1,0:T(8,128)(2,1)S(1)}, bf16[64,512]{1,0:T(8,128)(2,1)S(1)}, u32[]{:S(2)}, u32[]{:S(2)}) collective-permute-start(bf16[64,512]{1,0:T(8,128)(2,1)S(1)} %get-tuple-element.45), channel_id=1, source_target_pairs={{0,2},{1,3},{2,4},{3,5},{4,6},{5,7},{6,0},{7,1},{8,10},{9,11},{10,... | collective-permute-start | bytes 196616 | tf_op jit(solution)/shard_map/ppermute | solution.py:35
  89.5 39.6 %collective-permute-start.7 = (bf16[64,512]{1,0:T(8,128)(2,1)S(1)}, bf16[64,512]{1,0:T(8,128)(2,1)S(1)}, u32[]{:S(2)}, u32[]{:S(2)}) collective-permute-start(bf16[64,512]{1,0:T(8,128)(2,1)S(1)} %get-tuple-element.43), channel_id=1, source_target_pairs={{0,6},{1,7},{2,0},{3,1},{4,2},{5,3},{6,4},{7,5},{8,14},{9,15},{10,... | collective-permute-start | bytes 196616 | tf_op jit(solution)/shard_map/ppermute | solution.py:35
  96.7 20.2 %collective-permute-start.27 = (bf16[64,512]{1,0:T(8,128)(2,1)S(1)}, bf16[64,512]{1,0:T(8,128)(2,1)S(1)}, u32[]{:S(2)}, u32[]{:S(2)}) collective-permute-start(bf16[64,512]{1,0:T(8,128)(2,1)S(1)} %fusion.11), channel_id=1, source_target_pairs={{0,8},{1,9},{2,10},{3,11},{4,12},{5,13},{6,14},{7,15},{8,16},{9,17... | collective-permute-start | bytes 196616 | tf_op jit(solution)/shard_map/ppermute | solution.py:35
  100.2 25.0 %collective-permute-start.28 = (bf16[64,512]{1,0:T(8,128)(2,1)S(1)}, bf16[64,512]{1,0:T(8,128)(2,1)S(1)}, u32[]{:S(2)}, u32[]{:S(2)}) collective-permute-start(bf16[64,512]{1,0:T(8,128)(2,1)S(1)} %fusion.11), channel_id=1, source_target_pairs={{0,10},{1,11},{2,12},{3,13},{4,14},{5,15},{6,8},{7,9},{8,18},{9,19... | collective-permute-start | bytes 196616 | tf_op jit(solution)/shard_map/ppermute | solution.py:35
  104.3 22.9 %collective-permute-start.29 = (bf16[64,512]{1,0:T(8,128)(2,1)S(1)}, bf16[64,512]{1,0:T(8,128)(2,1)S(1)}, u32[]{:S(2)}, u32[]{:S(2)}) collective-permute-start(bf16[64,512]{1,0:T(8,128)(2,1)S(1)} %fusion.11), channel_id=1, source_target_pairs={{0,12},{1,13},{2,14},{3,15},{4,8},{5,9},{6,10},{7,11},{8,20},{9,21... | collective-permute-start | bytes 196616 | tf_op jit(solution)/shard_map/ppermute | solution.py:35
  112.7 14.5 %collective-permute-start.30 = (bf16[64,512]{1,0:T(8,128)(2,1)S(1)}, bf16[64,512]{1,0:T(8,128)(2,1)S(1)}, u32[]{:S(2)}, u32[]{:S(2)}) collective-permute-start(bf16[64,512]{1,0:T(8,128)(2,1)S(1)} %fusion.11), channel_id=1, source_target_pairs={{0,14},{1,15},{2,8},{3,9},{4,10},{5,11},{6,12},{7,13},{8,22},{9,23... | collective-permute-start | bytes 196616 | tf_op jit(solution)/shard_map/ppermute | solution.py:35
  116.8 42.8 %copy-start.2 = (bf16[64,512]{1,0:T(8,128)(2,1)}, bf16[64,512]{1,0:T(8,128)(2,1)S(1)}, u32[]{:S(2)}) copy-start(bf16[64,512]{1,0:T(8,128)(2,1)S(1)} %collective-permute-done.27.refs_0_) | copy-start | bytes 196612
  116.8 14.2 %collective-permute-start.6 = (bf16[64,512]{1,0:T(8,128)(2,1)S(1)}, bf16[64,512]{1,0:T(8,128)(2,1)S(1)}, u32[]{:S(2)}, u32[]{:S(2)}) collective-permute-start(bf16[64,512]{1,0:T(8,128)(2,1)S(1)} %get-tuple-element.44), channel_id=1, source_target_pairs={{0,4},{1,5},{2,6},{3,7},{4,0},{5,1},{6,2},{7,3},{8,12},{9,13},{10,... | collective-permute-start | bytes 196616 | tf_op jit(solution)/shard_map/ppermute | solution.py:35
  125.2 34.5 %copy-start.13 = (bf16[64,512]{1,0:T(8,128)(2,1)}, bf16[64,512]{1,0:T(8,128)(2,1)S(1)}, u32[]{:S(2)}) copy-start(bf16[64,512]{1,0:T(8,128)(2,1)S(1)} %collective-permute-done.28.refs_1_) | copy-start | bytes 196612
  125.2 10.8 %collective-permute-start.5 = (bf16[64,512]{1,0:T(8,128)(2,1)S(1)}, bf16[64,512]{1,0:T(8,128)(2,1)S(1)}, u32[]{:S(2)}, u32[]{:S(2)}) collective-permute-start(bf16[64,512]{1,0:T(8,128)(2,1)S(1)} %get-tuple-element.42), channel_id=1, source_target_pairs={{0,2},{1,3},{2,4},{3,5},{4,6},{5,7},{6,0},{7,1},{8,10},{9,11},{10,... | collective-permute-start | bytes 196616 | tf_op jit(solution)/shard_map/ppermute | solution.py:35
  127.2 32.5 %copy-start.14 = (bf16[64,512]{1,0:T(8,128)(2,1)}, bf16[64,512]{1,0:T(8,128)(2,1)S(1)}, u32[]{:S(2)}) copy-start(bf16[64,512]{1,0:T(8,128)(2,1)S(1)} %collective-permute-done.29.refs_2_) | copy-start | bytes 196612
  127.2 32.5 %copy-start.15 = (bf16[64,512]{1,0:T(8,128)(2,1)}, bf16[64,512]{1,0:T(8,128)(2,1)S(1)}, u32[]{:S(2)}) copy-start(bf16[64,512]{1,0:T(8,128)(2,1)S(1)} %collective-permute-done.30.refs_3_) | copy-start | bytes 196612
  127.2 32.4 %collective-permute-start.31 = (bf16[256,512]{1,0:T(8,128)(2,1)S(1)}, bf16[256,512]{1,0:T(8,128)(2,1)S(1)}, u32[]{:S(2)}, u32[]{:S(2)}) collective-permute-start(bf16[256,512]{1,0:T(8,128)(2,1)S(1)} %pad_maximum_fusion.3), channel_id=1, source_target_pairs={{0,1},{1,0},{2,3},{3,2},{4,5},{5,4},{6,7},{7,6},{8,9},{9,8},{10,11... | collective-permute-start | bytes 786440 | tf_op jit(solution)/shard_map/ppermute | solution.py:35
  136.1 15.1 %collective-permute-start.18 = (bf16[64,512]{1,0:T(8,128)(2,1)S(1)}, bf16[64,512]{1,0:T(8,128)(2,1)S(1)}, u32[]{:S(2)}, u32[]{:S(2)}) collective-permute-start(bf16[64,512]{1,0:T(8,128)(2,1)S(1)} %get-tuple-element.23), channel_id=1, source_target_pairs={{0,8},{1,9},{2,10},{3,11},{4,12},{5,13},{6,14},{7,15},{8,16},{9,17... | collective-permute-start | bytes 196616 | tf_op jit(solution)/shard_map/ppermute | solution.py:35
  138.7 12.5 %collective-permute-start.19 = (bf16[64,512]{1,0:T(8,128)(2,1)S(1)}, bf16[64,512]{1,0:T(8,128)(2,1)S(1)}, u32[]{:S(2)}, u32[]{:S(2)}) collective-permute-start(bf16[64,512]{1,0:T(8,128)(2,1)S(1)} %get-tuple-element.23), channel_id=1, source_target_pairs={{0,10},{1,11},{2,12},{3,13},{4,14},{5,15},{6,8},{7,9},{8,18},{9,19... | collective-permute-start | bytes 196616 | tf_op jit(solution)/shard_map/ppermute | solution.py:35
  141.3 13.6 %collective-permute-start.20 = (bf16[64,512]{1,0:T(8,128)(2,1)S(1)}, bf16[64,512]{1,0:T(8,128)(2,1)S(1)}, u32[]{:S(2)}, u32[]{:S(2)}) collective-permute-start(bf16[64,512]{1,0:T(8,128)(2,1)S(1)} %get-tuple-element.23), channel_id=1, source_target_pairs={{0,12},{1,13},{2,14},{3,15},{4,8},{5,9},{6,10},{7,11},{8,20},{9,21... | collective-permute-start | bytes 196616 | tf_op jit(solution)/shard_map/ppermute | solution.py:35
  147.0 10.7 %collective-permute-start.21 = (bf16[64,512]{1,0:T(8,128)(2,1)S(1)}, bf16[64,512]{1,0:T(8,128)(2,1)S(1)}, u32[]{:S(2)}, u32[]{:S(2)}) collective-permute-start(bf16[64,512]{1,0:T(8,128)(2,1)S(1)} %get-tuple-element.23), channel_id=1, source_target_pairs={{0,14},{1,15},{2,8},{3,9},{4,10},{5,11},{6,12},{7,13},{8,22},{9,23... | collective-permute-start | bytes 196616 | tf_op jit(solution)/shard_map/ppermute | solution.py:35
  151.1 14.4 %copy-start.4 = (bf16[64,512]{1,0:T(8,128)(2,1)}, bf16[64,512]{1,0:T(8,128)(2,1)S(1)}, u32[]{:S(2)}) copy-start(bf16[64,512]{1,0:T(8,128)(2,1)S(1)} %collective-permute-done.18.refs_0_) | copy-start | bytes 196612
  151.2 14.4 %copy-start.16 = (bf16[64,512]{1,0:T(8,128)(2,1)}, bf16[64,512]{1,0:T(8,128)(2,1)S(1)}, u32[]{:S(2)}) copy-start(bf16[64,512]{1,0:T(8,128)(2,1)S(1)} %collective-permute-done.19.refs_1_) | copy-start | bytes 196612
  154.9 10.7 %copy-start.17 = (bf16[64,512]{1,0:T(8,128)(2,1)}, bf16[64,512]{1,0:T(8,128)(2,1)S(1)}, u32[]{:S(2)}) copy-start(bf16[64,512]{1,0:T(8,128)(2,1)S(1)} %collective-permute-done.20.refs_2_) | copy-start | bytes 196612
  157.7 7.9 %copy-start.18 = (bf16[64,512]{1,0:T(8,128)(2,1)}, bf16[64,512]{1,0:T(8,128)(2,1)S(1)}, u32[]{:S(2)}) copy-start(bf16[64,512]{1,0:T(8,128)(2,1)S(1)} %collective-permute-done.21.refs_3_) | copy-start | bytes 196612
  157.7 13.9 %collective-permute-start.22 = (bf16[256,512]{1,0:T(8,128)(2,1)S(1)}, bf16[256,512]{1,0:T(8,128)(2,1)S(1)}, u32[]{:S(2)}, u32[]{:S(2)}) collective-permute-start(bf16[256,512]{1,0:T(8,128)(2,1)S(1)} %pad_maximum_fusion.2), channel_id=1, source_target_pairs={{0,1},{1,0},{2,3},{3,2},{4,5},{5,4},{6,7},{7,6},{8,9},{9,8},{10,11... | collective-permute-start | bytes 786440 | tf_op jit(solution)/shard_map/ppermute | solution.py:35
  159.7 0.7 copy-start.20
  165.6 14.0 %collective-permute-start.32 = (bf16[256,512]{1,0:T(8,128)(2,1)}, bf16[256,512]{1,0:T(8,128)(2,1)S(1)}, u32[]{:S(2)}, u32[]{:S(2)}) collective-permute-start(bf16[256,512]{1,0:T(8,128)(2,1)} %get-tuple-element.17), channel_id=1, source_target_pairs={{0,1},{1,0},{2,3},{3,2},{4,5},{5,4},{6,7},{7,6},{8,9},{9,8},{10,11... | collective-permute-start | bytes 786440 | tf_op jit(solution)/shard_map/ppermute | solution.py:35
  168.0 52.2 %collective-permute-start.17 = (bf16[64,512]{1,0:T(8,128)(2,1)S(1)}, bf16[64,512]{1,0:T(8,128)(2,1)S(1)}, u32[]{:S(2)}, u32[]{:S(2)}) collective-permute-start(bf16[64,512]{1,0:T(8,128)(2,1)S(1)} %fusion.11), channel_id=1, source_target_pairs={{0,64},{64,128},{128,192},{192,256},{256,320},{320,384},{384,448},... | collective-permute-start | bytes 196616 | tf_op jit(solution)/shard_map/ppermute | solution.py:40
  171.6 0.7 copy-start.24
  172.3 7.3 %copy-start.23 = (bf16[256,512]{1,0:T(8,128)(2,1)S(1)}, bf16[256,512]{1,0:T(8,128)(2,1)}, u32[]{:S(2)}) copy-start(bf16[256,512]{1,0:T(8,128)(2,1)} %get-tuple-element.16) | copy-start | bytes 786436
  177.6 32.0 %copy-start.3 = (bf16[64,512]{1,0:T(8,128)(2,1)S(1)}, bf16[64,512]{1,0:T(8,128)(2,1)}, u32[]{:S(2)}) copy-start(bf16[64,512]{1,0:T(8,128)(2,1)} %copy-done.2) | copy-start | bytes 196612
  177.6 42.6 %copy-start.5 = (bf16[64,512]{1,0:T(8,128)(2,1)S(1)}, bf16[64,512]{1,0:T(8,128)(2,1)}, u32[]{:S(2)}) copy-start(bf16[64,512]{1,0:T(8,128)(2,1)} %copy-done.4) | copy-start | bytes 196612
  177.6 19.0 %collective-permute-start.23 = (bf16[256,512]{1,0:T(8,128)(2,1)}, bf16[256,512]{1,0:T(8,128)(2,1)S(1)}, u32[]{:S(2)}, u32[]{:S(2)}) collective-permute-start(bf16[256,512]{1,0:T(8,128)(2,1)} %get-tuple-element.15), channel_id=1, source_target_pairs={{0,1},{1,0},{2,3},{3,2},{4,5},{5,4},{6,7},{7,6},{8,9},{9,8},{10,11... | collective-permute-start | bytes 786440 | tf_op jit(solution)/shard_map/ppermute | solution.py:35
  179.8 21.7 %collective-permute-start.35 = (bf16[64,512]{1,0:T(8,128)(2,1)S(1)}, bf16[64,512]{1,0:T(8,128)(2,1)S(1)}, u32[]{:S(2)}, u32[]{:S(2)}) collective-permute-start(bf16[64,512]{1,0:T(8,128)(2,1)S(1)} %get-tuple-element.40), channel_id=1, source_target_pairs={{0,6},{1,7},{2,0},{3,1},{4,2},{5,3},{6,4},{7,5},{8,14},{9,15},{10,... | collective-permute-start | bytes 196616 | tf_op jit(solution)/shard_map/ppermute | solution.py:35
  184.2 22.4 %collective-permute-start.34 = (bf16[64,512]{1,0:T(8,128)(2,1)S(1)}, bf16[64,512]{1,0:T(8,128)(2,1)S(1)}, u32[]{:S(2)}, u32[]{:S(2)}) collective-permute-start(bf16[64,512]{1,0:T(8,128)(2,1)S(1)} %get-tuple-element.41), channel_id=1, source_target_pairs={{0,4},{1,5},{2,6},{3,7},{4,0},{5,1},{6,2},{7,3},{8,12},{9,13},{10,... | collective-permute-start | bytes 196616 | tf_op jit(solution)/shard_map/ppermute | solution.py:35
  191.5 18.1 %collective-permute-start.33 = (bf16[64,512]{1,0:T(8,128)(2,1)S(1)}, bf16[64,512]{1,0:T(8,128)(2,1)S(1)}, u32[]{:S(2)}, u32[]{:S(2)}) collective-permute-start(bf16[64,512]{1,0:T(8,128)(2,1)S(1)} %get-tuple-element.39), channel_id=1, source_target_pairs={{0,2},{1,3},{2,4},{3,5},{4,6},{5,7},{6,0},{7,1},{8,10},{9,11},{10,... | collective-permute-start | bytes 196616 | tf_op jit(solution)/shard_map/ppermute | solution.py:35
  197.7 16.3 %collective-permute-start.26 = (bf16[64,512]{1,0:T(8,128)(2,1)S(1)}, bf16[64,512]{1,0:T(8,128)(2,1)S(1)}, u32[]{:S(2)}, u32[]{:S(2)}) collective-permute-start(bf16[64,512]{1,0:T(8,128)(2,1)S(1)} %get-tuple-element.37), channel_id=1, source_target_pairs={{0,6},{1,7},{2,0},{3,1},{4,2},{5,3},{6,4},{7,5},{8,14},{9,15},{10,... | collective-permute-start | bytes 196616 | tf_op jit(solution)/shard_map/ppermute | solution.py:35
  201.5 14.1 %collective-permute-start.25 = (bf16[64,512]{1,0:T(8,128)(2,1)S(1)}, bf16[64,512]{1,0:T(8,128)(2,1)S(1)}, u32[]{:S(2)}, u32[]{:S(2)}) collective-permute-start(bf16[64,512]{1,0:T(8,128)(2,1)S(1)} %get-tuple-element.38), channel_id=1, source_target_pairs={{0,4},{1,5},{2,6},{3,7},{4,0},{5,1},{6,2},{7,3},{8,12},{9,13},{10,... | collective-permute-start | bytes 196616 | tf_op jit(solution)/shard_map/ppermute | solution.py:35
  206.6 13.5 %collective-permute-start.24 = (bf16[64,512]{1,0:T(8,128)(2,1)S(1)}, bf16[64,512]{1,0:T(8,128)(2,1)S(1)}, u32[]{:S(2)}, u32[]{:S(2)}) collective-permute-start(bf16[64,512]{1,0:T(8,128)(2,1)S(1)} %get-tuple-element.36), channel_id=1, source_target_pairs={{0,2},{1,3},{2,4},{3,5},{4,6},{5,7},{6,0},{7,1},{8,10},{9,11},{10,... | collective-permute-start | bytes 196616 | tf_op jit(solution)/shard_map/ppermute | solution.py:35
  209.7 10.6 %collective-permute-start.36 = (bf16[64,512]{1,0:T(8,128)(2,1)S(1)}, bf16[64,512]{1,0:T(8,128)(2,1)S(1)}, u32[]{:S(2)}, u32[]{:S(2)}) collective-permute-start(bf16[64,512]{1,0:T(8,128)(2,1)S(1)} %fusion.3), channel_id=1, source_target_pairs={{0,64},{64,128},{128,192},{192,256},{256,320},{320,384},{384,448},... | collective-permute-start | bytes 196616 | tf_op jit(solution)/shard_map/ppermute | solution.py:40

commit v2 on v1

v2 whole, which is shorter than its diff:
```python
import jax
import jax.numpy as jnp
from jax import lax
from jax.experimental import pallas as pl
from jax.experimental.pallas import tpu as pltpu
from jax.sharding import PartitionSpec as P

HD = 128
SECT = 8
SPAN = 256
EPS = 1e-05
CORES = 2


def chip_route(size, turn, step, sections_on):
    per_section = size // SECT
    chips = per_section // CORES
    route = []
    for source in range(size):
        section, group = divmod(source, per_section)
        chip, core = divmod(group, CORES)
        if section + sections_on >= SECT:
            continue
        ahead = step if core == 0 else -step
        target = (section + sections_on) * per_section + (chip + ahead) % chips * CORES + (core ^ turn)
        route.append((source, target))
    return route


def along_chips(block, step, sections_on=0):
    return lax.ppermute(block, "segment", chip_route(lax.axis_size("segment"), 0, step, sections_on))


def swap_cores(block):
    return lax.ppermute(block, "segment", chip_route(lax.axis_size("segment"), 1, 0, 0))


def edge_from_previous(block):
    spans, groups = lax.axis_size("seq"), lax.axis_size("segment")
    route = [
        (s * groups + g, (s + 1) * groups + g) for s in range(spans - 1) for g in range(groups) if g % CORES == 1
    ]
    return lax.ppermute(block, ("seq", "segment"), route)


def attend(queries, keys, values):
    scores = lax.dot_general(
        queries, keys, (((1,), (1,)), ((), ())), preferred_element_type=jnp.float32
    ) * HD ** (-0.5)
    exponent = jnp.exp(scores)
    weights = (exponent / jnp.sum(exponent, axis=-1, keepdims=True)).astype(jnp.bfloat16)
    return jnp.dot(weights, values, preferred_element_type=jnp.float32)


def layer_kernel(
    where_ref, own_ref, front_ref, back_ref, far_ref, wq0_ref, wq1_ref, main_ref, kv_ref, other_kv_ref, wo0_ref, wo1_ref,
    t_own_ref, t_front_ref, t_back_ref, t_far_ref,
):
    chip = where_ref[0]
    core = where_ref[1]
    chips = 4
    ahead = 1 - 2 * core
    rows, width = own_ref.shape
    total = jnp.zeros((rows, 1), jnp.float32)
    queries = [jnp.zeros((rows, wq0_ref.shape[1]), jnp.float32) for _ in range(CORES)]
    sources = (chip, chip - ahead, chip + ahead, chip + 2)
    for source, ref in zip(sources, (own_ref, front_ref, back_ref, far_ref)):
        part = ref[...]
        wide = part.astype(jnp.float32)
        total += jnp.sum(wide * wide, axis=-1, keepdims=True)
        offset = pl.multiple_of(lax.rem(source + chips, chips) * width, width)
        for i, wq_ref in enumerate((wq0_ref, wq1_ref)):
            queries[i] += jnp.dot(part, wq_ref[pl.ds(offset, width), :], preferred_element_type=jnp.float32)
    scale = lax.rsqrt(total / (chips * width) + EPS)
    last_row = lax.broadcasted_iota(jnp.int32, (16, HD), 0) == 15
    attended = []
    for i in range(CORES):
        q = (queries[i] * scale).astype(jnp.bfloat16)
        heads = []
        for h in range(q.shape[1] // HD):
            cols = slice(h * HD, (h + 1) * HD)
            main = attend(q[:, cols], main_ref[i, 0, :, cols], main_ref[i, 1, :, cols])
            if i == 0:
                keys, values = kv_ref[0, SPAN:, cols], kv_ref[1, SPAN:, cols]
            else:
                keys, values = other_kv_ref[0, :, cols], other_kv_ref[1, :, cols]
            end = attend(q[rows - 16 :, cols], keys, values)
            end = jnp.where(last_row & (core > 0), end, main[rows - 16 :])
            heads.append(jnp.concatenate([main[: rows - 16], end], axis=0))
        attended.append(jnp.concatenate(heads, axis=1).astype(jnp.bfloat16))
    targets = (chip + 2, chip - ahead, chip + ahead, chip)
    for target, ref in zip(targets, (t_far_ref, t_back_ref, t_front_ref, t_own_ref)):
        offset = pl.multiple_of(lax.rem(target + chips, chips) * width, width)
        term = jnp.dot(attended[0], wo0_ref[:, pl.ds(offset, width)], preferred_element_type=jnp.float32)
        term += jnp.dot(attended[1], wo1_ref[:, pl.ds(offset, width)], preferred_element_type=jnp.float32)
        ref[...] = term.astype(ref.dtype)


def layer(where, blocks, *operands):
    shape = blocks[0].shape
    vmem = pl.BlockSpec(memory_space=pltpu.VMEM)
    return pl.pallas_call(
        layer_kernel,
        in_specs=[pl.BlockSpec(memory_space=pltpu.SMEM)] + [vmem] * (len(blocks) + len(operands)),
        out_specs=(vmem,) * 4,
        out_shape=(jax.ShapeDtypeStruct(shape, jnp.float32),) + (jax.ShapeDtypeStruct(shape, jnp.bfloat16),) * 3,
        cost_estimate=pl.CostEstimate(flops=600_000_000, bytes_accessed=20_000_000, transcendentals=80_000),
        compiler_params=pltpu.CompilerParams(vmem_limit_bytes=24 << 20),
        name="layer",
    )(where, *blocks, *operands)


def per_device(stream, w_query, w_out, neighbour_kv):
    per_section = lax.axis_size("segment") // SECT
    group = lax.axis_index("segment") % per_section
    core = group % CORES
    first_core = core == 0
    where = jnp.stack([group // CORES, core]).astype(jnp.int32)
    half = stream.shape[0] // 2
    width = stream.shape[1]
    end = lax.broadcasted_iota(jnp.int32, (half, width), 0) == half - 1

    def trade_ends(top, low):
        return jnp.where(end, low[half - 1 :], top), jnp.where(end, top[half - 1 :], low)

    def by_core(here, there):
        return jnp.where(first_core, jnp.concatenate([here, there], axis=1), jnp.concatenate([there, here], axis=1))

    top, low = trade_ends(stream[:half], stream[half:])
    own = by_core(jnp.where(first_core, low, top), swap_cores(jnp.where(first_core, top, low)))

    near, far = neighbour_kv[:, :, :SPAN], neighbour_kv[:, :, SPAN:]
    other_kv = swap_cores(jnp.where(first_core, far, near))
    wq_other = swap_cores(w_query)
    wo_other = swap_cores(w_out)
    mains = []
    for tick in range(2):
        edge = edge_from_previous(jnp.stack([far[tick], other_kv[tick]]))
        mains.append(jnp.where(first_core, jnp.stack([near[tick], other_kv[tick]]), edge))

    outputs = []
    for tick in range(2):
        if tick == 0:
            front, back = along_chips(own, 1), along_chips(own, -1)
        else:
            front, back, own = along_chips(own, 1, 1), along_chips(own, -1, 1), along_chips(own, 0, 1)
        blocks = (own, front, back, along_chips(front, 1))
        t_own, t_front, t_back, t_far = layer(
            where, blocks, w_query, wq_other, mains[tick], neighbour_kv[tick], other_kv[tick], w_out, wo_other
        )
        passed = along_chips(t_far, 1)
        from_back = along_chips(t_back, -1)
        t_front = (t_front.astype(jnp.float32) + passed.astype(jnp.float32)).astype(jnp.bfloat16)
        from_front = along_chips(t_front, 1)
        result = own.astype(jnp.float32) + t_own + from_back.astype(jnp.float32) + from_front.astype(jnp.float32)
        own = result.astype(jnp.bfloat16)
        kept = jnp.where(first_core, own[:, :width], own[:, width:])
        moved = swap_cores(jnp.where(first_core, own[:, width:], own[:, :width]))
        out_top, out_low = trade_ends(jnp.where(first_core, moved, kept), jnp.where(first_core, kept, moved))
        outputs.append(jnp.concatenate([out_top, out_low], axis=0))
    return tuple(outputs)


def solution(mesh):
    placed = (
        P("seq", "segment"),
        P(None, "segment"),
        P("segment", None),
        P(None, None, "seq", "segment"),
    )
    return jax.shard_map(
        per_device,
        mesh=mesh,
        in_specs=placed,
        out_specs=(P("seq", "segment"), P("seq", "segment")),
        check_vma=False,
    )
```

time: 222 us -> 149 us (0.67)
  the two profiles are of different devices: /device:TPU:8 before, /device:TPU:73 now
where the time goes in v2:
time: 149 us; the launch traced here: 148 us
  starting transfers between devices  91.7 us (62%)
  waiting for transfers between devices  31.9 us (21%)
  Pallas kernels  11.9 us (8%)
  other arithmetic  5.82 us (4%)
  local copies, waits for them, and re-layouts  5.29 us (4%)
    ppermute x13, starting transfers between devices, along_chips(): lax.ppermute(block, 'segment', chip_route(lax.axis_size('segment'), 0, st...  69.2 us
    ppermute x13, waiting for transfers between devices, along_chips(): lax.ppermute(block, 'segment', chip_route(lax.axis_size('segment'), 0, st...  31 us
    ppermute x6, starting transfers between devices, swap_cores(): lax.ppermute(block, 'segment', chip_route(lax.axis_size('segment'), 1, 0,...  16.5 us
    pallas_call x2, Pallas kernels, layer(): pl.pallas_call(layer_kernel, in_specs=[pl.BlockSpec(memory_space=pltpu.SM...  11.9 us
    ppermute x2, starting transfers between devices, edge_from_previous(): return lax.ppermute(block, ('seq', 'segment'), route)  6.04 us
  transfers between devices with their start and end apart: 21, of which 8 were waited for; matrix products, arithmetic and copies ran while one was open for 5% of the time, Pallas kernels for 0%

profile of v2, /device:TPU:73, one launch (start us, length us, event | category | flops | bytes accessed | tf_op | source)
XLA Modules:
  0.0 147.7 jit_solution(12560643440509304462)
XLA Ops:
  0.6 0.0 copy-start.4
  0.6 2.7 %collective-permute-start.4 = (bf16[4096,256]{1,0:T(8,128)(2,1)}, bf16[4096,256]{1,0:T(8,128)(2,1)}, u32[]{:S(2)}, u32[]{:S(2)}) collective-permute-start(bf16[4096,256]{1,0:T(8,128)(2,1)} %wq0_ref.3), channel_id=1, source_target_pairs={{0,1},{1,0},{2,3},{3,2},{4,5},{5,4},{6,7},{7,6},{8,9},{9,8},{10,11... | collective-permute-start | bytes 6291464 | tf_op jit(solution)/shard_map/ppermute | solution.py:35
  3.4 1.9 %collective-permute-start.7 = (bf16[256,4096]{1,0:T(8,128)(2,1)}, bf16[256,4096]{1,0:T(8,128)(2,1)}, u32[]{:S(2)}, u32[]{:S(2)}) collective-permute-start(bf16[256,4096]{1,0:T(8,128)(2,1)} %wo0_ref.3), channel_id=1, source_target_pairs={{0,1},{1,0},{2,3},{3,2},{4,5},{5,4},{6,7},{7,6},{8,9},{9,8},{10,11... | collective-permute-start | bytes 6291464 | tf_op jit(solution)/shard_map/ppermute | solution.py:35
  5.3 1.3 slice_select_fusion
  6.6 2.4 %collective-permute-start.5 = (bf16[2,2,256,256]{3,2,1,0:T(8,128)(2,1)S(1)}, bf16[2,2,256,256]{3,2,1,0:T(8,128)(2,1)S(1)}, u32[]{:S(2)}, u32[]{:S(2)}) collective-permute-start(bf16[2,2,256,256]{3,2,1,0:T(8,128)(2,1)S(1)} %slice_select_fusion), channel_id=1, source_target_pairs={{0,1},{1,0},{2,3},{3,2},{4,5},{5,4},{6,7},{7,6},{8,9},{9,8},{10,11... | collective-permute-start | bytes 1572872 | tf_op jit(solution)/shard_map/ppermute | solution.py:35
  9.0 0.7 slice_reduce_fusion.4
  9.8 1.0 broadcast_select_fusion.13
  10.7 0.0 copy-start.5
  10.7 2.1 %collective-permute-start = (bf16[64,512]{1,0:T(8,128)(2,1)S(1)}, bf16[64,512]{1,0:T(8,128)(2,1)S(1)}, u32[]{:S(2)}, u32[]{:S(2)}) collective-permute-start(bf16[64,512]{1,0:T(8,128)(2,1)S(1)} %get-tuple-element.35), channel_id=1, source_target_pairs={{0,1},{1,0},{2,3},{3,2},{4,5},{5,4},{6,7},{7,6},{8,9},{9,8},{10,11... | collective-permute-start | bytes 196616 | tf_op jit(solution)/shard_map/ppermute | solution.py:35
  12.8 0.9 fusion.2
  13.8 0.0 collective-permute-done.5
  13.8 0.9 slice_bitcast_fusion.2
  14.6 0.9 pad_maximum_fusion
  15.5 4.1 %collective-permute-start.6 = (bf16[2,2,256,256]{3,2,1,0:T(8,128)(2,1)}, bf16[2,2,256,256]{3,2,1,0:T(8,128)(2,1)}, u32[]{:S(2)}, u32[]{:S(2)}) collective-permute-start(bf16[2,2,256,256]{3,2,1,0:T(8,128)(2,1)} %pad_maximum_fusion), channel_id=1, source_target_pairs={{1,65},{3,67},{5,69},{7,71},{9,73},{11,75},{13,77},{15,79},{17,81}... | collective-permute-start | bytes 1572872 | tf_op jit(solution)/shard_map/ppermute | solution.py:43
  19.7 0.0 collective-permute-done
  19.7 12.5 %collective-permute-start.1 = (bf16[64,1024]{1,0:T(8,128)(2,1)S(1)}, bf16[64,1024]{1,0:T(8,128)(2,1)}, u32[]{:S(2)}, u32[]{:S(2)}) collective-permute-start(bf16[64,1024]{1,0:T(8,128)(2,1)S(1)} %maximum_select_fusion.own_ref), channel_id=1, source_target_pairs={{0,2},{1,7},{2,4},{3,1},{4,6},{5,3},{6,0},{7,5},{8,10},{9,15},{10,... | collective-permute-start | bytes 393224 | tf_op jit(solution)/shard_map/ppermute | solution.py:31
  32.2 0.1 slice_bitcast_fusion
  32.3 0.1 pad_add_fusion.where_ref
  32.4 1.9 %collective-permute-start.2 = (bf16[64,1024]{1,0:T(8,128)(2,1)S(1)}, bf16[64,1024]{1,0:T(8,128)(2,1)S(1)}, u32[]{:S(2)}, u32[]{:S(2)}) collective-permute-start(bf16[64,1024]{1,0:T(8,128)(2,1)S(1)} %maximum_select_fusion.own_ref), channel_id=1, source_target_pairs={{0,6},{1,3},{2,0},{3,5},{4,2},{5,7},{6,4},{7,1},{8,14},{9,11},{10,... | collective-permute-start | bytes 393224 | tf_op jit(solution)/shard_map/ppermute | solution.py:31
  34.3 7.4 %collective-permute-done.1.front_ref = bf16[64,1024]{1,0:T(8,128)(2,1)} collective-permute-done((bf16[64,1024]{1,0:T(8,128)(2,1)S(1)}, bf16[64,1024]{1,0:T(8,128)(2,1)}, u32[]{:S(2)}, u32[]{:S(2)}) %collective-permute-start.1) | collective-permute-done | bytes 131104 | tf_op jit(solution)/shard_map/ppermute | solution.py:31
  41.7 4.6 %collective-permute-start.3 = (bf16[64,1024]{1,0:T(8,128)(2,1)}, bf16[64,1024]{1,0:T(8,128)(2,1)S(1)}, u32[]{:S(2)}, u32[]{:S(2)}) collective-permute-start(bf16[64,1024]{1,0:T(8,128)(2,1)} %collective-permute-done.1.front_ref), channel_id=1, source_target_pairs={{0,2},{1,7},{2,4},{3,1},{4,6},{5,3},{6,0},{7,5},{8,10},{9,15},{10,... | collective-permute-start | bytes 393224 | tf_op jit(solution)/shard_map/ppermute | solution.py:31
  46.2 0.0 collective-permute-done.6
  46.3 1.3 fusion.1.main_ref
  47.5 0.0 collective-permute-done.2.back_ref
  47.5 5.1 %collective-permute-done.3.far_ref = bf16[64,1024]{1,0:T(8,128)(2,1)S(1)} collective-permute-done((bf16[64,1024]{1,0:T(8,128)(2,1)}, bf16[64,1024]{1,0:T(8,128)(2,1)S(1)}, u32[]{:S(2)}, u32[]{:S(2)}) %collective-permute-start.3) | collective-permute-done | bytes 131104 | tf_op jit(solution)/shard_map/ppermute | solution.py:31
  52.6 0.0 collective-permute-done.4.wq1_ref
  52.7 0.0 collective-permute-done.7.wo1_ref
  52.7 0.0 copy-start.1
  52.7 1.6 %copy-done.1 = bf16[256,4096]{1,0:T(8,128)(2,1)S(1)} copy-done((bf16[256,4096]{1,0:T(8,128)(2,1)S(1)}, bf16[256,4096]{1,0:T(8,128)(2,1)}, u32[]{:S(2)}) %copy-start.1) | copy-done | bytes 2097176
  54.3 0.9 copy-done.3
  55.2 6.0 %layer.2 = (f32[64,1024]{1,0:T(8,128)S(1)}, bf16[64,1024]{1,0:T(8,128)(2,1)S(1)}, bf16[64,1024]{1,0:T(8,128)(2,1)S(1)}, bf16[64,1024]{1,0:T(8,128)(2,1)S(1)}) custom-call(s32[2]{0:T(128)S(1)} %pad_add_fusion.where_ref, bf16[64,1024]{1,0:T(8,128)(2,1)S(1)} %maximum_select_fusion.own_ref, bf16[64,1024]{1,0:T(8,128)(2,1)} %collective-permute-done.1.front_ref, ...), custom_call_target="tpu_custom_call" | custom-call | flops 600000000 | bytes 20000000 | tf_op jit(solution)/shard_map/layer/pallas_call | solution.py:102
  61.2 0.0 copy-start.2
  61.2 4.8 %collective-permute-start.9 = (bf16[64,1024]{1,0:T(8,128)(2,1)S(1)}, bf16[64,1024]{1,0:T(8,128)(2,1)S(1)}, u32[]{:S(2)}, u32[]{:S(2)}) collective-permute-start(bf16[64,1024]{1,0:T(8,128)(2,1)S(1)} %get-tuple-element.13), channel_id=1, source_target_pairs={{0,2},{1,7},{2,4},{3,1},{4,6},{5,3},{6,0},{7,5},{8,10},{9,15},{10,... | collective-permute-start | bytes 393224 | tf_op jit(solution)/shard_map/ppermute | solution.py:31
  66.1 0.1 pad_maximum_fusion.2
  66.1 1.9 %collective-permute-start.16 = (bf16[2,2,256,256]{3,2,1,0:T(8,128)(2,1)S(1)}, bf16[2,2,256,256]{3,2,1,0:T(8,128)(2,1)S(1)}, u32[]{:S(2)}, u32[]{:S(2)}) collective-permute-start(bf16[2,2,256,256]{3,2,1,0:T(8,128)(2,1)S(1)} %pad_maximum_fusion.2), channel_id=1, source_target_pairs={{1,65},{3,67},{5,69},{7,71},{9,73},{11,75},{13,77},{15,79},{17,81}... | collective-permute-start | bytes 1572872 | tf_op jit(solution)/shard_map/ppermute | solution.py:43
  68.1 3.9 %collective-permute-start.8 = (bf16[64,1024]{1,0:T(8,128)(2,1)S(1)}, bf16[64,1024]{1,0:T(8,128)(2,1)S(1)}, u32[]{:S(2)}, u32[]{:S(2)}) collective-permute-start(bf16[64,1024]{1,0:T(8,128)(2,1)S(1)} %get-tuple-element.11), channel_id=1, source_target_pairs={{0,6},{1,3},{2,0},{3,5},{4,2},{5,7},{6,4},{7,1},{8,14},{9,11},{10,... | collective-permute-start | bytes 393224 | tf_op jit(solution)/shard_map/ppermute | solution.py:31
  71.9 10.4 %collective-permute-done.9 = bf16[64,1024]{1,0:T(8,128)(2,1)S(1)} collective-permute-done((bf16[64,1024]{1,0:T(8,128)(2,1)S(1)}, bf16[64,1024]{1,0:T(8,128)(2,1)S(1)}, u32[]{:S(2)}, u32[]{:S(2)}) %collective-permute-start.9) | collective-permute-done | bytes 131104 | tf_op jit(solution)/shard_map/ppermute | solution.py:31
  82.4 6.1 %collective-permute-start.10 = (bf16[64,1024]{1,0:T(8,128)(2,1)S(1)}, bf16[64,1024]{1,0:T(8,128)(2,1)S(1)}, u32[]{:S(2)}, u32[]{:S(2)}) collective-permute-start(bf16[64,1024]{1,0:T(8,128)(2,1)S(1)} %add_convert_fusion.3), channel_id=1, source_target_pairs={{0,2},{1,7},{2,4},{3,1},{4,6},{5,3},{6,0},{7,5},{8,10},{9,15},{10,... | collective-permute-start | bytes 393224 | tf_op jit(solution)/shard_map/ppermute | solution.py:31
  88.5 0.0 collective-permute-done.8
  88.5 2.7 %collective-permute-done.10 = bf16[64,1024]{1,0:T(8,128)(2,1)S(1)} collective-permute-done((bf16[64,1024]{1,0:T(8,128)(2,1)S(1)}, bf16[64,1024]{1,0:T(8,128)(2,1)S(1)}, u32[]{:S(2)}, u32[]{:S(2)}) %collective-permute-start.10) | collective-permute-done | bytes 131104 | tf_op jit(solution)/shard_map/ppermute | solution.py:31
  91.2 0.1 add_convert_fusion.2
  91.3 7.0 %collective-permute-start.13 = (bf16[64,1024]{1,0:T(8,128)(2,1)S(1)}, bf16[64,1024]{1,0:T(8,128)(2,1)S(1)}, u32[]{:S(2)}, u32[]{:S(2)}) collective-permute-start(bf16[64,1024]{1,0:T(8,128)(2,1)S(1)} %add_convert_fusion.2), channel_id=1, source_target_pairs={{0,10},{1,15},{2,12},{3,9},{4,14},{5,11},{6,8},{7,13},{8,18},{9,23... | collective-permute-start | bytes 393224 | tf_op jit(solution)/shard_map/ppermute | solution.py:31
  98.3 3.3 %collective-permute-start.14 = (bf16[64,1024]{1,0:T(8,128)(2,1)S(1)}, bf16[64,1024]{1,0:T(8,128)(2,1)S(1)}, u32[]{:S(2)}, u32[]{:S(2)}) collective-permute-start(bf16[64,1024]{1,0:T(8,128)(2,1)S(1)} %add_convert_fusion.2), channel_id=1, source_target_pairs={{0,14},{1,11},{2,8},{3,13},{4,10},{5,15},{6,12},{7,9},{8,22},{9,19... | collective-permute-start | bytes 393224 | tf_op jit(solution)/shard_map/ppermute | solution.py:31
  101.6 4.5 %collective-permute-start.12 = (bf16[64,1024]{1,0:T(8,128)(2,1)S(1)}, bf16[64,1024]{1,0:T(8,128)(2,1)S(1)}, u32[]{:S(2)}, u32[]{:S(2)}) collective-permute-start(bf16[64,1024]{1,0:T(8,128)(2,1)S(1)} %add_convert_fusion.2), channel_id=1, source_target_pairs={{0,8},{1,9},{2,10},{3,11},{4,12},{5,13},{6,14},{7,15},{8,16},{9,17... | collective-permute-start | bytes 393224 | tf_op jit(solution)/shard_map/ppermute | solution.py:31
  106.1 6.2 %collective-permute-start.15 = (bf16[64,1024]{1,0:T(8,128)(2,1)S(1)}, bf16[64,1024]{1,0:T(8,128)(2,1)S(1)}, u32[]{:S(2)}, u32[]{:S(2)}) collective-permute-start(bf16[64,1024]{1,0:T(8,128)(2,1)S(1)} %collective-permute-done.13.front_ref), channel_id=1, source_target_pairs={{0,2},{1,7},{2,4},{3,1},{4,6},{5,3},{6,0},{7,5},{8,10},{9,15},{10,... | collective-permute-start | bytes 393224 | tf_op jit(solution)/shard_map/ppermute | solution.py:31
  112.3 0.0 collective-permute-done.16
  112.4 0.1 fusion.main_ref
  112.4 0.0 collective-permute-done.12.own_ref
  112.5 2.4 %collective-permute-done.15.far_ref = bf16[64,1024]{1,0:T(8,128)(2,1)S(1)} collective-permute-done((bf16[64,1024]{1,0:T(8,128)(2,1)S(1)}, bf16[64,1024]{1,0:T(8,128)(2,1)S(1)}, u32[]{:S(2)}, u32[]{:S(2)}) %collective-permute-start.15) | collective-permute-done | bytes 131104 | tf_op jit(solution)/shard_map/ppermute | solution.py:31
  114.9 5.9 %layer.3 = (f32[64,1024]{1,0:T(8,128)S(1)}, bf16[64,1024]{1,0:T(8,128)(2,1)S(1)}, bf16[64,1024]{1,0:T(8,128)(2,1)S(1)}, bf16[64,1024]{1,0:T(8,128)(2,1)S(1)}) custom-call(s32[2]{0:T(128)S(1)} %pad_add_fusion.where_ref, bf16[64,1024]{1,0:T(8,128)(2,1)S(1)} %collective-permute-done.12.own_ref, bf16[64,1024]{1,0:T(8,128)(2,1)S(1)} %collective-permute-done.13.front_ref, ...), custom_call_target="tpu_custom_call" | custom-call | flops 600000000 | bytes 20000000 | tf_op jit(solution)/shard_map/layer/pallas_call | solution.py:102
  120.7 6.2 %collective-permute-start.18 = (bf16[64,1024]{1,0:T(8,128)(2,1)S(1)}, bf16[64,1024]{1,0:T(8,128)(2,1)S(1)}, u32[]{:S(2)}, u32[]{:S(2)}) collective-permute-start(bf16[64,1024]{1,0:T(8,128)(2,1)S(1)} %get-tuple-element.17), channel_id=1, source_target_pairs={{0,2},{1,7},{2,4},{3,1},{4,6},{5,3},{6,0},{7,5},{8,10},{9,15},{10,... | collective-permute-start | bytes 393224 | tf_op jit(solution)/shard_map/ppermute | solution.py:31
  126.9 1.9 %collective-permute-start.11 = (bf16[64,512]{1,0:T(8,128)(2,1)S(1)}, bf16[64,512]{1,0:T(8,128)(2,1)S(1)}, u32[]{:S(2)}, u32[]{:S(2)}) collective-permute-start(bf16[64,512]{1,0:T(8,128)(2,1)S(1)} %broadcast_select_fusion.10), channel_id=1, source_target_pairs={{0,1},{1,0},{2,3},{3,2},{4,5},{5,4},{6,7},{7,6},{8,9},{9,8},{10,11... | collective-permute-start | bytes 196616 | tf_op jit(solution)/shard_map/ppermute | solution.py:35
  128.9 2.1 %collective-permute-start.17 = (bf16[64,1024]{1,0:T(8,128)(2,1)S(1)}, bf16[64,1024]{1,0:T(8,128)(2,1)S(1)}, u32[]{:S(2)}, u32[]{:S(2)}) collective-permute-start(bf16[64,1024]{1,0:T(8,128)(2,1)S(1)} %get-tuple-element.15), channel_id=1, source_target_pairs={{0,6},{1,3},{2,0},{3,5},{4,2},{5,7},{6,4},{7,1},{8,14},{9,11},{10,... | collective-permute-start | bytes 393224 | tf_op jit(solution)/shard_map/ppermute | solution.py:31
  131.1 6.2 %collective-permute-start.19 = (bf16[64,1024]{1,0:T(8,128)(2,1)S(1)}, bf16[64,1024]{1,0:T(8,128)(2,1)S(1)}, u32[]{:S(2)}, u32[]{:S(2)}) collective-permute-start(bf16[64,1024]{1,0:T(8,128)(2,1)S(1)} %add_convert_fusion.1), channel_id=1, source_target_pairs={{0,2},{1,7},{2,4},{3,1},{4,6},{5,3},{6,0},{7,5},{8,10},{9,15},{10,... | collective-permute-start | bytes 393224 | tf_op jit(solution)/shard_map/ppermute | solution.py:31
  137.2 0.0 collective-permute-done.11
  137.3 0.9 collective-permute-done.17
  138.2 2.0 %collective-permute-done.19 = bf16[64,1024]{1,0:T(8,128)(2,1)S(1)} collective-permute-done((bf16[64,1024]{1,0:T(8,128)(2,1)S(1)}, bf16[64,1024]{1,0:T(8,128)(2,1)S(1)}, u32[]{:S(2)}, u32[]{:S(2)}) %collective-permute-start.19) | collective-permute-done | bytes 131104 | tf_op jit(solution)/shard_map/ppermute | solution.py:31
  140.2 0.1 add_convert_fusion
  140.3 5.4 %collective-permute-start.20 = (bf16[64,512]{1,0:T(8,128)(2,1)S(1)}, bf16[64,512]{1,0:T(8,128)(2,1)S(1)}, u32[]{:S(2)}, u32[]{:S(2)}) collective-permute-start(bf16[64,512]{1,0:T(8,128)(2,1)S(1)} %broadcast_select_fusion.6), channel_id=1, source_target_pairs={{0,1},{1,0},{2,3},{3,2},{4,5},{5,4},{6,7},{7,6},{8,9},{9,8},{10,11... | collective-permute-start | bytes 196616 | tf_op jit(solution)/shard_map/ppermute | solution.py:35
  145.8 0.9 collective-permute-done.20
  146.7 0.1 broadcast_select_fusion.1
  146.8 0.1 broadcast_select_fusion.3
  146.9 0.1 broadcast_select_fusion.2
  147.0 0.7 pad_maximum_fusion.4
  (29 shorter events, 0.3 us)
Async XLA Ops:
  0.6 12.2 %copy-start.4 = (bf16[2,2,512,256]{3,2,1,0:T(8,128)(2,1)S(1)}, bf16[2,2,512,256]{3,2,1,0:T(8,128)(2,1)}, u32[]{:S(2)}) copy-start(bf16[2,2,512,256]{3,2,1,0:T(8,128)(2,1)} %param.7) | copy-start | bytes 3145732
  0.6 52.0 %collective-permute-start.4 = (bf16[4096,256]{1,0:T(8,128)(2,1)}, bf16[4096,256]{1,0:T(8,128)(2,1)}, u32[]{:S(2)}, u32[]{:S(2)}) collective-permute-start(bf16[4096,256]{1,0:T(8,128)(2,1)} %wq0_ref.3), channel_id=1, source_target_pairs={{0,1},{1,0},{2,3},{3,2},{4,5},{5,4},{6,7},{7,6},{8,9},{9,8},{10,11... | collective-permute-start | bytes 6291464 | tf_op jit(solution)/shard_map/ppermute | solution.py:35
  3.4 49.3 %collective-permute-start.7 = (bf16[256,4096]{1,0:T(8,128)(2,1)}, bf16[256,4096]{1,0:T(8,128)(2,1)}, u32[]{:S(2)}, u32[]{:S(2)}) collective-permute-start(bf16[256,4096]{1,0:T(8,128)(2,1)} %wo0_ref.3), channel_id=1, source_target_pairs={{0,1},{1,0},{2,3},{3,2},{4,5},{5,4},{6,7},{7,6},{8,9},{9,8},{10,11... | collective-permute-start | bytes 6291464 | tf_op jit(solution)/shard_map/ppermute | solution.py:35
  6.6 7.2 %collective-permute-start.5 = (bf16[2,2,256,256]{3,2,1,0:T(8,128)(2,1)S(1)}, bf16[2,2,256,256]{3,2,1,0:T(8,128)(2,1)S(1)}, u32[]{:S(2)}, u32[]{:S(2)}) collective-permute-start(bf16[2,2,256,256]{3,2,1,0:T(8,128)(2,1)S(1)} %slice_select_fusion), channel_id=1, source_target_pairs={{0,1},{1,0},{2,3},{3,2},{4,5},{5,4},{6,7},{7,6},{8,9},{9,8},{10,11... | collective-permute-start | bytes 1572872 | tf_op jit(solution)/shard_map/ppermute | solution.py:35
  10.7 21.5 %copy-start.5 = (bf16[2,2,512,256]{3,2,1,0:T(8,128)(2,1)S(1)}, bf16[2,2,512,256]{3,2,1,0:T(8,128)(2,1)}, u32[]{:S(2)}) copy-start(bf16[2,2,512,256]{3,2,1,0:T(8,128)(2,1)} %param.7) | copy-start | bytes 3145732
  10.7 8.9 %collective-permute-start = (bf16[64,512]{1,0:T(8,128)(2,1)S(1)}, bf16[64,512]{1,0:T(8,128)(2,1)S(1)}, u32[]{:S(2)}, u32[]{:S(2)}) collective-permute-start(bf16[64,512]{1,0:T(8,128)(2,1)S(1)} %get-tuple-element.35), channel_id=1, source_target_pairs={{0,1},{1,0},{2,3},{3,2},{4,5},{5,4},{6,7},{7,6},{8,9},{9,8},{10,11... | collective-permute-start | bytes 196616 | tf_op jit(solution)/shard_map/ppermute | solution.py:35
  14.6 5.1 %copy-start.7 = (bf16[1,2,256,256]{3,2,1,0:T(8,128)(2,1)}, bf16[1,2,256,256]{3,2,1,0:T(8,128)(2,1)S(1)}, u32[]{:S(2)}) copy-start(bf16[1,2,256,256]{3,2,1,0:T(8,128)(2,1)S(1)} %get-tuple-element.33) | copy-start | bytes 786436
  15.5 37.1 %copy-start = (bf16[4096,256]{1,0:T(8,128)(2,1)S(1)}, bf16[4096,256]{1,0:T(8,128)(2,1)}, u32[]{:S(2)}) copy-start(bf16[4096,256]{1,0:T(8,128)(2,1)} %wq0_ref.3) | copy-start | bytes 6291460
  15.5 30.7 %collective-permute-start.6 = (bf16[2,2,256,256]{3,2,1,0:T(8,128)(2,1)}, bf16[2,2,256,256]{3,2,1,0:T(8,128)(2,1)}, u32[]{:S(2)}, u32[]{:S(2)}) collective-permute-start(bf16[2,2,256,256]{3,2,1,0:T(8,128)(2,1)} %pad_maximum_fusion), channel_id=1, source_target_pairs={{1,65},{3,67},{5,69},{7,71},{9,73},{11,75},{13,77},{15,79},{17,81}... | collective-permute-start | bytes 1572872 | tf_op jit(solution)/shard_map/ppermute | solution.py:43
  19.7 22.0 %collective-permute-start.1 = (bf16[64,1024]{1,0:T(8,128)(2,1)S(1)}, bf16[64,1024]{1,0:T(8,128)(2,1)}, u32[]{:S(2)}, u32[]{:S(2)}) collective-permute-start(bf16[64,1024]{1,0:T(8,128)(2,1)S(1)} %maximum_select_fusion.own_ref), channel_id=1, source_target_pairs={{0,2},{1,7},{2,4},{3,1},{4,6},{5,3},{6,0},{7,5},{8,10},{9,15},{10,... | collective-permute-start | bytes 393224 | tf_op jit(solution)/shard_map/ppermute | solution.py:31
  32.4 15.1 %collective-permute-start.2 = (bf16[64,1024]{1,0:T(8,128)(2,1)S(1)}, bf16[64,1024]{1,0:T(8,128)(2,1)S(1)}, u32[]{:S(2)}, u32[]{:S(2)}) collective-permute-start(bf16[64,1024]{1,0:T(8,128)(2,1)S(1)} %maximum_select_fusion.own_ref), channel_id=1, source_target_pairs={{0,6},{1,3},{2,0},{3,5},{4,2},{5,7},{6,4},{7,1},{8,14},{9,11},{10,... | collective-permute-start | bytes 393224 | tf_op jit(solution)/shard_map/ppermute | solution.py:31
  41.7 11.0 %collective-permute-start.3 = (bf16[64,1024]{1,0:T(8,128)(2,1)}, bf16[64,1024]{1,0:T(8,128)(2,1)S(1)}, u32[]{:S(2)}, u32[]{:S(2)}) collective-permute-start(bf16[64,1024]{1,0:T(8,128)(2,1)} %collective-permute-done.1.front_ref), channel_id=1, source_target_pairs={{0,2},{1,7},{2,4},{3,1},{4,6},{5,3},{6,0},{7,5},{8,10},{9,15},{10,... | collective-permute-start | bytes 393224 | tf_op jit(solution)/shard_map/ppermute | solution.py:31
  52.7 1.6 %copy-start.1 = (bf16[256,4096]{1,0:T(8,128)(2,1)S(1)}, bf16[256,4096]{1,0:T(8,128)(2,1)}, u32[]{:S(2)}) copy-start(bf16[256,4096]{1,0:T(8,128)(2,1)} %wo0_ref.3) | copy-start | bytes 6291460
  54.3 0.9 copy-start.3
  55.2 10.8 %copy-start.6 = (bf16[1,2,256,256]{3,2,1,0:T(8,128)(2,1)S(1)}, bf16[1,2,256,256]{3,2,1,0:T(8,128)(2,1)}, u32[]{:S(2)}) copy-start(bf16[1,2,256,256]{3,2,1,0:T(8,128)(2,1)} %get-tuple-element.32) | copy-start | bytes 786436
  55.2 10.9 %copy-start.9 = (bf16[1,2,256,256]{3,2,1,0:T(8,128)(2,1)S(1)}, bf16[1,2,256,256]{3,2,1,0:T(8,128)(2,1)}, u32[]{:S(2)}) copy-start(bf16[1,2,256,256]{3,2,1,0:T(8,128)(2,1)} %get-tuple-element.29) | copy-start | bytes 786436
  55.2 57.1 %copy-start.8 = (bf16[1,2,256,256]{3,2,1,0:T(8,128)(2,1)S(1)}, bf16[1,2,256,256]{3,2,1,0:T(8,128)(2,1)}, u32[]{:S(2)}) copy-start(bf16[1,2,256,256]{3,2,1,0:T(8,128)(2,1)} %get-tuple-element.26) | copy-start | bytes 786436
  61.2 53.7 %copy-start.2 = (bf16[256,4096]{1,0:T(8,128)(2,1)S(1)}, bf16[256,4096]{1,0:T(8,128)(2,1)}, u32[]{:S(2)}) copy-start(bf16[256,4096]{1,0:T(8,128)(2,1)} %wo0_ref.3) | copy-start | bytes 6291460
  61.2 21.2 %collective-permute-start.9 = (bf16[64,1024]{1,0:T(8,128)(2,1)S(1)}, bf16[64,1024]{1,0:T(8,128)(2,1)S(1)}, u32[]{:S(2)}, u32[]{:S(2)}) collective-permute-start(bf16[64,1024]{1,0:T(8,128)(2,1)S(1)} %get-tuple-element.13), channel_id=1, source_target_pairs={{0,2},{1,7},{2,4},{3,1},{4,6},{5,3},{6,0},{7,5},{8,10},{9,15},{10,... | collective-permute-start | bytes 393224 | tf_op jit(solution)/shard_map/ppermute | solution.py:31
  66.1 46.2 %collective-permute-start.16 = (bf16[2,2,256,256]{3,2,1,0:T(8,128)(2,1)S(1)}, bf16[2,2,256,256]{3,2,1,0:T(8,128)(2,1)S(1)}, u32[]{:S(2)}, u32[]{:S(2)}) collective-permute-start(bf16[2,2,256,256]{3,2,1,0:T(8,128)(2,1)S(1)} %pad_maximum_fusion.2), channel_id=1, source_target_pairs={{1,65},{3,67},{5,69},{7,71},{9,73},{11,75},{13,77},{15,79},{17,81}... | collective-permute-start | bytes 1572872 | tf_op jit(solution)/shard_map/ppermute | solution.py:43
  68.1 20.4 %collective-permute-start.8 = (bf16[64,1024]{1,0:T(8,128)(2,1)S(1)}, bf16[64,1024]{1,0:T(8,128)(2,1)S(1)}, u32[]{:S(2)}, u32[]{:S(2)}) collective-permute-start(bf16[64,1024]{1,0:T(8,128)(2,1)S(1)} %get-tuple-element.11), channel_id=1, source_target_pairs={{0,6},{1,3},{2,0},{3,5},{4,2},{5,7},{6,4},{7,1},{8,14},{9,11},{10,... | collective-permute-start | bytes 393224 | tf_op jit(solution)/shard_map/ppermute | solution.py:31
  82.4 8.8 %collective-permute-start.10 = (bf16[64,1024]{1,0:T(8,128)(2,1)S(1)}, bf16[64,1024]{1,0:T(8,128)(2,1)S(1)}, u32[]{:S(2)}, u32[]{:S(2)}) collective-permute-start(bf16[64,1024]{1,0:T(8,128)(2,1)S(1)} %add_convert_fusion.3), channel_id=1, source_target_pairs={{0,2},{1,7},{2,4},{3,1},{4,6},{5,3},{6,0},{7,5},{8,10},{9,15},{10,... | collective-permute-start | bytes 393224 | tf_op jit(solution)/shard_map/ppermute | solution.py:31
  91.3 14.8 %collective-permute-start.13 = (bf16[64,1024]{1,0:T(8,128)(2,1)S(1)}, bf16[64,1024]{1,0:T(8,128)(2,1)S(1)}, u32[]{:S(2)}, u32[]{:S(2)}) collective-permute-start(bf16[64,1024]{1,0:T(8,128)(2,1)S(1)} %add_convert_fusion.2), channel_id=1, source_target_pairs={{0,10},{1,15},{2,12},{3,9},{4,14},{5,11},{6,8},{7,13},{8,18},{9,23... | collective-permute-start | bytes 393224 | tf_op jit(solution)/shard_map/ppermute | solution.py:31
  98.3 14.1 %collective-permute-start.14 = (bf16[64,1024]{1,0:T(8,128)(2,1)S(1)}, bf16[64,1024]{1,0:T(8,128)(2,1)S(1)}, u32[]{:S(2)}, u32[]{:S(2)}) collective-permute-start(bf16[64,1024]{1,0:T(8,128)(2,1)S(1)} %add_convert_fusion.2), channel_id=1, source_target_pairs={{0,14},{1,11},{2,8},{3,13},{4,10},{5,15},{6,12},{7,9},{8,22},{9,19... | collective-permute-start | bytes 393224 | tf_op jit(solution)/shard_map/ppermute | solution.py:31
  101.6 10.8 %collective-permute-start.12 = (bf16[64,1024]{1,0:T(8,128)(2,1)S(1)}, bf16[64,1024]{1,0:T(8,128)(2,1)S(1)}, u32[]{:S(2)}, u32[]{:S(2)}) collective-permute-start(bf16[64,1024]{1,0:T(8,128)(2,1)S(1)} %add_convert_fusion.2), channel_id=1, source_target_pairs={{0,8},{1,9},{2,10},{3,11},{4,12},{5,13},{6,14},{7,15},{8,16},{9,17... | collective-permute-start | bytes 393224 | tf_op jit(solution)/shard_map/ppermute | solution.py:31
  106.1 8.7 %collective-permute-start.15 = (bf16[64,1024]{1,0:T(8,128)(2,1)S(1)}, bf16[64,1024]{1,0:T(8,128)(2,1)S(1)}, u32[]{:S(2)}, u32[]{:S(2)}) collective-permute-start(bf16[64,1024]{1,0:T(8,128)(2,1)S(1)} %collective-permute-done.13.front_ref), channel_id=1, source_target_pairs={{0,2},{1,7},{2,4},{3,1},{4,6},{5,3},{6,0},{7,5},{8,10},{9,15},{10,... | collective-permute-start | bytes 393224 | tf_op jit(solution)/shard_map/ppermute | solution.py:31
  120.7 10.3 %collective-permute-start.18 = (bf16[64,1024]{1,0:T(8,128)(2,1)S(1)}, bf16[64,1024]{1,0:T(8,128)(2,1)S(1)}, u32[]{:S(2)}, u32[]{:S(2)}) collective-permute-start(bf16[64,1024]{1,0:T(8,128)(2,1)S(1)} %get-tuple-element.17), channel_id=1, source_target_pairs={{0,2},{1,7},{2,4},{3,1},{4,6},{5,3},{6,0},{7,5},{8,10},{9,15},{10,... | collective-permute-start | bytes 393224 | tf_op jit(solution)/shard_map/ppermute | solution.py:31
  126.9 10.3 %collective-permute-start.11 = (bf16[64,512]{1,0:T(8,128)(2,1)S(1)}, bf16[64,512]{1,0:T(8,128)(2,1)S(1)}, u32[]{:S(2)}, u32[]{:S(2)}) collective-permute-start(bf16[64,512]{1,0:T(8,128)(2,1)S(1)} %broadcast_select_fusion.10), channel_id=1, source_target_pairs={{0,1},{1,0},{2,3},{3,2},{4,5},{5,4},{6,7},{7,6},{8,9},{9,8},{10,11... | collective-permute-start | bytes 196616 | tf_op jit(solution)/shard_map/ppermute | solution.py:35
  128.9 9.3 %collective-permute-start.17 = (bf16[64,1024]{1,0:T(8,128)(2,1)S(1)}, bf16[64,1024]{1,0:T(8,128)(2,1)S(1)}, u32[]{:S(2)}, u32[]{:S(2)}) collective-permute-start(bf16[64,1024]{1,0:T(8,128)(2,1)S(1)} %get-tuple-element.15), channel_id=1, source_target_pairs={{0,6},{1,3},{2,0},{3,5},{4,2},{5,7},{6,4},{7,1},{8,14},{9,11},{10,... | collective-permute-start | bytes 393224 | tf_op jit(solution)/shard_map/ppermute | solution.py:31
  131.1 9.2 %collective-permute-start.19 = (bf16[64,1024]{1,0:T(8,128)(2,1)S(1)}, bf16[64,1024]{1,0:T(8,128)(2,1)S(1)}, u32[]{:S(2)}, u32[]{:S(2)}) collective-permute-start(bf16[64,1024]{1,0:T(8,128)(2,1)S(1)} %add_convert_fusion.1), channel_id=1, source_target_pairs={{0,2},{1,7},{2,4},{3,1},{4,6},{5,3},{6,0},{7,5},{8,10},{9,15},{10,... | collective-permute-start | bytes 393224 | tf_op jit(solution)/shard_map/ppermute | solution.py:31
  140.3 6.3 %collective-permute-start.20 = (bf16[64,512]{1,0:T(8,128)(2,1)S(1)}, bf16[64,512]{1,0:T(8,128)(2,1)S(1)}, u32[]{:S(2)}, u32[]{:S(2)}) collective-permute-start(bf16[64,512]{1,0:T(8,128)(2,1)S(1)} %broadcast_select_fusion.6), channel_id=1, source_target_pairs={{0,1},{1,0},{2,3},{3,2},{4,5},{5,4},{6,7},{7,6},{8,9},{9,8},{10,11... | collective-permute-start | bytes 196616 | tf_op jit(solution)/shard_map/ppermute | solution.py:35

commit v3 on v2

v3 whole, which is shorter than its diff:
```python
import functools

import jax
import jax.numpy as jnp
from jax import lax
from jax.experimental import pallas as pl
from jax.experimental.pallas import tpu as pltpu
from jax.sharding import PartitionSpec as P


HD = 128
SECT = 8
SPAN = 256
EPS = 1e-05
CORES = 2


def beside(chip, core):
    return chip ^ 1 if core == 0 else 3 - chip


def across(chip, core):
    return 3 - chip if core == 0 else chip ^ 1


def beside_of_other(chip, core):
    return beside(chip, 1 - core)


def here(chip, core):
    return chip


def permuted(block, place, sections_on=0, turn=0):
    size = lax.axis_size("segment")
    per_section = size // SECT
    assert per_section == 4 * CORES
    route = []
    for source in range(size - sections_on * per_section):
        section, group = divmod(source, per_section)
        chip, core = divmod(group, CORES)
        route.append((source, (section + sections_on) * per_section + place(chip, core) * CORES + (core ^ turn)))
    return lax.ppermute(block, "segment", route)


def swap_cores(block):
    return permuted(block, here, turn=1)


def from_previous(block):
    size = lax.axis_size("seq")
    return lax.ppermute(block, "seq", [(i, i + 1) for i in range(size - 1)])


def attend(queries, keys, values):
    scores = lax.dot_general(
        queries, keys, (((1,), (1,)), ((), ())), preferred_element_type=jnp.float32
    ) * HD ** (-0.5)
    exponent = jnp.exp(scores)
    weights = (exponent / jnp.sum(exponent, axis=-1, keepdims=True)).astype(jnp.bfloat16)
    return jnp.dot(weights, values, preferred_element_type=jnp.float32)


def add_queries(ref, sources, wq_refs, queries, total):
    rows, width = ref.shape[0] // 2, ref.shape[1]
    for i, source in enumerate(sources):
        part = ref[i * rows : (i + 1) * rows, :]
        wide = part.astype(jnp.float32)
        total += jnp.sum(wide * wide, axis=-1, keepdims=True)
        offset = pl.multiple_of(source * width, width)
        queries = [
            q + jnp.dot(part, wq_ref[pl.ds(offset, width), :], preferred_element_type=jnp.float32)
            for q, wq_ref in zip(queries, wq_refs)
        ]
    return queries, total


def put_terms(attended, targets, wo_refs, out_ref):
    rows, width = out_ref.shape[0] // 2, out_ref.shape[1]
    for i, target in enumerate(targets):
        offset = pl.multiple_of(target * width, width)
        cols = wo_refs[0].shape[0]
        term = sum(
            jnp.dot(attended[:, n * cols : (n + 1) * cols], wo_ref[:, pl.ds(offset, width)], preferred_element_type=jnp.float32)
            for n, wo_ref in enumerate(wo_refs)
        )
        out_ref[i * rows : (i + 1) * rows, :] = term.astype(out_ref.dtype)


def front_kernel(where_ref, pair_ref, wq0_ref, wq1_ref, queries_ref, total_ref):
    rows, cols = queries_ref.shape[0], wq0_ref.shape[1]
    queries = [jnp.zeros((rows, cols), jnp.float32) for _ in range(CORES)]
    total = jnp.zeros((rows, 1), jnp.float32)
    queries, total = add_queries(pair_ref, (where_ref[0], where_ref[1]), (wq0_ref, wq1_ref), queries, total)
    for i in range(CORES):
        queries_ref[:, i * cols : (i + 1) * cols] = queries[i]
    total_ref[...] = jnp.broadcast_to(total, total_ref.shape)


def middle_kernel(
    tick, where_ref, distant_ref, queries_ref, total_ref, wq0_ref, wq1_ref, kv_ref, edge_ref, other_ref, wo0_ref, wo1_ref,
    attended_ref, terms_ref,
):
    core = where_ref[4]
    rows, cols = attended_ref.shape[0], wq0_ref.shape[1]
    queries = [queries_ref[:, i * cols : (i + 1) * cols] for i in range(CORES)]
    distant = (where_ref[2], where_ref[3])
    queries, total = add_queries(distant_ref, distant, (wq0_ref, wq1_ref), queries, total_ref[:, :1])
    scale = lax.rsqrt(total / wq0_ref.shape[0] + EPS)
    last_row = lax.broadcasted_iota(jnp.int32, (16, HD), 0) == 15
    for i in range(CORES):
        q = (queries[i] * scale).astype(jnp.bfloat16)
        for h in range(cols // HD):
            head = slice(h * HD, (h + 1) * HD)
            out = slice(i * cols + h * HD, i * cols + (h + 1) * HD)
            if i == 0:
                mains = [jnp.where(core == 0, kv_ref[tick, n, :SPAN, head], edge_ref[n, :, head]) for n in range(2)]
                ends = [kv_ref[tick, n, SPAN:, head] for n in range(2)]
            else:
                mains = [other_ref[0, n, :, head] for n in range(2)]
                ends = [other_ref[1, n, :, head] for n in range(2)]
            main = attend(q[:, head], *mains)
            end = attend(q[rows - 16 :, head], *ends)
            end = jnp.where(last_row & (core > 0), end, main[rows - 16 :])
            attended_ref[: rows - 16, out] = main[: rows - 16].astype(jnp.bfloat16)
            attended_ref[rows - 16 :, out] = end.astype(jnp.bfloat16)
    put_terms(attended_ref[...], distant, (wo0_ref, wo1_ref), terms_ref)


def back_kernel(where_ref, attended_ref, wo0_ref, wo1_ref, terms_ref):
    put_terms(attended_ref[...], (where_ref[0], where_ref[1]), (wo0_ref, wo1_ref), terms_ref)


def pair_kernel(where_ref, mine_ref, moved_ref, beside_mine_ref, beside_given_ref, pair_ref):
    rows, width = mine_ref.shape
    first_core = where_ref[4] == 0
    for i, (own_ref, other_ref) in enumerate(((mine_ref, moved_ref), (beside_mine_ref, beside_given_ref))):
        own, other = own_ref[...], other_ref[...]
        pair_ref[i * rows : (i + 1) * rows, :width] = jnp.where(first_core, own, other)
        pair_ref[i * rows : (i + 1) * rows, width:] = jnp.where(first_core, other, own)


def join_kernel(where_ref, ours_ref, theirs_ref, pair_ref):
    rows = pair_ref.shape[0] // 2
    for i in range(2):
        here_rows, other_rows = slice(i * rows, (i + 1) * rows), slice((1 - i) * rows, (2 - i) * rows)
        total = ours_ref[here_rows, :].astype(jnp.float32) + theirs_ref[other_rows, :].astype(jnp.float32)
        pair_ref[here_rows, :] = total.astype(pair_ref.dtype)


def call(kernel, shapes, flops, nbytes, *operands):
    vmem = pl.BlockSpec(memory_space=pltpu.VMEM)
    return pl.pallas_call(
        kernel,
        in_specs=[pl.BlockSpec(memory_space=pltpu.SMEM)] + [vmem] * (len(operands) - 1),
        out_specs=(vmem,) * len(shapes),
        out_shape=tuple(jax.ShapeDtypeStruct(*shape) for shape in shapes),
        cost_estimate=pl.CostEstimate(flops=flops, bytes_accessed=nbytes, transcendentals=0),
        compiler_params=pltpu.CompilerParams(vmem_limit_bytes=12 << 20),
    )(*operands)


def per_device(stream, w_query, w_out, neighbour_kv):
    per_section = lax.axis_size("segment") // SECT
    group = lax.axis_index("segment") % per_section
    chip, core = group // CORES, group % CORES
    first_core = core == 0
    near = jnp.where(first_core, chip ^ 1, 3 - chip)
    far = jnp.where(first_core, 3 - chip, chip ^ 1)
    where = jnp.stack([chip, near, far, chip ^ 2, core]).astype(jnp.int32)
    half, width = stream.shape[0] // 2, stream.shape[1]
    end = lax.broadcasted_iota(jnp.int32, (half, width), 0) == half - 1
    low_first = first_core != end

    def features(block, wanted):
        return jnp.where(wanted, block[:, :width], block[:, width:])

    def arranged(own, other):
        return jnp.concatenate([jnp.where(low_first, other, own), jnp.where(low_first, own, other)], axis=0)

    top, low = stream[:half], stream[half:]
    mine = jnp.where(low_first, low, top)
    given = jnp.where(low_first, top, low)
    beside_mine = permuted(mine, beside)
    beside_given = permuted(given, beside_of_other, turn=1)
    moved = swap_cores(given)
    block = (2 * half, 2 * width)
    (pair,) = call(
        pair_kernel, ((block, jnp.bfloat16),), 0, 500_000, where, mine, moved, beside_mine, beside_given
    )

    edges = [from_previous(neighbour_kv[0, :, SPAN:])]
    later_kv, _ = lax.optimization_barrier((neighbour_kv, pair))
    near_kv, far_kv = later_kv[:, :, :SPAN], later_kv[:, :, SPAN:]
    edges.append(from_previous(far_kv[1]))
    wq_other = swap_cores(w_query)
    wo_other = swap_cores(w_out)

    for tick in range(2):
        distant = permuted(pair, across)
        given = jnp.where(first_core, jnp.stack([edges[tick], far_kv[tick]]), jnp.stack([near_kv[tick]] * 2))
        other_kv = swap_cores(given)
        wide = (half, 2 * wq_other.shape[1])
        queries, total = call(
            front_kernel, ((wide, jnp.float32), ((half, HD), jnp.float32)), 140_000_000, 3_000_000, where, pair, w_query, wq_other
        )
        attended, terms = call(
            functools.partial(middle_kernel, tick), ((wide, jnp.bfloat16), (block, jnp.bfloat16)), 350_000_000, 10_000_000,
            where, distant, queries, total, w_query, wq_other, neighbour_kv, edges[tick], other_kv, w_out, wo_other,
        )
        summed = permuted(terms, across)
        (terms,) = call(back_kernel, ((block, jnp.float32),), 140_000_000, 3_000_000, where, attended, w_out, wo_other)
        base = jnp.concatenate([pair[:half], jnp.zeros_like(pair[half:])], axis=0)
        part = (terms + summed.astype(jnp.float32) + base.astype(jnp.float32)).astype(jnp.bfloat16)
        own, theirs = part[:half], part[half:]
        if tick == 0:
            ours = permuted(part, beside, 1)
            pair = permuted(part, here, 1)
            (pair,) = call(join_kernel, ((block, jnp.bfloat16),), 0, 800_000, where, pair, ours)
            from_near = permuted(theirs, beside)
            own = (own.astype(jnp.float32) + from_near.astype(jnp.float32)).astype(jnp.bfloat16)
            other = swap_cores(features(own, core == 1))
            first = arranged(features(own, first_core), other)
        else:
            from_near = permuted(features(theirs, first_core), beside)
            other_near = permuted(features(theirs, core == 1), beside, turn=1)
            other = swap_cores(features(own, core == 1))
            own = features(own, first_core).astype(jnp.float32) + from_near.astype(jnp.float32)
            other = other.astype(jnp.float32) + other_near.astype(jnp.float32)
            second = arranged(own.astype(jnp.bfloat16), other.astype(jnp.bfloat16))
    return first, second


def solution(mesh):
    placed = (
        P("seq", "segment"),
        P(None, "segment"),
        P("segment", None),
        P(None, None, "seq", "segment"),
    )
    return jax.shard_map(
        per_device,
        mesh=mesh,
        in_specs=placed,
        out_specs=(P("seq", "segment"), P("seq", "segment")),
        check_vma=False,
    )
```

time: 149 us -> 155 us (1.040)
  the two profiles are of different devices: /device:TPU:73 before, /device:TPU:18 now
where the time goes in v3:
time: 155 us
  starting transfers between devices  85.4 us (55%)
  waiting for transfers between devices  41.5 us (27%)
  Pallas kernels  20.5 us (13%)
  other arithmetic  4.26 us (3%)
  local copies, waits for them, and re-layouts  1.85 us (1%)
    ppermute x18, starting transfers between devices, permuted(): return lax.ppermute(block, 'segment', route)  79.3 us
    ppermute x18, waiting for transfers between devices, permuted(): return lax.ppermute(block, 'segment', route)  34 us
    pallas_call x8, Pallas kernels, call(): pl.pallas_call(kernel, in_specs=[pl.BlockSpec(memory_space=pltpu.SMEM)] +...  20.5 us
    ppermute x2, waiting for transfers between devices, from_previous(): return lax.ppermute(block, 'seq', [(i, i + 1) for i in range(size - 1)])  7.5 us
    ppermute x2, starting transfers between devices, from_previous(): return lax.ppermute(block, 'seq', [(i, i + 1) for i in range(size - 1)])  6.04 us
  transfers between devices with their start and end apart: 20, of which 9 were waited for; matrix products, arithmetic and copies ran while one was open for 3% of the time, Pallas kernels for 13%

profile of v3, /device:TPU:18, one launch (start us, length us, event | category | flops | bytes accessed | tf_op | source)
XLA Modules:
  0.0 154.5 jit_solution(3892635941942422195)
XLA Ops:
  0.6 0.0 copy-start.2
  0.6 2.1 %collective-permute-start.4 = (bf16[4096,256]{1,0:T(8,128)(2,1)}, bf16[4096,256]{1,0:T(8,128)(2,1)}, u32[]{:S(2)}, u32[]{:S(2)}) collective-permute-start(bf16[4096,256]{1,0:T(8,128)(2,1)} %wq0_ref.7), channel_id=1, source_target_pairs={{0,1},{1,0},{2,3},{3,2},{4,5},{5,4},{6,7},{7,6},{8,9},{9,8},{10,11... | collective-permute-start | bytes 6291464 | tf_op jit(solution)/shard_map/ppermute | solution.py:43
  2.7 2.4 %collective-permute-start.7 = (bf16[256,4096]{1,0:T(8,128)(2,1)}, bf16[256,4096]{1,0:T(8,128)(2,1)}, u32[]{:S(2)}, u32[]{:S(2)}) collective-permute-start(bf16[256,4096]{1,0:T(8,128)(2,1)} %wo0_ref.7), channel_id=1, source_target_pairs={{0,1},{1,0},{2,3},{3,2},{4,5},{5,4},{6,7},{7,6},{8,9},{9,8},{10,11... | collective-permute-start | bytes 6291464 | tf_op jit(solution)/shard_map/ppermute | solution.py:43
  5.2 1.0 broadcast_select_fusion.4
  6.1 14.2 %collective-permute-start.2 = (bf16[64,512]{1,0:T(8,128)(2,1)S(1)}, bf16[64,512]{1,0:T(8,128)(2,1)S(1)}, u32[]{:S(2)}, u32[]{:S(2)}) collective-permute-start(bf16[64,512]{1,0:T(8,128)(2,1)S(1)} %get-tuple-element.32), channel_id=1, source_target_pairs={{0,7},{1,2},{2,5},{3,0},{4,3},{5,6},{6,1},{7,4},{8,15},{9,10},{10,... | collective-permute-start | bytes 196616 | tf_op jit(solution)/shard_map/ppermute | solution.py:43
  20.3 1.9 %collective-permute-start = (bf16[64,512]{1,0:T(8,128)(2,1)S(1)}, bf16[64,512]{1,0:T(8,128)(2,1)S(1)}, u32[]{:S(2)}, u32[]{:S(2)}) collective-permute-start(bf16[64,512]{1,0:T(8,128)(2,1)S(1)} %get-tuple-element.32), channel_id=1, source_target_pairs={{0,1},{1,0},{2,3},{3,2},{4,5},{5,4},{6,7},{7,6},{8,9},{9,8},{10,11... | collective-permute-start | bytes 196616 | tf_op jit(solution)/shard_map/ppermute | solution.py:43
  22.2 2.4 %collective-permute-start.1 = (bf16[64,512]{1,0:T(8,128)(2,1)S(1)}, bf16[64,512]{1,0:T(8,128)(2,1)S(1)}, u32[]{:S(2)}, u32[]{:S(2)}) collective-permute-start(bf16[64,512]{1,0:T(8,128)(2,1)S(1)} %get-tuple-element.33.mine_ref), channel_id=1, source_target_pairs={{0,2},{1,7},{2,0},{3,5},{4,6},{5,3},{6,4},{7,1},{8,10},{9,15},{10,... | collective-permute-start | bytes 196616 | tf_op jit(solution)/shard_map/ppermute | solution.py:43
  24.7 1.0 slice_bitcast_fusion
  25.7 0.0 collective-permute-done.2.beside_given_ref
  25.7 4.0 %collective-permute-start.5 = (bf16[2,256,256]{2,1,0:T(8,128)(2,1)S(1)}, bf16[2,256,256]{2,1,0:T(8,128)(2,1)S(1)}, u32[]{:S(2)}, u32[]{:S(2)}) collective-permute-start(bf16[2,256,256]{2,1,0:T(8,128)(2,1)S(1)} %slice_bitcast_fusion), channel_id=1, source_target_pairs={{0,64},{64,128},{128,192},{192,256},{256,320},{320,384},{384,448},... | collective-permute-start | bytes 786440 | tf_op jit(solution)/shard_map/ppermute | solution.py:52
  29.7 0.1 stack.41.where_ref
  29.8 0.0 collective-permute-done.moved_ref
  29.8 0.4 collective-permute-done.1.beside_mine_ref
  30.2 0.6 shard_map.59.pair_ref
  30.8 0.1 fusion
  30.9 7.5 %collective-permute-done.5.edge_ref = bf16[2,256,256]{2,1,0:T(8,128)(2,1)S(1)} collective-permute-done((bf16[2,256,256]{2,1,0:T(8,128)(2,1)S(1)}, bf16[2,256,256]{2,1,0:T(8,128)(2,1)S(1)}, u32[]{:S(2)}, u32[]{:S(2)}) %collective-permute-start.5) | collective-permute-done | bytes 262176 | tf_op jit(solution)/shard_map/ppermute | solution.py:52
  38.4 0.1 maximum_select_fusion
  38.5 1.9 %collective-permute-start.6 = (bf16[2,2,256,256]{3,2,1,0:T(8,128)(2,1)S(1)}, bf16[2,2,256,256]{3,2,1,0:T(8,128)(2,1)S(1)}, u32[]{:S(2)}, u32[]{:S(2)}) collective-permute-start(bf16[2,2,256,256]{3,2,1,0:T(8,128)(2,1)S(1)} %maximum_select_fusion), channel_id=1, source_target_pairs={{0,1},{1,0},{2,3},{3,2},{4,5},{5,4},{6,7},{7,6},{8,9},{9,8},{10,11... | collective-permute-start | bytes 1572872 | tf_op jit(solution)/shard_map/ppermute | solution.py:43
  40.4 5.8 %collective-permute-start.3 = (bf16[128,1024]{1,0:T(8,128)(2,1)S(1)}, bf16[128,1024]{1,0:T(8,128)(2,1)S(1)}, u32[]{:S(2)}, u32[]{:S(2)}) collective-permute-start(bf16[128,1024]{1,0:T(8,128)(2,1)S(1)} %shard_map.59.pair_ref), channel_id=1, source_target_pairs={{0,6},{1,3},{2,4},{3,1},{4,2},{5,7},{6,0},{7,5},{8,14},{9,11},{10,... | collective-permute-start | bytes 786440 | tf_op jit(solution)/shard_map/ppermute | solution.py:43
  46.2 0.0 copy-start
  46.2 2.1 %collective-permute-start.14 = (bf16[2,256,256]{2,1,0:T(8,128)(2,1)S(1)}, bf16[2,256,256]{2,1,0:T(8,128)(2,1)S(1)}, u32[]{:S(2)}, u32[]{:S(2)}) collective-permute-start(bf16[2,256,256]{2,1,0:T(8,128)(2,1)S(1)} %get-tuple-element.23), channel_id=1, source_target_pairs={{0,64},{64,128},{128,192},{192,256},{256,320},{320,384},{384,448},... | collective-permute-start | bytes 786440 | tf_op jit(solution)/shard_map/ppermute | solution.py:52
  48.3 0.0 collective-permute-done.4.wq1_ref
  48.3 2.1 %shard_map.60 = (f32[64,512]{1,0:T(8,128)S(1)}, f32[64,128]{1,0:T(8,128)S(1)}) custom-call(s32[5]{0:T(128)S(1)} %stack.41.where_ref, bf16[128,1024]{1,0:T(8,128)(2,1)S(1)} %shard_map.59.pair_ref, bf16[4096,256]{1,0:T(8,128)(2,1)S(1)} %copy-done.1, bf16[4096,256]{1,0:T(8,128)(2,1)} %collective-permute-done.4.wq1_ref), custom_call_target="tpu_custom_call" | custom-call | flops 140000000 | bytes 3000000 | tf_op jit(solution)/shard_map/pallas_call | solution.py:153
  50.4 9.6 %collective-permute-done.3.distant_ref = bf16[128,1024]{1,0:T(8,128)(2,1)S(1)} collective-permute-done((bf16[128,1024]{1,0:T(8,128)(2,1)S(1)}, bf16[128,1024]{1,0:T(8,128)(2,1)S(1)}, u32[]{:S(2)}, u32[]{:S(2)}) %collective-permute-start.3) | collective-permute-done | bytes 262176 | tf_op jit(solution)/shard_map/ppermute | solution.py:43
  60.0 0.0 collective-permute-done.6.other_ref
  60.0 0.0 collective-permute-done.7.wo1_ref
  60.0 5.1 %shard_map.61 = (bf16[64,512]{1,0:T(8,128)(2,1)S(1)}, bf16[128,1024]{1,0:T(8,128)(2,1)S(1)}) custom-call(s32[5]{0:T(128)S(1)} %stack.41.where_ref, bf16[128,1024]{1,0:T(8,128)(2,1)S(1)} %collective-permute-done.3.distant_ref, f32[64,512]{1,0:T(8,128)S(1)} %get-tuple-element.11.queries_ref, f32[64,128]{1,0:T(8,128)S(1)} %get-tuple-element.12.total_ref, ...), custom_call_target="tpu_custom_call" | custom-call | flops 350000000 | bytes 10000000 | tf_op jit(solution)/shard_map/pallas_call | solution.py:153
  65.1 2.3 %collective-permute-start.8 = (bf16[128,1024]{1,0:T(8,128)(2,1)S(1)}, bf16[128,1024]{1,0:T(8,128)(2,1)S(1)}, u32[]{:S(2)}, u32[]{:S(2)}) collective-permute-start(bf16[128,1024]{1,0:T(8,128)(2,1)S(1)} %get-tuple-element.15), channel_id=1, source_target_pairs={{0,6},{1,3},{2,4},{3,1},{4,2},{5,7},{6,0},{7,5},{8,14},{9,11},{10,... | collective-permute-start | bytes 786440 | tf_op jit(solution)/shard_map/ppermute | solution.py:43
  67.4 0.0 collective-permute-done.14.edge_ref
  67.4 0.1 maximum_select_fusion.1
  67.5 0.0 copy-start.4
  67.5 2.1 %shard_map.62 = f32[128,1024]{1,0:T(8,128)S(1)} custom-call(s32[5]{0:T(128)S(1)} %stack.41.where_ref, bf16[64,512]{1,0:T(8,128)(2,1)S(1)} %get-tuple-element.14.attended_ref, bf16[256,4096]{1,0:T(8,128)(2,1)S(1)} %copy-done, bf16[256,4096]{1,0:T(8,128)(2,1)} %collective-permute-done.7.wo1_ref), custom_call_target="tpu_custom_call" | custom-call | flops 140000000 | bytes 3000000 | tf_op jit(solution)/shard_map/pallas_call | solution.py:153
  69.6 6.9 %collective-permute-done.8 = bf16[128,1024]{1,0:T(8,128)(2,1)S(1)} collective-permute-done((bf16[128,1024]{1,0:T(8,128)(2,1)S(1)}, bf16[128,1024]{1,0:T(8,128)(2,1)S(1)}, u32[]{:S(2)}, u32[]{:S(2)}) %collective-permute-start.8) | collective-permute-done | bytes 262176 | tf_op jit(solution)/shard_map/ppermute | solution.py:43
  76.5 0.1 add_convert_fusion.1
  76.7 3.9 %collective-permute-start.12 = (bf16[128,1024]{1,0:T(8,128)(2,1)S(1)}, bf16[128,1024]{1,0:T(8,128)(2,1)S(1)}, u32[]{:S(2)}, u32[]{:S(2)}) collective-permute-start(bf16[128,1024]{1,0:T(8,128)(2,1)S(1)} %add_convert_fusion.1), channel_id=1, source_target_pairs={{0,10},{1,15},{2,8},{3,13},{4,14},{5,11},{6,12},{7,9},{8,18},{9,23... | collective-permute-start | bytes 786440 | tf_op jit(solution)/shard_map/ppermute | solution.py:43
  80.5 4.7 %collective-permute-start.11 = (bf16[128,1024]{1,0:T(8,128)(2,1)S(1)}, bf16[128,1024]{1,0:T(8,128)(2,1)S(1)}, u32[]{:S(2)}, u32[]{:S(2)}) collective-permute-start(bf16[128,1024]{1,0:T(8,128)(2,1)S(1)} %add_convert_fusion.1), channel_id=1, source_target_pairs={{0,8},{1,9},{2,10},{3,11},{4,12},{5,13},{6,14},{7,15},{8,16},{9,17... | collective-permute-start | bytes 786440 | tf_op jit(solution)/shard_map/ppermute | solution.py:43
  85.2 1.9 %collective-permute-start.15 = (bf16[2,2,256,256]{3,2,1,0:T(8,128)(2,1)S(1)}, bf16[2,2,256,256]{3,2,1,0:T(8,128)(2,1)S(1)}, u32[]{:S(2)}, u32[]{:S(2)}) collective-permute-start(bf16[2,2,256,256]{3,2,1,0:T(8,128)(2,1)S(1)} %maximum_select_fusion.1), channel_id=1, source_target_pairs={{0,1},{1,0},{2,3},{3,2},{4,5},{5,4},{6,7},{7,6},{8,9},{9,8},{10,11... | collective-permute-start | bytes 1572872 | tf_op jit(solution)/shard_map/ppermute | solution.py:43
  87.2 3.1 %collective-permute-done.12.theirs_ref = bf16[128,1024]{1,0:T(8,128)(2,1)S(1)} collective-permute-done((bf16[128,1024]{1,0:T(8,128)(2,1)S(1)}, bf16[128,1024]{1,0:T(8,128)(2,1)S(1)}, u32[]{:S(2)}, u32[]{:S(2)}) %collective-permute-start.12) | collective-permute-done | bytes 262176 | tf_op jit(solution)/shard_map/ppermute | solution.py:43
  90.3 5.2 %collective-permute-done.11.ours_ref = bf16[128,1024]{1,0:T(8,128)(2,1)S(1)} collective-permute-done((bf16[128,1024]{1,0:T(8,128)(2,1)S(1)}, bf16[128,1024]{1,0:T(8,128)(2,1)S(1)}, u32[]{:S(2)}, u32[]{:S(2)}) %collective-permute-start.11) | collective-permute-done | bytes 262176 | tf_op jit(solution)/shard_map/ppermute | solution.py:43
  95.5 0.6 shard_map.63.pair_ref
  96.1 4.0 %collective-permute-start.13 = (bf16[128,1024]{1,0:T(8,128)(2,1)S(1)}, bf16[128,1024]{1,0:T(8,128)(2,1)S(1)}, u32[]{:S(2)}, u32[]{:S(2)}) collective-permute-start(bf16[128,1024]{1,0:T(8,128)(2,1)S(1)} %shard_map.63.pair_ref), channel_id=1, source_target_pairs={{0,6},{1,3},{2,4},{3,1},{4,2},{5,7},{6,0},{7,5},{8,14},{9,11},{10,... | collective-permute-start | bytes 786440 | tf_op jit(solution)/shard_map/ppermute | solution.py:43
  100.1 0.7 slice.84
  100.8 7.8 %collective-permute-start.9 = (bf16[64,1024]{1,0:T(8,128)(2,1)}, bf16[64,1024]{1,0:T(8,128)(2,1)}, u32[]{:S(2)}, u32[]{:S(2)}) collective-permute-start(bf16[64,1024]{1,0:T(8,128)(2,1)} %slice.84), channel_id=1, source_target_pairs={{0,2},{1,7},{2,0},{3,5},{4,6},{5,3},{6,4},{7,1},{8,10},{9,15},{10,... | collective-permute-start | bytes 393224 | tf_op jit(solution)/shard_map/ppermute | solution.py:43
  108.7 2.1 %shard_map.64 = (f32[64,512]{1,0:T(8,128)S(1)}, f32[64,128]{1,0:T(8,128)S(1)}) custom-call(s32[5]{0:T(128)S(1)} %stack.41.where_ref, bf16[128,1024]{1,0:T(8,128)(2,1)S(1)} %shard_map.63.pair_ref, bf16[4096,256]{1,0:T(8,128)(2,1)S(1)} %copy-done.1, bf16[4096,256]{1,0:T(8,128)(2,1)} %collective-permute-done.4.wq1_ref), custom_call_target="tpu_custom_call" | custom-call | flops 140000000 | bytes 3000000 | tf_op jit(solution)/shard_map/pallas_call | solution.py:153
  110.8 0.0 collective-permute-done.15.other_ref
  110.8 0.4 collective-permute-done.13.distant_ref
  111.2 5.8 %shard_map.65 = (bf16[64,512]{1,0:T(8,128)(2,1)S(1)}, bf16[128,1024]{1,0:T(8,128)(2,1)}) custom-call(s32[5]{0:T(128)S(1)} %stack.41.where_ref, bf16[128,1024]{1,0:T(8,128)(2,1)S(1)} %collective-permute-done.13.distant_ref, f32[64,512]{1,0:T(8,128)S(1)} %get-tuple-element.16.queries_ref, f32[64,128]{1,0:T(8,128)S(1)} %get-tuple-element.17.total_ref, ...), custom_call_target="tpu_custom_call" | custom-call | flops 350000000 | bytes 10000000 | tf_op jit(solution)/shard_map/pallas_call | solution.py:153
  117.0 7.4 %collective-permute-start.16 = (bf16[128,1024]{1,0:T(8,128)(2,1)}, bf16[128,1024]{1,0:T(8,128)(2,1)}, u32[]{:S(2)}, u32[]{:S(2)}) collective-permute-start(bf16[128,1024]{1,0:T(8,128)(2,1)} %get-tuple-element.19), channel_id=1, source_target_pairs={{0,6},{1,3},{2,4},{3,1},{4,2},{5,7},{6,0},{7,5},{8,14},{9,11},{10,... | collective-permute-start | bytes 786440 | tf_op jit(solution)/shard_map/ppermute | solution.py:43
  124.5 0.0 collective-permute-done.9
  124.5 1.0 add_convert_fusion.2
  125.5 2.1 %shard_map.66 = f32[128,1024]{1,0:T(8,128)S(1)} custom-call(s32[5]{0:T(128)S(1)} %stack.41.where_ref, bf16[64,512]{1,0:T(8,128)(2,1)S(1)} %get-tuple-element.18.attended_ref, bf16[256,4096]{1,0:T(8,128)(2,1)S(1)} %copy-done, bf16[256,4096]{1,0:T(8,128)(2,1)} %collective-permute-done.7.wo1_ref), custom_call_target="tpu_custom_call" | custom-call | flops 140000000 | bytes 3000000 | tf_op jit(solution)/shard_map/pallas_call | solution.py:153
  127.6 6.0 %collective-permute-done.16 = bf16[128,1024]{1,0:T(8,128)(2,1)} collective-permute-done((bf16[128,1024]{1,0:T(8,128)(2,1)}, bf16[128,1024]{1,0:T(8,128)(2,1)}, u32[]{:S(2)}, u32[]{:S(2)}) %collective-permute-start.16) | collective-permute-done | bytes 262176 | tf_op jit(solution)/shard_map/ppermute | solution.py:43
  133.6 1.1 add_convert_fusion
  134.8 10.3 %collective-permute-start.19 = (bf16[64,512]{1,0:T(8,128)(2,1)S(1)}, bf16[64,512]{1,0:T(8,128)(2,1)S(1)}, u32[]{:S(2)}, u32[]{:S(2)}) collective-permute-start(bf16[64,512]{1,0:T(8,128)(2,1)S(1)} %get-tuple-element.27), channel_id=1, source_target_pairs={{0,2},{1,7},{2,0},{3,5},{4,6},{5,3},{6,4},{7,1},{8,10},{9,15},{10,... | collective-permute-start | bytes 196616 | tf_op jit(solution)/shard_map/ppermute | solution.py:43
  145.0 1.9 %collective-permute-start.18 = (bf16[64,512]{1,0:T(8,128)(2,1)S(1)}, bf16[64,512]{1,0:T(8,128)(2,1)S(1)}, u32[]{:S(2)}, u32[]{:S(2)}) collective-permute-start(bf16[64,512]{1,0:T(8,128)(2,1)S(1)} %get-tuple-element.28), channel_id=1, source_target_pairs={{0,3},{1,6},{2,1},{3,4},{4,7},{5,2},{6,5},{7,0},{8,11},{9,14},{10,... | collective-permute-start | bytes 196616 | tf_op jit(solution)/shard_map/ppermute | solution.py:43
  147.0 2.2 %collective-permute-start.17 = (bf16[64,512]{1,0:T(8,128)(2,1)S(1)}, bf16[64,512]{1,0:T(8,128)(2,1)S(1)}, u32[]{:S(2)}, u32[]{:S(2)}) collective-permute-start(bf16[64,512]{1,0:T(8,128)(2,1)S(1)} %get-tuple-element.29), channel_id=1, source_target_pairs={{0,1},{1,0},{2,3},{3,2},{4,5},{5,4},{6,7},{7,6},{8,9},{9,8},{10,11... | collective-permute-start | bytes 196616 | tf_op jit(solution)/shard_map/ppermute | solution.py:43
  149.2 2.2 %collective-permute-start.10 = (bf16[64,512]{1,0:T(8,128)(2,1)S(1)}, bf16[64,512]{1,0:T(8,128)(2,1)S(1)}, u32[]{:S(2)}, u32[]{:S(2)}) collective-permute-start(bf16[64,512]{1,0:T(8,128)(2,1)S(1)} %broadcast_select_fusion.10), channel_id=1, source_target_pairs={{0,1},{1,0},{2,3},{3,2},{4,5},{5,4},{6,7},{7,6},{8,9},{9,8},{10,11... | collective-permute-start | bytes 196616 | tf_op jit(solution)/shard_map/ppermute | solution.py:43
  151.3 0.0 collective-permute-done.19
  151.3 2.3 %collective-permute-done.18 = bf16[64,512]{1,0:T(8,128)(2,1)S(1)} collective-permute-done((bf16[64,512]{1,0:T(8,128)(2,1)S(1)}, bf16[64,512]{1,0:T(8,128)(2,1)S(1)}, u32[]{:S(2)}, u32[]{:S(2)}) %collective-permute-start.18) | collective-permute-done | bytes 65568 | tf_op jit(solution)/shard_map/ppermute | solution.py:43
  153.6 0.0 collective-permute-done.17
  153.6 0.1 broadcast_select_fusion.1
  153.7 0.0 collective-permute-done.10
  153.7 0.1 broadcast_select_fusion.3
  153.8 0.7 pad_maximum_fusion
  (10 shorter events, 0.1 us)
Async XLA Ops:
  0.6 30.2 %copy-start.2 = (bf16[2,2,512,256]{3,2,1,0:T(8,128)(2,1)S(1)}, bf16[2,2,512,256]{3,2,1,0:T(8,128)(2,1)}, u32[]{:S(2)}) copy-start(bf16[2,2,512,256]{3,2,1,0:T(8,128)(2,1)} %kv_ref.3) | copy-start | bytes 3145732
  0.6 47.7 %collective-permute-start.4 = (bf16[4096,256]{1,0:T(8,128)(2,1)}, bf16[4096,256]{1,0:T(8,128)(2,1)}, u32[]{:S(2)}, u32[]{:S(2)}) collective-permute-start(bf16[4096,256]{1,0:T(8,128)(2,1)} %wq0_ref.7), channel_id=1, source_target_pairs={{0,1},{1,0},{2,3},{3,2},{4,5},{5,4},{6,7},{7,6},{8,9},{9,8},{10,11... | collective-permute-start | bytes 6291464 | tf_op jit(solution)/shard_map/ppermute | solution.py:43
  2.7 57.3 %collective-permute-start.7 = (bf16[256,4096]{1,0:T(8,128)(2,1)}, bf16[256,4096]{1,0:T(8,128)(2,1)}, u32[]{:S(2)}, u32[]{:S(2)}) collective-permute-start(bf16[256,4096]{1,0:T(8,128)(2,1)} %wo0_ref.7), channel_id=1, source_target_pairs={{0,1},{1,0},{2,3},{3,2},{4,5},{5,4},{6,7},{7,6},{8,9},{9,8},{10,11... | collective-permute-start | bytes 6291464 | tf_op jit(solution)/shard_map/ppermute | solution.py:43
  6.1 19.5 %collective-permute-start.2 = (bf16[64,512]{1,0:T(8,128)(2,1)S(1)}, bf16[64,512]{1,0:T(8,128)(2,1)S(1)}, u32[]{:S(2)}, u32[]{:S(2)}) collective-permute-start(bf16[64,512]{1,0:T(8,128)(2,1)S(1)} %get-tuple-element.32), channel_id=1, source_target_pairs={{0,7},{1,2},{2,5},{3,0},{4,3},{5,6},{6,1},{7,4},{8,15},{9,10},{10,... | collective-permute-start | bytes 196616 | tf_op jit(solution)/shard_map/ppermute | solution.py:43
  20.3 9.5 %collective-permute-start = (bf16[64,512]{1,0:T(8,128)(2,1)S(1)}, bf16[64,512]{1,0:T(8,128)(2,1)S(1)}, u32[]{:S(2)}, u32[]{:S(2)}) collective-permute-start(bf16[64,512]{1,0:T(8,128)(2,1)S(1)} %get-tuple-element.32), channel_id=1, source_target_pairs={{0,1},{1,0},{2,3},{3,2},{4,5},{5,4},{6,7},{7,6},{8,9},{9,8},{10,11... | collective-permute-start | bytes 196616 | tf_op jit(solution)/shard_map/ppermute | solution.py:43
  22.2 8.0 %collective-permute-start.1 = (bf16[64,512]{1,0:T(8,128)(2,1)S(1)}, bf16[64,512]{1,0:T(8,128)(2,1)S(1)}, u32[]{:S(2)}, u32[]{:S(2)}) collective-permute-start(bf16[64,512]{1,0:T(8,128)(2,1)S(1)} %get-tuple-element.33.mine_ref), channel_id=1, source_target_pairs={{0,2},{1,7},{2,0},{3,5},{4,6},{5,3},{6,4},{7,1},{8,10},{9,15},{10,... | collective-permute-start | bytes 196616 | tf_op jit(solution)/shard_map/ppermute | solution.py:43
  25.7 12.7 %collective-permute-start.5 = (bf16[2,256,256]{2,1,0:T(8,128)(2,1)S(1)}, bf16[2,256,256]{2,1,0:T(8,128)(2,1)S(1)}, u32[]{:S(2)}, u32[]{:S(2)}) collective-permute-start(bf16[2,256,256]{2,1,0:T(8,128)(2,1)S(1)} %slice_bitcast_fusion), channel_id=1, source_target_pairs={{0,64},{64,128},{128,192},{192,256},{256,320},{320,384},{384,448},... | collective-permute-start | bytes 786440 | tf_op jit(solution)/shard_map/ppermute | solution.py:52
  29.8 18.5 %copy-start.1 = (bf16[4096,256]{1,0:T(8,128)(2,1)S(1)}, bf16[4096,256]{1,0:T(8,128)(2,1)}, u32[]{:S(2)}) copy-start(bf16[4096,256]{1,0:T(8,128)(2,1)} %wq0_ref.7) | copy-start | bytes 6291460
  38.5 21.5 %collective-permute-start.6 = (bf16[2,2,256,256]{3,2,1,0:T(8,128)(2,1)S(1)}, bf16[2,2,256,256]{3,2,1,0:T(8,128)(2,1)S(1)}, u32[]{:S(2)}, u32[]{:S(2)}) collective-permute-start(bf16[2,2,256,256]{3,2,1,0:T(8,128)(2,1)S(1)} %maximum_select_fusion), channel_id=1, source_target_pairs={{0,1},{1,0},{2,3},{3,2},{4,5},{5,4},{6,7},{7,6},{8,9},{9,8},{10,11... | collective-permute-start | bytes 1572872 | tf_op jit(solution)/shard_map/ppermute | solution.py:43
  40.4 19.6 %collective-permute-start.3 = (bf16[128,1024]{1,0:T(8,128)(2,1)S(1)}, bf16[128,1024]{1,0:T(8,128)(2,1)S(1)}, u32[]{:S(2)}, u32[]{:S(2)}) collective-permute-start(bf16[128,1024]{1,0:T(8,128)(2,1)S(1)} %shard_map.59.pair_ref), channel_id=1, source_target_pairs={{0,6},{1,3},{2,4},{3,1},{4,2},{5,7},{6,0},{7,5},{8,14},{9,11},{10,... | collective-permute-start | bytes 786440 | tf_op jit(solution)/shard_map/ppermute | solution.py:43
  46.2 13.8 %copy-start = (bf16[256,4096]{1,0:T(8,128)(2,1)S(1)}, bf16[256,4096]{1,0:T(8,128)(2,1)}, u32[]{:S(2)}) copy-start(bf16[256,4096]{1,0:T(8,128)(2,1)} %wo0_ref.7) | copy-start | bytes 6291460
  46.2 21.2 %collective-permute-start.14 = (bf16[2,256,256]{2,1,0:T(8,128)(2,1)S(1)}, bf16[2,256,256]{2,1,0:T(8,128)(2,1)S(1)}, u32[]{:S(2)}, u32[]{:S(2)}) collective-permute-start(bf16[2,256,256]{2,1,0:T(8,128)(2,1)S(1)} %get-tuple-element.23), channel_id=1, source_target_pairs={{0,64},{64,128},{128,192},{192,256},{256,320},{320,384},{384,448},... | collective-permute-start | bytes 786440 | tf_op jit(solution)/shard_map/ppermute | solution.py:52
  65.1 11.4 %collective-permute-start.8 = (bf16[128,1024]{1,0:T(8,128)(2,1)S(1)}, bf16[128,1024]{1,0:T(8,128)(2,1)S(1)}, u32[]{:S(2)}, u32[]{:S(2)}) collective-permute-start(bf16[128,1024]{1,0:T(8,128)(2,1)S(1)} %get-tuple-element.15), channel_id=1, source_target_pairs={{0,6},{1,3},{2,4},{3,1},{4,2},{5,7},{6,0},{7,5},{8,14},{9,11},{10,... | collective-permute-start | bytes 786440 | tf_op jit(solution)/shard_map/ppermute | solution.py:43
  67.5 9.0 %copy-start.4 = (pred[128]{0:T(512)(128)(4,1)S(1)}, pred[128]{0:T(512)(128)(4,1)}, u32[]{:S(2)}) copy-start(pred[128]{0:T(512)(128)(4,1)} %constant.47.clone.1) | copy-start | bytes 388
  76.7 34.1 %copy-start.3 = (bf16[128,1024]{1,0:T(8,128)(2,1)}, bf16[128,1024]{1,0:T(8,128)(2,1)S(1)}, u32[]{:S(2)}) copy-start(bf16[128,1024]{1,0:T(8,128)(2,1)S(1)} %add_convert_fusion.1) | copy-start | bytes 786436
  76.7 13.6 %collective-permute-start.12 = (bf16[128,1024]{1,0:T(8,128)(2,1)S(1)}, bf16[128,1024]{1,0:T(8,128)(2,1)S(1)}, u32[]{:S(2)}, u32[]{:S(2)}) collective-permute-start(bf16[128,1024]{1,0:T(8,128)(2,1)S(1)} %add_convert_fusion.1), channel_id=1, source_target_pairs={{0,10},{1,15},{2,8},{3,13},{4,14},{5,11},{6,12},{7,9},{8,18},{9,23... | collective-permute-start | bytes 786440 | tf_op jit(solution)/shard_map/ppermute | solution.py:43
  80.5 15.0 %collective-permute-start.11 = (bf16[128,1024]{1,0:T(8,128)(2,1)S(1)}, bf16[128,1024]{1,0:T(8,128)(2,1)S(1)}, u32[]{:S(2)}, u32[]{:S(2)}) collective-permute-start(bf16[128,1024]{1,0:T(8,128)(2,1)S(1)} %add_convert_fusion.1), channel_id=1, source_target_pairs={{0,8},{1,9},{2,10},{3,11},{4,12},{5,13},{6,14},{7,15},{8,16},{9,17... | collective-permute-start | bytes 786440 | tf_op jit(solution)/shard_map/ppermute | solution.py:43
  85.2 25.5 %collective-permute-start.15 = (bf16[2,2,256,256]{3,2,1,0:T(8,128)(2,1)S(1)}, bf16[2,2,256,256]{3,2,1,0:T(8,128)(2,1)S(1)}, u32[]{:S(2)}, u32[]{:S(2)}) collective-permute-start(bf16[2,2,256,256]{3,2,1,0:T(8,128)(2,1)S(1)} %maximum_select_fusion.1), channel_id=1, source_target_pairs={{0,1},{1,0},{2,3},{3,2},{4,5},{5,4},{6,7},{7,6},{8,9},{9,8},{10,11... | collective-permute-start | bytes 1572872 | tf_op jit(solution)/shard_map/ppermute | solution.py:43
  96.1 15.1 %collective-permute-start.13 = (bf16[128,1024]{1,0:T(8,128)(2,1)S(1)}, bf16[128,1024]{1,0:T(8,128)(2,1)S(1)}, u32[]{:S(2)}, u32[]{:S(2)}) collective-permute-start(bf16[128,1024]{1,0:T(8,128)(2,1)S(1)} %shard_map.63.pair_ref), channel_id=1, source_target_pairs={{0,6},{1,3},{2,4},{3,1},{4,2},{5,7},{6,0},{7,5},{8,14},{9,11},{10,... | collective-permute-start | bytes 786440 | tf_op jit(solution)/shard_map/ppermute | solution.py:43
  100.8 23.7 %collective-permute-start.9 = (bf16[64,1024]{1,0:T(8,128)(2,1)}, bf16[64,1024]{1,0:T(8,128)(2,1)}, u32[]{:S(2)}, u32[]{:S(2)}) collective-permute-start(bf16[64,1024]{1,0:T(8,128)(2,1)} %slice.84), channel_id=1, source_target_pairs={{0,2},{1,7},{2,0},{3,5},{4,6},{5,3},{6,4},{7,1},{8,10},{9,15},{10,... | collective-permute-start | bytes 393224 | tf_op jit(solution)/shard_map/ppermute | solution.py:43
  117.0 16.6 %collective-permute-start.16 = (bf16[128,1024]{1,0:T(8,128)(2,1)}, bf16[128,1024]{1,0:T(8,128)(2,1)}, u32[]{:S(2)}, u32[]{:S(2)}) collective-permute-start(bf16[128,1024]{1,0:T(8,128)(2,1)} %get-tuple-element.19), channel_id=1, source_target_pairs={{0,6},{1,3},{2,4},{3,1},{4,2},{5,7},{6,0},{7,5},{8,14},{9,11},{10,... | collective-permute-start | bytes 786440 | tf_op jit(solution)/shard_map/ppermute | solution.py:43
  134.8 16.6 %collective-permute-start.19 = (bf16[64,512]{1,0:T(8,128)(2,1)S(1)}, bf16[64,512]{1,0:T(8,128)(2,1)S(1)}, u32[]{:S(2)}, u32[]{:S(2)}) collective-permute-start(bf16[64,512]{1,0:T(8,128)(2,1)S(1)} %get-tuple-element.27), channel_id=1, source_target_pairs={{0,2},{1,7},{2,0},{3,5},{4,6},{5,3},{6,4},{7,1},{8,10},{9,15},{10,... | collective-permute-start | bytes 196616 | tf_op jit(solution)/shard_map/ppermute | solution.py:43
  145.0 8.6 %collective-permute-start.18 = (bf16[64,512]{1,0:T(8,128)(2,1)S(1)}, bf16[64,512]{1,0:T(8,128)(2,1)S(1)}, u32[]{:S(2)}, u32[]{:S(2)}) collective-permute-start(bf16[64,512]{1,0:T(8,128)(2,1)S(1)} %get-tuple-element.28), channel_id=1, source_target_pairs={{0,3},{1,6},{2,1},{3,4},{4,7},{5,2},{6,5},{7,0},{8,11},{9,14},{10,... | collective-permute-start | bytes 196616 | tf_op jit(solution)/shard_map/ppermute | solution.py:43
  147.0 6.7 %collective-permute-start.17 = (bf16[64,512]{1,0:T(8,128)(2,1)S(1)}, bf16[64,512]{1,0:T(8,128)(2,1)S(1)}, u32[]{:S(2)}, u32[]{:S(2)}) collective-permute-start(bf16[64,512]{1,0:T(8,128)(2,1)S(1)} %get-tuple-element.29), channel_id=1, source_target_pairs={{0,1},{1,0},{2,3},{3,2},{4,5},{5,4},{6,7},{7,6},{8,9},{9,8},{10,11... | collective-permute-start | bytes 196616 | tf_op jit(solution)/shard_map/ppermute | solution.py:43
  149.2 4.6 %collective-permute-start.10 = (bf16[64,512]{1,0:T(8,128)(2,1)S(1)}, bf16[64,512]{1,0:T(8,128)(2,1)S(1)}, u32[]{:S(2)}, u32[]{:S(2)}) collective-permute-start(bf16[64,512]{1,0:T(8,128)(2,1)S(1)} %broadcast_select_fusion.10), channel_id=1, source_target_pairs={{0,1},{1,0},{2,3},{3,2},{4,5},{5,4},{6,7},{7,6},{8,9},{9,8},{10,11... | collective-permute-start | bytes 196616 | tf_op jit(solution)/shard_map/ppermute | solution.py:43

commit v4 on v3

--- a/solution.py
+++ b/solution.py
@@ -61,18 +61,18 @@
     return jnp.dot(weights, values, preferred_element_type=jnp.float32)
 
 
-def add_queries(ref, sources, wq_refs, queries, total):
-    rows, width = ref.shape[0] // 2, ref.shape[1]
-    for i, source in enumerate(sources):
+def add_queries(ref, blocks, queries, total):
+    rows = ref.shape[0] // 2
+    for i, weights in enumerate(blocks):
         part = ref[i * rows : (i + 1) * rows, :]
         wide = part.astype(jnp.float32)
         total += jnp.sum(wide * wide, axis=-1, keepdims=True)
-        offset = pl.multiple_of(source * width, width)
-        queries = [
-            q + jnp.dot(part, wq_ref[pl.ds(offset, width), :], preferred_element_type=jnp.float32)
-            for q, wq_ref in zip(queries, wq_refs)
-        ]
+        queries = [q + jnp.dot(part, w(), preferred_element_type=jnp.float32) for q, w in zip(queries, weights)]
     return queries, total
+
+
+def rows_of(ref, source, width):
+    return lambda: ref[pl.ds(pl.multiple_of(source * width, width), width), :]
 
 
 def put_terms(attended, targets, wo_refs, out_ref):
@@ -89,9 +89,11 @@
 
 def front_kernel(where_ref, pair_ref, wq0_ref, wq1_ref, queries_ref, total_ref):
     rows, cols = queries_ref.shape[0], wq0_ref.shape[1]
+    width = pair_ref.shape[1]
+    blocks = [[rows_of(wq_ref, where_ref[i], width) for wq_ref in (wq0_ref, wq1_ref)] for i in range(2)]
     queries = [jnp.zeros((rows, cols), jnp.float32) for _ in range(CORES)]
     total = jnp.zeros((rows, 1), jnp.float32)
-    queries, total = add_queries(pair_ref, (where_ref[0], where_ref[1]), (wq0_ref, wq1_ref), queries, total)
+    queries, total = add_queries(pair_ref, blocks, queries, total)
     for i in range(CORES):
         queries_ref[:, i * cols : (i + 1) * cols] = queries[i]
     total_ref[...] = jnp.broadcast_to(total, total_ref.shape)
@@ -105,7 +107,9 @@
     rows, cols = attended_ref.shape[0], wq0_ref.shape[1]
     queries = [queries_ref[:, i * cols : (i + 1) * cols] for i in range(CORES)]
     distant = (where_ref[2], where_ref[3])
-    queries, total = add_queries(distant_ref, distant, (wq0_ref, wq1_ref), queries, total_ref[:, :1])
+    width = distant_ref.shape[1]
+    blocks = [[rows_of(wq_ref, source, width) for wq_ref in (wq0_ref, wq1_ref)] for source in distant]
+    queries, total = add_queries(distant_ref, blocks, queries, total_ref[:, :1])
     scale = lax.rsqrt(total / wq0_ref.shape[0] + EPS)
     last_row = lax.broadcasted_iota(jnp.int32, (16, HD), 0) == 15
     for i in range(CORES):
@@ -148,11 +152,39 @@
         pair_ref[here_rows, :] = total.astype(pair_ref.dtype)
 
 
+def total_of(terms_ref, summed_ref, pair_ref, i):
+    rows = terms_ref.shape[0] // 2
+    rows = slice(i * rows, (i + 1) * rows)
+    total = terms_ref[rows, :] + summed_ref[rows, :].astype(jnp.float32)
+    return total + pair_ref[rows, :].astype(jnp.float32) if i == 0 else total
+
+
+def first_sum_kernel(terms_ref, summed_ref, pair_ref, part_ref, theirs_ref):
+    rows = theirs_ref.shape[0]
+    part_ref[:rows, :] = total_of(terms_ref, summed_ref, pair_ref, 0).astype(part_ref.dtype)
+    theirs = total_of(terms_ref, summed_ref, pair_ref, 1).astype(part_ref.dtype)
+    part_ref[rows:, :] = theirs
+    theirs_ref[...] = theirs
+
+
+def last_sum_kernel(where_ref, terms_ref, summed_ref, pair_ref, kept_ref, given_ref, near_kept_ref, near_given_ref):
+    width = kept_ref.shape[1]
+    first_core = where_ref[4] == 0
+    for i, (here_ref, there_ref) in enumerate(((kept_ref, given_ref), (near_kept_ref, near_given_ref))):
+        total = total_of(terms_ref, summed_ref, pair_ref, i)
+        left, right = total[:, :width], total[:, width:]
+        here_ref[...] = jnp.where(first_core, left, right).astype(here_ref.dtype)
+        there_ref[...] = jnp.where(first_core, right, left).astype(there_ref.dtype)
+
+
 def call(kernel, shapes, flops, nbytes, *operands):
     vmem = pl.BlockSpec(memory_space=pltpu.VMEM)
+    specs = [vmem] * len(operands)
+    if operands[0].ndim == 1:
+        specs[0] = pl.BlockSpec(memory_space=pltpu.SMEM)
     return pl.pallas_call(
         kernel,
-        in_specs=[pl.BlockSpec(memory_space=pltpu.SMEM)] + [vmem] * (len(operands) - 1),
+        in_specs=specs,
         out_specs=(vmem,) * len(shapes),
         out_shape=tuple(jax.ShapeDtypeStruct(*shape) for shape in shapes),
         cost_estimate=pl.CostEstimate(flops=flops, bytes_accessed=nbytes, transcendentals=0),
@@ -202,7 +234,8 @@
         other_kv = swap_cores(given)
         wide = (half, 2 * wq_other.shape[1])
         queries, total = call(
-            front_kernel, ((wide, jnp.float32), ((half, HD), jnp.float32)), 140_000_000, 3_000_000, where, pair, w_query, wq_other
+            front_kernel, ((wide, jnp.float32), ((half, HD), jnp.float32)), 140_000_000, 3_000_000,
+            where, pair, w_query, wq_other,
         )
         attended, terms = call(
             functools.partial(middle_kernel, tick), ((wide, jnp.bfloat16), (block, jnp.bfloat16)), 350_000_000, 10_000_000,
@@ -210,22 +243,26 @@
         )
         summed = permuted(terms, across)
         (terms,) = call(back_kernel, ((block, jnp.float32),), 140_000_000, 3_000_000, where, attended, w_out, wo_other)
-        base = jnp.concatenate([pair[:half], jnp.zeros_like(pair[half:])], axis=0)
-        part = (terms + summed.astype(jnp.float32) + base.astype(jnp.float32)).astype(jnp.bfloat16)
-        own, theirs = part[:half], part[half:]
         if tick == 0:
+            part, theirs = call(
+                first_sum_kernel, ((block, jnp.bfloat16), ((half, 2 * width), jnp.bfloat16)), 0, 1_200_000, terms, summed, pair
+            )
+            pair = permuted(part, here, 1)
             ours = permuted(part, beside, 1)
-            pair = permuted(part, here, 1)
             (pair,) = call(join_kernel, ((block, jnp.bfloat16),), 0, 800_000, where, pair, ours)
             from_near = permuted(theirs, beside)
-            own = (own.astype(jnp.float32) + from_near.astype(jnp.float32)).astype(jnp.bfloat16)
+            own = (part[:half].astype(jnp.float32) + from_near.astype(jnp.float32)).astype(jnp.bfloat16)
             other = swap_cores(features(own, core == 1))
             first = arranged(features(own, first_core), other)
         else:
-            from_near = permuted(features(theirs, first_core), beside)
-            other_near = permuted(features(theirs, core == 1), beside, turn=1)
-            other = swap_cores(features(own, core == 1))
-            own = features(own, first_core).astype(jnp.float32) + from_near.astype(jnp.float32)
+            quarter = (half, width)
+            kept, given, near_kept, near_given = call(
+                last_sum_kernel, ((quarter, jnp.float32),) + ((quarter, jnp.bfloat16),) * 3, 0, 1_200_000, where, terms, summed, pair
+            )
+            from_near = permuted(near_kept, beside)
+            other_near = permuted(near_given, beside, turn=1)
+            other = swap_cores(given)
+            own = kept + from_near.astype(jnp.float32)
             other = other.astype(jnp.float32) + other_near.astype(jnp.float32)
             second = arranged(own.astype(jnp.bfloat16), other.astype(jnp.bfloat16))
     return first, second

time: 155 us -> 154 us (level)
  the two profiles are of different devices: /device:TPU:18 before, /device:TPU:29 now
where the time goes in v4:
time: 154 us; the launch traced here: 153 us
  starting transfers between devices  90.8 us (59%)
  waiting for transfers between devices  34.1 us (22%)
  Pallas kernels  20.8 us (14%)
  other arithmetic  3.71 us (2%)
  local copies, waits for them, and re-layouts  2.78 us (2%)
    ppermute x18, starting transfers between devices, permuted(): return lax.ppermute(block, 'segment', route)  85.1 us
    ppermute x18, waiting for transfers between devices, permuted(): return lax.ppermute(block, 'segment', route)  27.7 us
    pallas_call x10, Pallas kernels, call(): pl.pallas_call(kernel, in_specs=specs, out_specs=(vmem,) * len(shapes), o...  20.8 us
    ppermute x2, waiting for transfers between devices, from_previous(): return lax.ppermute(block, 'seq', [(i, i + 1) for i in range(size - 1)])  6.38 us
    ppermute x2, starting transfers between devices, from_previous(): return lax.ppermute(block, 'seq', [(i, i + 1) for i in range(size - 1)])  5.76 us
  transfers between devices with their start and end apart: 20, of which 8 were waited for; matrix products, arithmetic and copies ran while one was open for 3% of the time, Pallas kernels for 14%

profile of v4, /device:TPU:29, one launch (start us, length us, event | category | flops | bytes accessed | tf_op | source)
XLA Modules:
  0.0 153.4 jit_solution(2501478930618568479)
XLA Ops:
  0.6 0.0 copy-start.3
  0.6 2.7 %collective-permute-start.4 = (bf16[4096,256]{1,0:T(8,128)(2,1)}, bf16[4096,256]{1,0:T(8,128)(2,1)}, u32[]{:S(2)}, u32[]{:S(2)}) collective-permute-start(bf16[4096,256]{1,0:T(8,128)(2,1)} %wq0_ref.7), channel_id=1, source_target_pairs={{0,1},{1,0},{2,3},{3,2},{4,5},{5,4},{6,7},{7,6},{8,9},{9,8},{10,11... | collective-permute-start | bytes 6291464 | tf_op jit(solution)/shard_map/ppermute | solution.py:43
  3.4 1.9 %collective-permute-start.7 = (bf16[256,4096]{1,0:T(8,128)(2,1)}, bf16[256,4096]{1,0:T(8,128)(2,1)}, u32[]{:S(2)}, u32[]{:S(2)}) collective-permute-start(bf16[256,4096]{1,0:T(8,128)(2,1)} %wo0_ref.7), channel_id=1, source_target_pairs={{0,1},{1,0},{2,3},{3,2},{4,5},{5,4},{6,7},{7,6},{8,9},{9,8},{10,11... | collective-permute-start | bytes 6291464 | tf_op jit(solution)/shard_map/ppermute | solution.py:43
  5.3 1.0 broadcast_select_fusion.4
  6.3 8.0 %collective-permute-start.2 = (bf16[64,512]{1,0:T(8,128)(2,1)S(1)}, bf16[64,512]{1,0:T(8,128)(2,1)S(1)}, u32[]{:S(2)}, u32[]{:S(2)}) collective-permute-start(bf16[64,512]{1,0:T(8,128)(2,1)S(1)} %get-tuple-element.41), channel_id=1, source_target_pairs={{0,7},{1,2},{2,5},{3,0},{4,3},{5,6},{6,1},{7,4},{8,15},{9,10},{10,... | collective-permute-start | bytes 196616 | tf_op jit(solution)/shard_map/ppermute | solution.py:43
  14.3 8.6 %collective-permute-start = (bf16[64,512]{1,0:T(8,128)(2,1)S(1)}, bf16[64,512]{1,0:T(8,128)(2,1)S(1)}, u32[]{:S(2)}, u32[]{:S(2)}) collective-permute-start(bf16[64,512]{1,0:T(8,128)(2,1)S(1)} %get-tuple-element.41), channel_id=1, source_target_pairs={{0,1},{1,0},{2,3},{3,2},{4,5},{5,4},{6,7},{7,6},{8,9},{9,8},{10,11... | collective-permute-start | bytes 196616 | tf_op jit(solution)/shard_map/ppermute | solution.py:43
  22.9 2.8 %collective-permute-start.1 = (bf16[64,512]{1,0:T(8,128)(2,1)S(1)}, bf16[64,512]{1,0:T(8,128)(2,1)S(1)}, u32[]{:S(2)}, u32[]{:S(2)}) collective-permute-start(bf16[64,512]{1,0:T(8,128)(2,1)S(1)} %get-tuple-element.42.mine_ref), channel_id=1, source_target_pairs={{0,2},{1,7},{2,0},{3,5},{4,6},{5,3},{6,4},{7,1},{8,10},{9,15},{10,... | collective-permute-start | bytes 196616 | tf_op jit(solution)/shard_map/ppermute | solution.py:43
  25.7 1.0 slice_bitcast_fusion
  26.7 0.0 collective-permute-done.2.beside_given_ref
  26.7 3.7 %collective-permute-start.5 = (bf16[2,256,256]{2,1,0:T(8,128)(2,1)S(1)}, bf16[2,256,256]{2,1,0:T(8,128)(2,1)S(1)}, u32[]{:S(2)}, u32[]{:S(2)}) collective-permute-start(bf16[2,256,256]{2,1,0:T(8,128)(2,1)S(1)} %slice_bitcast_fusion), channel_id=1, source_target_pairs={{0,64},{64,128},{128,192},{192,256},{256,320},{320,384},{384,448},... | collective-permute-start | bytes 786440 | tf_op jit(solution)/shard_map/ppermute | solution.py:52
  30.4 0.1 stack.41.where_ref
  30.5 0.0 collective-permute-done.moved_ref
  30.5 1.0 collective-permute-done.1.beside_mine_ref
  31.5 0.6 shard_map.59.pair_ref
  32.1 0.1 fusion
  32.2 6.4 %collective-permute-done.5.edge_ref = bf16[2,256,256]{2,1,0:T(8,128)(2,1)S(1)} collective-permute-done((bf16[2,256,256]{2,1,0:T(8,128)(2,1)S(1)}, bf16[2,256,256]{2,1,0:T(8,128)(2,1)S(1)}, u32[]{:S(2)}, u32[]{:S(2)}) %collective-permute-start.5) | collective-permute-done | bytes 262176 | tf_op jit(solution)/shard_map/ppermute | solution.py:52
  38.5 0.1 maximum_select_fusion
  38.6 2.5 %collective-permute-start.6 = (bf16[2,2,256,256]{3,2,1,0:T(8,128)(2,1)S(1)}, bf16[2,2,256,256]{3,2,1,0:T(8,128)(2,1)S(1)}, u32[]{:S(2)}, u32[]{:S(2)}) collective-permute-start(bf16[2,2,256,256]{3,2,1,0:T(8,128)(2,1)S(1)} %maximum_select_fusion), channel_id=1, source_target_pairs={{0,1},{1,0},{2,3},{3,2},{4,5},{5,4},{6,7},{7,6},{8,9},{9,8},{10,11... | collective-permute-start | bytes 1572872 | tf_op jit(solution)/shard_map/ppermute | solution.py:43
  41.1 6.1 %collective-permute-start.3 = (bf16[128,1024]{1,0:T(8,128)(2,1)S(1)}, bf16[128,1024]{1,0:T(8,128)(2,1)S(1)}, u32[]{:S(2)}, u32[]{:S(2)}) collective-permute-start(bf16[128,1024]{1,0:T(8,128)(2,1)S(1)} %shard_map.59.pair_ref), channel_id=1, source_target_pairs={{0,6},{1,3},{2,4},{3,1},{4,2},{5,7},{6,0},{7,5},{8,14},{9,11},{10,... | collective-permute-start | bytes 786440 | tf_op jit(solution)/shard_map/ppermute | solution.py:43
  47.2 0.0 copy-start
  47.2 2.1 %collective-permute-start.14 = (bf16[2,256,256]{2,1,0:T(8,128)(2,1)S(1)}, bf16[2,256,256]{2,1,0:T(8,128)(2,1)S(1)}, u32[]{:S(2)}, u32[]{:S(2)}) collective-permute-start(bf16[2,256,256]{2,1,0:T(8,128)(2,1)S(1)} %get-tuple-element.33), channel_id=1, source_target_pairs={{0,64},{64,128},{128,192},{192,256},{256,320},{320,384},{384,448},... | collective-permute-start | bytes 786440 | tf_op jit(solution)/shard_map/ppermute | solution.py:52
  49.3 0.0 collective-permute-done.4.wq1_ref
  49.3 2.1 %shard_map.60 = (f32[64,512]{1,0:T(8,128)S(1)}, f32[64,128]{1,0:T(8,128)S(1)}) custom-call(s32[5]{0:T(128)S(1)} %stack.41.where_ref, bf16[128,1024]{1,0:T(8,128)(2,1)S(1)} %shard_map.59.pair_ref, bf16[4096,256]{1,0:T(8,128)(2,1)S(1)} %copy-done.1, bf16[4096,256]{1,0:T(8,128)(2,1)} %collective-permute-done.4.wq1_ref), custom_call_target="tpu_custom_call" | custom-call | flops 140000000 | bytes 3000000 | tf_op jit(solution)/shard_map/pallas_call | solution.py:185
  51.4 5.8 %collective-permute-done.3.distant_ref = bf16[128,1024]{1,0:T(8,128)(2,1)S(1)} collective-permute-done((bf16[128,1024]{1,0:T(8,128)(2,1)S(1)}, bf16[128,1024]{1,0:T(8,128)(2,1)S(1)}, u32[]{:S(2)}, u32[]{:S(2)}) %collective-permute-start.3) | collective-permute-done | bytes 262176 | tf_op jit(solution)/shard_map/ppermute | solution.py:43
  57.2 0.0 collective-permute-done.6.other_ref
  57.2 0.0 collective-permute-done.7.wo1_ref
  57.2 5.1 %shard_map.61 = (bf16[64,512]{1,0:T(8,128)(2,1)S(1)}, bf16[128,1024]{1,0:T(8,128)(2,1)S(1)}) custom-call(s32[5]{0:T(128)S(1)} %stack.41.where_ref, bf16[128,1024]{1,0:T(8,128)(2,1)S(1)} %collective-permute-done.3.distant_ref, f32[64,512]{1,0:T(8,128)S(1)} %get-tuple-element.17.queries_ref, f32[64,128]{1,0:T(8,128)S(1)} %get-tuple-element.18.total_ref, ...), custom_call_target="tpu_custom_call" | custom-call | flops 350000000 | bytes 10000000 | tf_op jit(solution)/shard_map/pallas_call | solution.py:185
  62.3 6.2 %collective-permute-start.8 = (bf16[128,1024]{1,0:T(8,128)(2,1)S(1)}, bf16[128,1024]{1,0:T(8,128)(2,1)S(1)}, u32[]{:S(2)}, u32[]{:S(2)}) collective-permute-start(bf16[128,1024]{1,0:T(8,128)(2,1)S(1)} %get-tuple-element.21), channel_id=1, source_target_pairs={{0,6},{1,3},{2,4},{3,1},{4,2},{5,7},{6,0},{7,5},{8,14},{9,11},{10,... | collective-permute-start | bytes 786440 | tf_op jit(solution)/shard_map/ppermute | solution.py:43
  68.5 0.0 collective-permute-done.14.edge_ref
  68.5 0.9 maximum_select_fusion.1
  69.4 2.1 %shard_map.62.terms_ref = f32[128,1024]{1,0:T(8,128)S(1)} custom-call(s32[5]{0:T(128)S(1)} %stack.41.where_ref, bf16[64,512]{1,0:T(8,128)(2,1)S(1)} %get-tuple-element.20.attended_ref, bf16[256,4096]{1,0:T(8,128)(2,1)S(1)} %copy-done, bf16[256,4096]{1,0:T(8,128)(2,1)} %collective-permute-done.7.wo1_ref), custom_call_target="tpu_custom_call" | custom-call | flops 140000000 | bytes 3000000 | tf_op jit(solution)/shard_map/pallas_call | solution.py:185
  71.5 3.9 %collective-permute-done.8.summed_ref = bf16[128,1024]{1,0:T(8,128)(2,1)S(1)} collective-permute-done((bf16[128,1024]{1,0:T(8,128)(2,1)S(1)}, bf16[128,1024]{1,0:T(8,128)(2,1)S(1)}, u32[]{:S(2)}, u32[]{:S(2)}) %collective-permute-start.8) | collective-permute-done | bytes 262176 | tf_op jit(solution)/shard_map/ppermute | solution.py:43
  75.4 0.1 shard_map.63
  75.5 5.6 %collective-permute-start.12 = (bf16[128,1024]{1,0:T(8,128)(2,1)S(1)}, bf16[128,1024]{1,0:T(8,128)(2,1)S(1)}, u32[]{:S(2)}, u32[]{:S(2)}) collective-permute-start(bf16[128,1024]{1,0:T(8,128)(2,1)S(1)} %get-tuple-element.22), channel_id=1, source_target_pairs={{0,10},{1,15},{2,8},{3,13},{4,14},{5,11},{6,12},{7,9},{8,18},{9,23... | collective-permute-start | bytes 786440 | tf_op jit(solution)/shard_map/ppermute | solution.py:43
  81.1 2.3 %collective-permute-start.11 = (bf16[128,1024]{1,0:T(8,128)(2,1)S(1)}, bf16[128,1024]{1,0:T(8,128)(2,1)S(1)}, u32[]{:S(2)}, u32[]{:S(2)}) collective-permute-start(bf16[128,1024]{1,0:T(8,128)(2,1)S(1)} %get-tuple-element.22), channel_id=1, source_target_pairs={{0,8},{1,9},{2,10},{3,11},{4,12},{5,13},{6,14},{7,15},{8,16},{9,17... | collective-permute-start | bytes 786440 | tf_op jit(solution)/shard_map/ppermute | solution.py:43
  83.4 3.5 %collective-permute-start.15 = (bf16[2,2,256,256]{3,2,1,0:T(8,128)(2,1)}, bf16[2,2,256,256]{3,2,1,0:T(8,128)(2,1)}, u32[]{:S(2)}, u32[]{:S(2)}) collective-permute-start(bf16[2,2,256,256]{3,2,1,0:T(8,128)(2,1)} %maximum_select_fusion.1), channel_id=1, source_target_pairs={{0,1},{1,0},{2,3},{3,2},{4,5},{5,4},{6,7},{7,6},{8,9},{9,8},{10,11... | collective-permute-start | bytes 1572872 | tf_op jit(solution)/shard_map/ppermute | solution.py:43
  86.9 2.7 %collective-permute-done.12.theirs_ref = bf16[128,1024]{1,0:T(8,128)(2,1)S(1)} collective-permute-done((bf16[128,1024]{1,0:T(8,128)(2,1)S(1)}, bf16[128,1024]{1,0:T(8,128)(2,1)S(1)}, u32[]{:S(2)}, u32[]{:S(2)}) %collective-permute-start.12) | collective-permute-done | bytes 262176 | tf_op jit(solution)/shard_map/ppermute | solution.py:43
  89.6 5.6 %collective-permute-done.11.ours_ref = bf16[128,1024]{1,0:T(8,128)(2,1)S(1)} collective-permute-done((bf16[128,1024]{1,0:T(8,128)(2,1)S(1)}, bf16[128,1024]{1,0:T(8,128)(2,1)S(1)}, u32[]{:S(2)}, u32[]{:S(2)}) %collective-permute-start.11) | collective-permute-done | bytes 262176 | tf_op jit(solution)/shard_map/ppermute | solution.py:43
  95.2 0.6 shard_map.64.pair_ref
  95.8 3.9 %collective-permute-start.13 = (bf16[128,1024]{1,0:T(8,128)(2,1)S(1)}, bf16[128,1024]{1,0:T(8,128)(2,1)}, u32[]{:S(2)}, u32[]{:S(2)}) collective-permute-start(bf16[128,1024]{1,0:T(8,128)(2,1)S(1)} %shard_map.64.pair_ref), channel_id=1, source_target_pairs={{0,6},{1,3},{2,4},{3,1},{4,2},{5,7},{6,0},{7,5},{8,14},{9,11},{10,... | collective-permute-start | bytes 786440 | tf_op jit(solution)/shard_map/ppermute | solution.py:43
  99.8 2.8 %collective-permute-start.9 = (bf16[64,1024]{1,0:T(8,128)(2,1)S(1)}, bf16[64,1024]{1,0:T(8,128)(2,1)}, u32[]{:S(2)}, u32[]{:S(2)}) collective-permute-start(bf16[64,1024]{1,0:T(8,128)(2,1)S(1)} %get-tuple-element.23), channel_id=1, source_target_pairs={{0,2},{1,7},{2,0},{3,5},{4,6},{5,3},{6,4},{7,1},{8,10},{9,15},{10,... | collective-permute-start | bytes 393224 | tf_op jit(solution)/shard_map/ppermute | solution.py:43
  102.6 0.0 copy-start.2
  102.6 1.6 %copy-done.2 = bf16[4096,256]{1,0:T(8,128)(2,1)S(1)} copy-done((bf16[4096,256]{1,0:T(8,128)(2,1)S(1)}, bf16[4096,256]{1,0:T(8,128)(2,1)}, u32[]{:S(2)}) %copy-start.2) | copy-done | bytes 2097176
  104.2 2.1 %shard_map.65 = (f32[64,512]{1,0:T(8,128)S(1)}, f32[64,128]{1,0:T(8,128)S(1)}) custom-call(s32[5]{0:T(128)S(1)} %stack.41.where_ref, bf16[128,1024]{1,0:T(8,128)(2,1)S(1)} %shard_map.64.pair_ref, bf16[4096,256]{1,0:T(8,128)(2,1)S(1)} %copy-done.2, bf16[4096,256]{1,0:T(8,128)(2,1)} %collective-permute-done.4.wq1_ref), custom_call_target="tpu_custom_call" | custom-call | flops 140000000 | bytes 3000000 | tf_op jit(solution)/shard_map/pallas_call | solution.py:185
  106.3 0.0 collective-permute-done.15.other_ref
  106.3 2.8 %collective-permute-done.13.distant_ref = bf16[128,1024]{1,0:T(8,128)(2,1)} collective-permute-done((bf16[128,1024]{1,0:T(8,128)(2,1)S(1)}, bf16[128,1024]{1,0:T(8,128)(2,1)}, u32[]{:S(2)}, u32[]{:S(2)}) %collective-permute-start.13) | collective-permute-done | bytes 262176 | tf_op jit(solution)/shard_map/ppermute | solution.py:43
  109.2 0.0 copy-done.5
  109.2 5.4 %shard_map.66 = (bf16[64,512]{1,0:T(8,128)(2,1)S(1)}, bf16[128,1024]{1,0:T(8,128)(2,1)S(1)}) custom-call(s32[5]{0:T(128)S(1)} %stack.41.where_ref, bf16[128,1024]{1,0:T(8,128)(2,1)} %collective-permute-done.13.distant_ref, f32[64,512]{1,0:T(8,128)S(1)} %get-tuple-element.24.queries_ref, f32[64,128]{1,0:T(8,128)S(1)} %get-tuple-element.25.total_ref, ...), custom_call_target="tpu_custom_call" | custom-call | flops 350000000 | bytes 10000000 | tf_op jit(solution)/shard_map/pallas_call | solution.py:185
  114.6 2.4 %collective-permute-start.16 = (bf16[128,1024]{1,0:T(8,128)(2,1)S(1)}, bf16[128,1024]{1,0:T(8,128)(2,1)S(1)}, u32[]{:S(2)}, u32[]{:S(2)}) collective-permute-start(bf16[128,1024]{1,0:T(8,128)(2,1)S(1)} %get-tuple-element.27), channel_id=1, source_target_pairs={{0,6},{1,3},{2,4},{3,1},{4,2},{5,7},{6,0},{7,5},{8,14},{9,11},{10,... | collective-permute-start | bytes 786440 | tf_op jit(solution)/shard_map/ppermute | solution.py:43
  117.0 0.0 collective-permute-done.9
  117.0 0.9 add_convert_fusion
  118.0 10.6 %collective-permute-start.10 = (bf16[64,512]{1,0:T(8,128)(2,1)S(1)}, bf16[64,512]{1,0:T(8,128)(2,1)S(1)}, u32[]{:S(2)}, u32[]{:S(2)}) collective-permute-start(bf16[64,512]{1,0:T(8,128)(2,1)S(1)} %broadcast_select_fusion.7), channel_id=1, source_target_pairs={{0,1},{1,0},{2,3},{3,2},{4,5},{5,4},{6,7},{7,6},{8,9},{9,8},{10,11... | collective-permute-start | bytes 196616 | tf_op jit(solution)/shard_map/ppermute | solution.py:43
  128.6 2.1 %shard_map.67.terms_ref = f32[128,1024]{1,0:T(8,128)S(1)} custom-call(s32[5]{0:T(128)S(1)} %stack.41.where_ref, bf16[64,512]{1,0:T(8,128)(2,1)S(1)} %get-tuple-element.26.attended_ref, bf16[256,4096]{1,0:T(8,128)(2,1)S(1)} %copy-done, bf16[256,4096]{1,0:T(8,128)(2,1)} %collective-permute-done.7.wo1_ref), custom_call_target="tpu_custom_call" | custom-call | flops 140000000 | bytes 3000000 | tf_op jit(solution)/shard_map/pallas_call | solution.py:185
  130.6 0.0 collective-permute-done.16.summed_ref
  130.7 0.6 shard_map.68
  131.3 6.2 %collective-permute-start.17 = (bf16[64,512]{1,0:T(8,128)(2,1)S(1)}, bf16[64,512]{1,0:T(8,128)(2,1)S(1)}, u32[]{:S(2)}, u32[]{:S(2)}) collective-permute-start(bf16[64,512]{1,0:T(8,128)(2,1)S(1)} %get-tuple-element.28), channel_id=1, source_target_pairs={{0,1},{1,0},{2,3},{3,2},{4,5},{5,4},{6,7},{7,6},{8,9},{9,8},{10,11... | collective-permute-start | bytes 196616 | tf_op jit(solution)/shard_map/ppermute | solution.py:43
  137.5 7.0 %collective-permute-start.18 = (bf16[64,512]{1,0:T(8,128)(2,1)S(1)}, bf16[64,512]{1,0:T(8,128)(2,1)S(1)}, u32[]{:S(2)}, u32[]{:S(2)}) collective-permute-start(bf16[64,512]{1,0:T(8,128)(2,1)S(1)} %get-tuple-element.29), channel_id=1, source_target_pairs={{0,3},{1,6},{2,1},{3,4},{4,7},{5,2},{6,5},{7,0},{8,11},{9,14},{10,... | collective-permute-start | bytes 196616 | tf_op jit(solution)/shard_map/ppermute | solution.py:43
  144.6 2.0 %collective-permute-start.19 = (bf16[64,512]{1,0:T(8,128)(2,1)S(1)}, bf16[64,512]{1,0:T(8,128)(2,1)S(1)}, u32[]{:S(2)}, u32[]{:S(2)}) collective-permute-start(bf16[64,512]{1,0:T(8,128)(2,1)S(1)} %get-tuple-element.31), channel_id=1, source_target_pairs={{0,2},{1,7},{2,0},{3,5},{4,6},{5,3},{6,4},{7,1},{8,10},{9,15},{10,... | collective-permute-start | bytes 196616 | tf_op jit(solution)/shard_map/ppermute | solution.py:43
  146.6 0.0 collective-permute-done.10
  146.6 0.0 collective-permute-done.17
  146.6 0.0 collective-permute-done.18
  146.6 6.0 %collective-permute-done.19 = bf16[64,512]{1,0:T(8,128)(2,1)S(1)} collective-permute-done((bf16[64,512]{1,0:T(8,128)(2,1)S(1)}, bf16[64,512]{1,0:T(8,128)(2,1)S(1)}, u32[]{:S(2)}, u32[]{:S(2)}) %collective-permute-start.19) | collective-permute-done | bytes 65568 | tf_op jit(solution)/shard_map/ppermute | solution.py:43
  152.6 0.1 broadcast_select_fusion.1
  152.7 0.7 pad_maximum_fusion
  (13 shorter events, 0.0 us)
Async XLA Ops:
  0.6 31.4 %copy-start.3 = (bf16[2,2,512,256]{3,2,1,0:T(8,128)(2,1)S(1)}, bf16[2,2,512,256]{3,2,1,0:T(8,128)(2,1)}, u32[]{:S(2)}) copy-start(bf16[2,2,512,256]{3,2,1,0:T(8,128)(2,1)} %kv_ref.3) | copy-start | bytes 3145732
  0.6 48.7 %collective-permute-start.4 = (bf16[4096,256]{1,0:T(8,128)(2,1)}, bf16[4096,256]{1,0:T(8,128)(2,1)}, u32[]{:S(2)}, u32[]{:S(2)}) collective-permute-start(bf16[4096,256]{1,0:T(8,128)(2,1)} %wq0_ref.7), channel_id=1, source_target_pairs={{0,1},{1,0},{2,3},{3,2},{4,5},{5,4},{6,7},{7,6},{8,9},{9,8},{10,11... | collective-permute-start | bytes 6291464 | tf_op jit(solution)/shard_map/ppermute | solution.py:43
  3.4 53.8 %collective-permute-start.7 = (bf16[256,4096]{1,0:T(8,128)(2,1)}, bf16[256,4096]{1,0:T(8,128)(2,1)}, u32[]{:S(2)}, u32[]{:S(2)}) collective-permute-start(bf16[256,4096]{1,0:T(8,128)(2,1)} %wo0_ref.7), channel_id=1, source_target_pairs={{0,1},{1,0},{2,3},{3,2},{4,5},{5,4},{6,7},{7,6},{8,9},{9,8},{10,11... | collective-permute-start | bytes 6291464 | tf_op jit(solution)/shard_map/ppermute | solution.py:43
  6.3 20.4 %collective-permute-start.2 = (bf16[64,512]{1,0:T(8,128)(2,1)S(1)}, bf16[64,512]{1,0:T(8,128)(2,1)S(1)}, u32[]{:S(2)}, u32[]{:S(2)}) collective-permute-start(bf16[64,512]{1,0:T(8,128)(2,1)S(1)} %get-tuple-element.41), channel_id=1, source_target_pairs={{0,7},{1,2},{2,5},{3,0},{4,3},{5,6},{6,1},{7,4},{8,15},{9,10},{10,... | collective-permute-start | bytes 196616 | tf_op jit(solution)/shard_map/ppermute | solution.py:43
  14.3 16.2 %collective-permute-start = (bf16[64,512]{1,0:T(8,128)(2,1)S(1)}, bf16[64,512]{1,0:T(8,128)(2,1)S(1)}, u32[]{:S(2)}, u32[]{:S(2)}) collective-permute-start(bf16[64,512]{1,0:T(8,128)(2,1)S(1)} %get-tuple-element.41), channel_id=1, source_target_pairs={{0,1},{1,0},{2,3},{3,2},{4,5},{5,4},{6,7},{7,6},{8,9},{9,8},{10,11... | collective-permute-start | bytes 196616 | tf_op jit(solution)/shard_map/ppermute | solution.py:43
  22.9 8.6 %collective-permute-start.1 = (bf16[64,512]{1,0:T(8,128)(2,1)S(1)}, bf16[64,512]{1,0:T(8,128)(2,1)S(1)}, u32[]{:S(2)}, u32[]{:S(2)}) collective-permute-start(bf16[64,512]{1,0:T(8,128)(2,1)S(1)} %get-tuple-element.42.mine_ref), channel_id=1, source_target_pairs={{0,2},{1,7},{2,0},{3,5},{4,6},{5,3},{6,4},{7,1},{8,10},{9,15},{10,... | collective-permute-start | bytes 196616 | tf_op jit(solution)/shard_map/ppermute | solution.py:43
  26.7 11.9 %collective-permute-start.5 = (bf16[2,256,256]{2,1,0:T(8,128)(2,1)S(1)}, bf16[2,256,256]{2,1,0:T(8,128)(2,1)S(1)}, u32[]{:S(2)}, u32[]{:S(2)}) collective-permute-start(bf16[2,256,256]{2,1,0:T(8,128)(2,1)S(1)} %slice_bitcast_fusion), channel_id=1, source_target_pairs={{0,64},{64,128},{128,192},{192,256},{256,320},{320,384},{384,448},... | collective-permute-start | bytes 786440 | tf_op jit(solution)/shard_map/ppermute | solution.py:52
  30.5 18.8 %copy-start.1 = (bf16[4096,256]{1,0:T(8,128)(2,1)S(1)}, bf16[4096,256]{1,0:T(8,128)(2,1)}, u32[]{:S(2)}) copy-start(bf16[4096,256]{1,0:T(8,128)(2,1)} %wq0_ref.7) | copy-start | bytes 6291460
  38.6 18.6 %collective-permute-start.6 = (bf16[2,2,256,256]{3,2,1,0:T(8,128)(2,1)S(1)}, bf16[2,2,256,256]{3,2,1,0:T(8,128)(2,1)S(1)}, u32[]{:S(2)}, u32[]{:S(2)}) collective-permute-start(bf16[2,2,256,256]{3,2,1,0:T(8,128)(2,1)S(1)} %maximum_select_fusion), channel_id=1, source_target_pairs={{0,1},{1,0},{2,3},{3,2},{4,5},{5,4},{6,7},{7,6},{8,9},{9,8},{10,11... | collective-permute-start | bytes 1572872 | tf_op jit(solution)/shard_map/ppermute | solution.py:43
  41.1 16.1 %collective-permute-start.3 = (bf16[128,1024]{1,0:T(8,128)(2,1)S(1)}, bf16[128,1024]{1,0:T(8,128)(2,1)S(1)}, u32[]{:S(2)}, u32[]{:S(2)}) collective-permute-start(bf16[128,1024]{1,0:T(8,128)(2,1)S(1)} %shard_map.59.pair_ref), channel_id=1, source_target_pairs={{0,6},{1,3},{2,4},{3,1},{4,2},{5,7},{6,0},{7,5},{8,14},{9,11},{10,... | collective-permute-start | bytes 786440 | tf_op jit(solution)/shard_map/ppermute | solution.py:43
  47.2 10.0 %copy-start = (bf16[256,4096]{1,0:T(8,128)(2,1)S(1)}, bf16[256,4096]{1,0:T(8,128)(2,1)}, u32[]{:S(2)}) copy-start(bf16[256,4096]{1,0:T(8,128)(2,1)} %wo0_ref.7) | copy-start | bytes 6291460
  47.2 21.3 %collective-permute-start.14 = (bf16[2,256,256]{2,1,0:T(8,128)(2,1)S(1)}, bf16[2,256,256]{2,1,0:T(8,128)(2,1)S(1)}, u32[]{:S(2)}, u32[]{:S(2)}) collective-permute-start(bf16[2,256,256]{2,1,0:T(8,128)(2,1)S(1)} %get-tuple-element.33), channel_id=1, source_target_pairs={{0,64},{64,128},{128,192},{192,256},{256,320},{320,384},{384,448},... | collective-permute-start | bytes 786440 | tf_op jit(solution)/shard_map/ppermute | solution.py:52
  62.3 13.1 %collective-permute-start.8 = (bf16[128,1024]{1,0:T(8,128)(2,1)S(1)}, bf16[128,1024]{1,0:T(8,128)(2,1)S(1)}, u32[]{:S(2)}, u32[]{:S(2)}) collective-permute-start(bf16[128,1024]{1,0:T(8,128)(2,1)S(1)} %get-tuple-element.21), channel_id=1, source_target_pairs={{0,6},{1,3},{2,4},{3,1},{4,2},{5,7},{6,0},{7,5},{8,14},{9,11},{10,... | collective-permute-start | bytes 786440 | tf_op jit(solution)/shard_map/ppermute | solution.py:43
  68.5 3.0 %copy-start.4 = (bf16[2,256,256]{2,1,0:T(8,128)(2,1)}, bf16[2,256,256]{2,1,0:T(8,128)(2,1)S(1)}, u32[]{:S(2)}) copy-start(bf16[2,256,256]{2,1,0:T(8,128)(2,1)S(1)} %collective-permute-done.14.edge_ref) | copy-start | bytes 786436
  75.5 14.1 %copy-start.6 = (bf16[128,1024]{1,0:T(8,128)(2,1)}, bf16[128,1024]{1,0:T(8,128)(2,1)S(1)}, u32[]{:S(2)}) copy-start(bf16[128,1024]{1,0:T(8,128)(2,1)S(1)} %get-tuple-element.22) | copy-start | bytes 786436
  75.5 14.1 %collective-permute-start.12 = (bf16[128,1024]{1,0:T(8,128)(2,1)S(1)}, bf16[128,1024]{1,0:T(8,128)(2,1)S(1)}, u32[]{:S(2)}, u32[]{:S(2)}) collective-permute-start(bf16[128,1024]{1,0:T(8,128)(2,1)S(1)} %get-tuple-element.22), channel_id=1, source_target_pairs={{0,10},{1,15},{2,8},{3,13},{4,14},{5,11},{6,12},{7,9},{8,18},{9,23... | collective-permute-start | bytes 786440 | tf_op jit(solution)/shard_map/ppermute | solution.py:43
  81.1 14.2 %collective-permute-start.11 = (bf16[128,1024]{1,0:T(8,128)(2,1)S(1)}, bf16[128,1024]{1,0:T(8,128)(2,1)S(1)}, u32[]{:S(2)}, u32[]{:S(2)}) collective-permute-start(bf16[128,1024]{1,0:T(8,128)(2,1)S(1)} %get-tuple-element.22), channel_id=1, source_target_pairs={{0,8},{1,9},{2,10},{3,11},{4,12},{5,13},{6,14},{7,15},{8,16},{9,17... | collective-permute-start | bytes 786440 | tf_op jit(solution)/shard_map/ppermute | solution.py:43
  83.4 23.0 %collective-permute-start.15 = (bf16[2,2,256,256]{3,2,1,0:T(8,128)(2,1)}, bf16[2,2,256,256]{3,2,1,0:T(8,128)(2,1)}, u32[]{:S(2)}, u32[]{:S(2)}) collective-permute-start(bf16[2,2,256,256]{3,2,1,0:T(8,128)(2,1)} %maximum_select_fusion.1), channel_id=1, source_target_pairs={{0,1},{1,0},{2,3},{3,2},{4,5},{5,4},{6,7},{7,6},{8,9},{9,8},{10,11... | collective-permute-start | bytes 1572872 | tf_op jit(solution)/shard_map/ppermute | solution.py:43
  95.8 13.3 %collective-permute-start.13 = (bf16[128,1024]{1,0:T(8,128)(2,1)S(1)}, bf16[128,1024]{1,0:T(8,128)(2,1)}, u32[]{:S(2)}, u32[]{:S(2)}) collective-permute-start(bf16[128,1024]{1,0:T(8,128)(2,1)S(1)} %shard_map.64.pair_ref), channel_id=1, source_target_pairs={{0,6},{1,3},{2,4},{3,1},{4,2},{5,7},{6,0},{7,5},{8,14},{9,11},{10,... | collective-permute-start | bytes 786440 | tf_op jit(solution)/shard_map/ppermute | solution.py:43
  99.8 17.2 %collective-permute-start.9 = (bf16[64,1024]{1,0:T(8,128)(2,1)S(1)}, bf16[64,1024]{1,0:T(8,128)(2,1)}, u32[]{:S(2)}, u32[]{:S(2)}) collective-permute-start(bf16[64,1024]{1,0:T(8,128)(2,1)S(1)} %get-tuple-element.23), channel_id=1, source_target_pairs={{0,2},{1,7},{2,0},{3,5},{4,6},{5,3},{6,4},{7,1},{8,10},{9,15},{10,... | collective-permute-start | bytes 393224 | tf_op jit(solution)/shard_map/ppermute | solution.py:43
  102.6 1.6 %copy-start.2 = (bf16[4096,256]{1,0:T(8,128)(2,1)S(1)}, bf16[4096,256]{1,0:T(8,128)(2,1)}, u32[]{:S(2)}) copy-start(bf16[4096,256]{1,0:T(8,128)(2,1)} %wq0_ref.7) | copy-start | bytes 6291460
  104.2 5.0 %copy-start.5 = (bf16[2,256,256]{2,1,0:T(8,128)(2,1)S(1)}, bf16[2,256,256]{2,1,0:T(8,128)(2,1)}, u32[]{:S(2)}) copy-start(bf16[2,256,256]{2,1,0:T(8,128)(2,1)} %copy-done.4) | copy-start | bytes 786436
  109.2 7.8 %copy-start.7 = (bf16[128,1024]{1,0:T(8,128)(2,1)S(1)}, bf16[128,1024]{1,0:T(8,128)(2,1)}, u32[]{:S(2)}) copy-start(bf16[128,1024]{1,0:T(8,128)(2,1)} %copy-done.6) | copy-start | bytes 786436
  114.6 16.0 %collective-permute-start.16 = (bf16[128,1024]{1,0:T(8,128)(2,1)S(1)}, bf16[128,1024]{1,0:T(8,128)(2,1)S(1)}, u32[]{:S(2)}, u32[]{:S(2)}) collective-permute-start(bf16[128,1024]{1,0:T(8,128)(2,1)S(1)} %get-tuple-element.27), channel_id=1, source_target_pairs={{0,6},{1,3},{2,4},{3,1},{4,2},{5,7},{6,0},{7,5},{8,14},{9,11},{10,... | collective-permute-start | bytes 786440 | tf_op jit(solution)/shard_map/ppermute | solution.py:43
  118.0 28.6 %collective-permute-start.10 = (bf16[64,512]{1,0:T(8,128)(2,1)S(1)}, bf16[64,512]{1,0:T(8,128)(2,1)S(1)}, u32[]{:S(2)}, u32[]{:S(2)}) collective-permute-start(bf16[64,512]{1,0:T(8,128)(2,1)S(1)} %broadcast_select_fusion.7), channel_id=1, source_target_pairs={{0,1},{1,0},{2,3},{3,2},{4,5},{5,4},{6,7},{7,6},{8,9},{9,8},{10,11... | collective-permute-start | bytes 196616 | tf_op jit(solution)/shard_map/ppermute | solution.py:43
  131.3 15.3 %collective-permute-start.17 = (bf16[64,512]{1,0:T(8,128)(2,1)S(1)}, bf16[64,512]{1,0:T(8,128)(2,1)S(1)}, u32[]{:S(2)}, u32[]{:S(2)}) collective-permute-start(bf16[64,512]{1,0:T(8,128)(2,1)S(1)} %get-tuple-element.28), channel_id=1, source_target_pairs={{0,1},{1,0},{2,3},{3,2},{4,5},{5,4},{6,7},{7,6},{8,9},{9,8},{10,11... | collective-permute-start | bytes 196616 | tf_op jit(solution)/shard_map/ppermute | solution.py:43
  137.5 9.1 %collective-permute-start.18 = (bf16[64,512]{1,0:T(8,128)(2,1)S(1)}, bf16[64,512]{1,0:T(8,128)(2,1)S(1)}, u32[]{:S(2)}, u32[]{:S(2)}) collective-permute-start(bf16[64,512]{1,0:T(8,128)(2,1)S(1)} %get-tuple-element.29), channel_id=1, source_target_pairs={{0,3},{1,6},{2,1},{3,4},{4,7},{5,2},{6,5},{7,0},{8,11},{9,14},{10,... | collective-permute-start | bytes 196616 | tf_op jit(solution)/shard_map/ppermute | solution.py:43
  144.6 8.0 %collective-permute-start.19 = (bf16[64,512]{1,0:T(8,128)(2,1)S(1)}, bf16[64,512]{1,0:T(8,128)(2,1)S(1)}, u32[]{:S(2)}, u32[]{:S(2)}) collective-permute-start(bf16[64,512]{1,0:T(8,128)(2,1)S(1)} %get-tuple-element.31), channel_id=1, source_target_pairs={{0,2},{1,7},{2,0},{3,5},{4,6},{5,3},{6,4},{7,1},{8,10},{9,15},{10,... | collective-permute-start | bytes 196616 | tf_op jit(solution)/shard_map/ppermute | solution.py:43
